TPU v7x, 256 devices: a whole 4x4x8 slice. The times are simulated.
256 devices in a mesh: dp: 2 (over core), row: 16 (over y, x), col: 8 (over z).
Axes of the slice: x: 4, y: 4, z: 8, core: 2. Of those that a mesh axis runs over, the one named last changes fastest.
Arguments:
- features: bfloat16 [256, 96, 2048], P(('dp', 'row'), 'col'), parts along dimension 0, may hold values from 0 to 40
- low_level: bfloat16 [512, 192, 256], P(('dp', 'row'), 'col'), parts along dimension 0, may hold values from -6 to 6
- point_weight: bfloat16 [2048, 256], P(None, 'row'), may hold values from -0.125 to 0.125
- atrous_weight: bfloat16 [3, 3, 3, 2048, 256], P(None, None, None, None, 'row'), may hold values from -0.046875 to 0.046875
- pool_weight: bfloat16 [2048, 256], P(None, 'row'), may hold values from -0.125 to 0.125
- aspp_bias: float32 [5, 256], P(None, 'row'), may hold values from -1.5 to 1.5
- proj_weight: bfloat16 [1280, 256], replicated, may hold values from -0.15625 to 0.15625
- proj_bias: float32 [256], replicated, may hold values from -1.5 to 1.5
- low_weight: bfloat16 [256, 48], replicated, may hold values from -0.375 to 0.375
- low_bias: float32 [48], replicated, may hold values from -1.5 to 1.5
- conv1_weight: bfloat16 [3, 3, 304, 256], replicated, may hold values from -0.109375 to 0.109375
- conv1_bias: float32 [256], replicated, may hold values from -1.5 to 1.5
- conv2_weight: bfloat16 [3, 3, 256, 256], replicated, may hold values from -0.125 to 0.125
- conv2_bias: float32 [256], replicated, may hold values from -1.5 to 1.5
Outputs:
- decoded: bfloat16 [512, 192, 256], P(('dp', 'row'), 'col'), parts along dimension 0
There are 2 independent parts, one for each index of `dp`. A program takes and returns all parts, laid end to end along the dimension named above; an argument that names none is the same for every part. Nothing has to cross between parts.
All inputs are finite; a program needn't handle non-finite values.
Results may differ from a plain program's by a relative error of at most 0.0057.
Values may be sent and summed in bfloat16 or wider, within the bound.
No kernel may reach another device: no remote copies, remote signals or barrier semaphores. Data moves between devices by JAX's collectives and lax.ppermute only.
A program may use at most 128 MiB of HBM per device.

v0:
```python
import jax
import jax.numpy as jnp
from jax import lax
from jax.sharding import Mesh
from jax.sharding import PartitionSpec as P

ROW = ("row_0", "row_1")
ROW_COL = ("row_0", "row_1", "col")
DP_ROW = ("dp", "row_0", "row_1")


RATES = (12, 24, 36)


def from_behind(value, axis, by):
    devices = lax.axis_size(axis)
    pairs = [(i, i + by) for i in range(devices) if 0 <= i + by < devices]
    return lax.ppermute(value, axis, pairs)


def one_axis_at_a_time(value, axes):
    for axis in axes:
        value = lax.psum(value, axis)
    return value


def padded_2(value, sides, width):
    for axis, dim in sides:
        devices, length = (lax.axis_size(axis), value.shape[dim])
        up = [(i, (i + 1) % devices) for i in range(devices - 1)]
        down = [(j, i) for i, j in up]
        last = lax.slice_in_dim(value, length - width, length, axis=dim)
        first = lax.slice_in_dim(value, 0, width, axis=dim)
        before = lax.ppermute(last, axis, up)
        after = lax.ppermute(first, axis, down)
        value = jnp.concatenate([before, value, after], axis=dim)
    return value


def enlarge(padded):
    values = padded.astype(jnp.float32)
    middle = values[1:-1]
    even = 0.75 * middle + 0.25 * values[:-2]
    odd = 0.75 * middle + 0.25 * values[2:]
    values = jnp.stack([even, odd], axis=1).reshape(
        2 * middle.shape[0], middle.shape[1], middle.shape[2]
    )
    middle = values[:, 1:-1]
    even = 0.75 * middle + 0.25 * values[:, :-2]
    odd = 0.75 * middle + 0.25 * values[:, 2:]
    values = jnp.stack([even, odd], axis=2).reshape(
        values.shape[0], 2 * middle.shape[1], middle.shape[2]
    )
    return values.astype(jnp.bfloat16)


def convolve(padded, weight, bias):
    height, width = (padded.shape[0] - 2, padded.shape[1] - 2)
    windows = []
    for row_tap in range(3):
        for col_tap in range(3):
            windows.append(padded[row_tap : row_tap + height, col_tap : col_tap + width])
    columns = jnp.concatenate(windows, axis=2)
    depth = columns.shape[2]
    result = jnp.dot(
        columns.reshape(-1, depth), weight.reshape(depth, -1), preferred_element_type=jnp.float32
    )
    result = jnp.maximum(result + bias, 0.0).astype(jnp.bfloat16)
    return result.reshape(height, width, -1)


def local_rows(values, offset):
    height = values.shape[0]
    extent = abs(offset)
    padded = jnp.pad(values, ((extent, extent), (0, 0), (0, 0)))
    return padded[extent + offset : extent + offset + height]


def bring_cols(values, steps):
    if steps == 0:
        return values
    return from_behind(values, "col", steps)


def move_cols(values, distance):
    width = values.shape[1]
    whole = distance // width
    pieces = bring_cols(values, -whole)
    return pieces


def fix_edges(padded, at_start, at_end, axis_number):
    size = padded.shape[axis_number]
    first = lax.slice_in_dim(padded, 0, 1, axis=axis_number)
    second = lax.slice_in_dim(padded, 1, 2, axis=axis_number)
    middle = lax.slice_in_dim(padded, 1, size - 1, axis=axis_number)
    before = lax.slice_in_dim(padded, size - 2, size - 1, axis=axis_number)
    final = lax.slice_in_dim(padded, size - 1, size, axis=axis_number)
    first = jnp.where(at_start, second, first)
    final = jnp.where(at_end, before, final)
    return jnp.concatenate([first, middle, final], axis=axis_number)


def on_device(
    features,
    low_level,
    point_weight,
    atrous_weight,
    pool_weight,
    aspp_bias,
    proj_weight,
    proj_bias,
    low_weight,
    low_bias,
    conv1_weight,
    conv1_bias,
    conv2_weight,
    conv2_bias,
):
    in_width = features.shape[2]
    own_width = point_weight.shape[1]
    out_width = proj_weight.shape[1]
    row_count = lax.axis_size(ROW)
    col_count = lax.axis_size("col")
    row_index = lax.axis_index(ROW)
    col_index = lax.axis_index("col")
    tile_rows, tile_cols = (features.shape[0], features.shape[1])
    full_rows = tile_rows * row_count
    full_cols = tile_cols * col_count
    atrous_flat = jnp.transpose(atrous_weight.reshape(27, in_width, own_width), (1, 0, 2)).reshape(
        in_width, 27 * own_width
    )
    own_stack = jnp.concatenate([point_weight, atrous_flat, pool_weight], axis=1)
    group_total = 28
    stacked = own_stack[:, : group_total * own_width]
    piece = lax.all_gather(features, ROW, axis=0, tiled=True)
    result = jnp.dot(piece.reshape(-1, in_width), stacked, preferred_element_type=jnp.float32)
    products = result.reshape(piece.shape[0], piece.shape[1], -1)
    map_rows = products.shape[0]

    def group(number):
        return products[:, :, number * own_width : (number + 1) * own_width]

    all_width = own_width * row_count
    first_col = jnp.where(col_index == 0, 1.0, 0.0).astype(jnp.float32)
    spread_bias = lax.dynamic_update_slice_in_dim(
        jnp.zeros((5, all_width), jnp.float32), aspp_bias * first_col, row_index * own_width, 1
    )
    tile_sum = jnp.sum(features.astype(jnp.float32), axis=(0, 1))
    scene_sum, full_bias = (
        one_axis_at_a_time(tile_sum, ROW_COL),
        one_axis_at_a_time(spread_bias, ROW_COL),
    )
    pooled = jnp.dot(
        scene_sum, pool_weight.astype(jnp.float32), precision=lax.Precision.HIGHEST
    ) / (full_rows * full_cols)
    last_axis = full_bias.ndim - 1
    bias_mine = lax.dynamic_slice_in_dim(full_bias, row_index * own_width, own_width, last_axis)

    def activate(values, number):
        return jnp.maximum(values + bias_mine[number], 0.0).astype(jnp.bfloat16)

    outputs = [activate(group(0), 0)]
    for rate_number in range(3):
        dilation = RATES[rate_number]
        running = jnp.zeros((map_rows, tile_cols, own_width), jnp.float32)
        for col_tap in range(3):
            column_sum = jnp.zeros((map_rows, tile_cols, own_width), jnp.float32)
            for row_tap in range(3):
                row_values = group(1 + rate_number * 9 + row_tap * 3 + col_tap)
                offset = (row_tap - 1) * RATES[rate_number]
                column_sum = column_sum + local_rows(row_values, offset)
            running = running + move_cols(column_sum, (col_tap - 1) * dilation)
        outputs.append(activate(running, rate_number + 1))
    pool_branch = jnp.maximum(pooled + bias_mine[4], 0.0).astype(jnp.bfloat16)
    outputs.append(jnp.broadcast_to(pool_branch, (map_rows, tile_cols, own_width)))
    branches = jnp.concatenate(outputs, axis=2)
    blocks = proj_weight.reshape(5, row_count, own_width, out_width)
    swapped = lax.all_to_all(branches, ROW, split_axis=0, concat_axis=2, tiled=True)
    reordered = jnp.transpose(blocks, (1, 0, 2, 3)).reshape(-1, out_width)
    summed = jnp.dot(
        swapped.reshape(-1, swapped.shape[2]), reordered, preferred_element_type=jnp.float32
    )
    coarse = (
        jnp.maximum(summed + proj_bias, 0.0)
        .astype(jnp.bfloat16)
        .reshape(tile_rows, tile_cols, out_width)
    )
    padded = padded_2(coarse, ((ROW, 0), ("col", 1)), 1)
    padded = fix_edges(padded, row_index == 0, row_index == row_count - 1, 0)
    padded = fix_edges(padded, col_index == 0, col_index == col_count - 1, 1)
    upsampled = enlarge(padded)
    low_rows = low_level.reshape(-1, low_level.shape[2])
    reduced = jnp.dot(low_rows, low_weight, preferred_element_type=jnp.float32)
    reduced = (
        jnp.maximum(reduced + low_bias, 0.0)
        .astype(jnp.bfloat16)
        .reshape(low_level.shape[0], low_level.shape[1], -1)
    )
    joined_fine = jnp.concatenate([upsampled, reduced], axis=2)
    padded_fine = padded_2(joined_fine, ((ROW, 0), ("col", 1)), 1)
    hidden = convolve(padded_fine, conv1_weight, conv1_bias)
    padded_hidden = padded_2(hidden, ((ROW, 0), ("col", 1)), 1)
    return convolve(padded_hidden, conv2_weight, conv2_bias)


def solution(mesh):
    torus = Mesh(
        mesh.devices.reshape(mesh.shape["dp"], 4, 4, mesh.shape["col"]),
        ("dp", "row_0", "row_1", "col"),
    )
    placed = (
        P(DP_ROW, "col", None),
        P(DP_ROW, "col", None),
        P(None, ROW),
        P(None, None, None, None, ROW),
        P(None, ROW),
        P(None, ROW),
        P(),
        P(),
        P(),
        P(),
        P(),
        P(),
        P(),
        P(),
    )
    return jax.shard_map(
        on_device, mesh=torus, in_specs=placed, out_specs=P(DP_ROW, "col", None), check_vma=False
    )
```

profile of v0, /device:TPU:32, one launch (start us, length us, event | category | flops | bytes accessed | tf_op | source)
XLA Modules:
  0.0 290.5 jit_solution(2077303134434737102)
XLA Ops:
  8.1 1.1 convert_reduce_fusion
  9.1 17.2 %all-reduce.20 = (f32[5,256]{1,0:T(8,128)S(1)}, f32[2048]{0:T(1024)S(1)}) all-reduce(f32[5,256]{1,0:T(8,128)S(1)} %dynamic_update_slice.3, f32[2048]{0:T(1024)S(1)} %convert_reduce_fusion), channel_id=1, replica_groups=mesh['dp'=2,'row_0'=4,'row_1'=4,'col'=8] {'row_0'}, use_global_device_ids=true, to_apply=%region_0.1 | all-reduce | flops 3328 | bytes 26624 | tf_op jit(solution)/shard_map/psum | solution.py:23
  26.4 17.0 %all-reduce.19 = (f32[5,256]{1,0:T(8,128)S(1)}, f32[2048]{0:T(1024)S(1)}) all-reduce(f32[5,256]{1,0:T(8,128)S(1)} %get-tuple-element.9, f32[2048]{0:T(1024)S(1)} %get-tuple-element.10), channel_id=1, replica_groups=mesh['dp'=2,'row_0'=4,'row_1'=4,'col'=8] {'row_1'}, use_global_device_ids=true, to_apply=%region_1.2 | all-reduce | flops 3328 | bytes 26624 | tf_op jit(solution)/shard_map/psum | solution.py:23
  43.3 29.4 %all-reduce.18 = (f32[5,256]{1,0:T(8,128)S(1)}, f32[2048]{0:T(1024)S(1)}) all-reduce(f32[5,256]{1,0:T(8,128)S(1)} %get-tuple-element.7, f32[2048]{0:T(1024)S(1)} %get-tuple-element.8), channel_id=1, replica_groups=mesh['dp'=2,'row_0'=4,'row_1'=4,'col'=8] {'col'}, use_global_device_ids=true, to_apply=%region_2.3 | all-reduce | flops 3328 | bytes 26624 | tf_op jit(solution)/shard_map/psum | solution.py:23
  73.8 4.9 %all-gather.2.cloned.1.call-done = bf16[128,12,2048]{2,0,1:T(8,128)(2,1)} async-done(((bf16[8,12,2048]{2,0,1:T(8,128)(2,1)}), bf16[128,12,2048]{2,0,1:T(8,128)(2,1)}) %all-gather.2.cloned.1.call-update) | async-done | bytes 6291472 | tf_op jit(solution)/shard_map/all_gather | solution.py:136
  78.7 9.7 %copy.180 = bf16[128,12,2048]{2,1,0:T(8,128)(2,1)} copy(bf16[128,12,2048]{2,0,1:T(8,128)(2,1)} %all-gather.2.cloned.1.call-done) | data formatting | bytes 12582912 | tf_op jit(solution)/shard_map/all_gather | solution.py:136
  88.4 10.8 %reshape.87 = bf16[1536,2048]{1,0:T(8,128)(2,1)} reshape(bf16[128,12,2048]{2,1,0:T(8,128)(2,1)} %copy.180) | data formatting | bytes 12582912 | tf_op jit(solution)/shard_map/reshape | solution.py:137
  99.3 7.3 %convolution_bitcast_fusion = f32[1536,448]{0,1:T(8,128)} fusion(bf16[1536,2048]{1,0:T(8,128)(2,1)} %reshape.87, bf16[2048,432]{0,1:T(8,128)(2,1)S(1)} %bitcast.118, bf16[2048,16]{0,1:T(8,128)(2,1)S(1)} %copy-done.19), kind=kOutput, calls=%fused_computation | convolution fusion | flops 2822242304 | bytes 10878976 | tf_op jit(solution)/shard_map/dot_general | solution.py:137
  106.6 3.4 %copy.181 = f32[1536,448]{1,0:T(8,128)} copy(f32[1536,448]{0,1:T(8,128)} %convolution_bitcast_fusion) | data formatting | bytes 5505024 | tf_op jit(solution)/shard_map/dot_general | solution.py:137
  110.1 4.6 %reshape.88 = f32[128,12,448]{2,1,0:T(8,128)} reshape(f32[1536,448]{1,0:T(8,128)} %copy.181) | data formatting | bytes 5505024 | tf_op jit(solution)/shard_map/reshape | solution.py:138
  114.7 13.5 %fusion.61 = (f32[128,12,16]{2,1,0:T(8,128)}, f32[128,12,16]{2,1,0:T(8,128)}, f32[128,12,16]{2,1,0:T(8,128)}, f32[128,12,16]{2,1,0:T(8,128)}, f32[128,12,16]{2,1...) fusion(f32[128,12,448]{2,1,0:T(8,128)} %reshape.88), kind=kLoop, calls=%fused_computation.144 | loop fusion | bytes 3735552 | tf_op jit(solution)/shard_map/slice | solution.py:142
  128.1 2.2 copy.224
  130.3 2.2 copy.225
  132.5 2.2 copy.223
  134.6 2.2 copy.222
  136.8 2.2 copy.221
  138.9 2.2 copy.220
  141.1 2.2 copy.219
  143.3 1.0 copy.218
  145.5 8.7 %fusion.62 = (f32[128,12,16]{2,1,0:T(8,128)}, f32[128,12,16]{2,1,0:T(8,128)}, f32[128,12,16]{2,1,0:T(8,128)}, f32[128,12,16]{2,1,0:T(8,128)}, f32[128,12,16]{2,1...) fusion(f32[128,12,448]{2,1,0:T(8,128)} %reshape.88, ...), kind=kLoop, calls=%fused_computation.145 | loop fusion | flops 245760 | bytes 2555904 | tf_op jit(solution)/shard_map/slice | solution.py:142
  154.2 1.6 fusion.16
  155.9 1.0 copy.183
  156.8 1.0 copy.226
  158.1 1.0 copy.193
  159.0 2.3 copy.188
  161.3 2.1 copy.187
  163.4 1.0 copy.197
  164.4 1.4 collective-permute-start.5
  165.8 2.4 collective-permute-start.1
  168.2 5.5 %collective-permute-start.2 = (f32[128,12,16]{0,2,1:T(8,128)}, f32[128,12,16]{0,2,1:T(8,128)}, u32[]{:S(2)}, u32[]{:S(2)}) collective-permute-start(f32[128,12,16]{0,2,1:T(8,128)} %copy.188), channel_id=1, source_target_pairs={{0,2},{1,3},{2,4},{3,5},{4,6},{5,7},{8,10},{9,11},{10,12},{11,13},... | collective-permute-start | bytes 294920 | tf_op jit(solution)/shard_map/ppermute | solution.py:18
  173.8 7.7 %collective-permute-start.4 = (f32[128,12,16]{0,2,1:T(8,128)}, f32[128,12,16]{0,2,1:T(8,128)}, u32[]{:S(2)}, u32[]{:S(2)}) collective-permute-start(f32[128,12,16]{0,2,1:T(8,128)} %copy.193), channel_id=1, source_target_pairs={{0,3},{1,4},{2,5},{3,6},{4,7},{8,11},{9,12},{10,13},{11,14},{12,15... | collective-permute-start | bytes 294920 | tf_op jit(solution)/shard_map/ppermute | solution.py:18
  181.5 3.4 %collective-permute-start = (f32[128,12,16]{0,2,1:T(8,128)}, f32[128,12,16]{0,2,1:T(8,128)S(1)}, u32[]{:S(2)}, u32[]{:S(2)}) collective-permute-start(f32[128,12,16]{0,2,1:T(8,128)} %copy.183), channel_id=1, source_target_pairs={{0,1},{1,2},{2,3},{3,4},{4,5},{5,6},{6,7},{8,9},{9,10},{10,11},{11... | collective-permute-start | bytes 294920 | tf_op jit(solution)/shard_map/ppermute | solution.py:18
  185.0 1.6 fusion.56
  187.5 1.3 collective-permute-start.3
  189.5 1.9 fusion.59
  191.4 4.8 %collective-permute-done.3 = f32[128,12,16]{0,2,1:T(8,128)S(1)} collective-permute-done((f32[128,12,16]{0,2,1:T(8,128)}, f32[128,12,16]{0,2,1:T(8,128)S(1)}, u32[]{:S(2)}, u32[]{:S(2)}) %collective-permute-start.3) | collective-permute-done | bytes 98336 | tf_op jit(solution)/shard_map/ppermute | solution.py:18
  196.2 1.8 fusion.58
  198.0 1.8 fusion.57
  200.5 1.4 copy.198
  201.8 1.4 reshape.102
  203.3 5.3 %all-to-all-start = ((bf16[16,2,3840]{2,1,0:T(2,128)(2,1)}), bf16[16,2,3840]{2,1,0:T(2,128)(2,1)S(1)}, u32[]{:S(2)}, u32[]{:S(2)}) async-start(bf16[16,2,3840]{2,1,0:T(2,128)(2,1)} %reshape.102), calls=%async_computation | async-start | bytes 491520 | tf_op jit(solution)/shard_map/all_to_all | solution.py:179
  208.6 8.5 %all-to-all-done = bf16[16,2,3840]{2,1,0:T(2,128)(2,1)S(1)} async-done(((bf16[16,2,3840]{2,1,0:T(2,128)(2,1)}), bf16[16,2,3840]{2,1,0:T(2,128)(2,1)S(1)}, u32[]{:S(2)}, u32[]{:S(2)}) %all-to-all-start) | async-done | bytes 245792 | tf_op jit(solution)/shard_map/all_to_all | solution.py:179
  218.9 2.5 collective-permute-start.6
  221.4 1.3 collective-permute-start.7
  222.7 4.2 %collective-permute-done.7 = bf16[1,12,256]{2,1,0:T(8,128)(2,1)S(1)} collective-permute-done((bf16[1,12,256]{2,1,0:T(8,128)(2,1)S(1)}, bf16[1,12,256]{2,1,0:T(8,128)(2,1)S(1)}, u32[]{:S(2)}, u32[]{:S(2)}) %collective-permute-start.7) | collective-permute-done | bytes 6176 | tf_op jit(solution)/shard_map/ppermute | solution.py:35
  227.0 2.3 collective-permute-start.8
  229.3 3.5 %collective-permute-start.9 = (bf16[10,1,256]{2,1,0:T(2,128)(2,1)S(1)}, bf16[10,1,256]{2,1,0:T(2,128)(2,1)S(1)}, u32[]{:S(2)}, u32[]{:S(2)}) collective-permute-start(bf16[10,1,256]{2,1,0:T(2,128)(2,1)S(1)} %get-tuple-element.75), channel_id=1, source_target_pairs={{1,0},{2,1},{3,2},{4,3},{5,4},{6,5},{7,6},{9,8},{10,9},{11,10},{12... | collective-permute-start | bytes 15368 | tf_op jit(solution)/shard_map/ppermute | solution.py:35
  233.2 1.6 collective-permute-done.9
  235.7 2.3 collective-permute-start.10
  238.0 1.3 collective-permute-start.11
  240.3 3.6 %collective-permute-done.11 = bf16[1,24,304]{2,0,1:T(2,128)(2,1)S(1)} collective-permute-done((bf16[1,24,304]{2,0,1:T(2,128)(2,1)S(1)}, bf16[1,24,304]{2,0,1:T(2,128)(2,1)S(1)}, u32[]{:S(2)}, u32[]{:S(2)}) %collective-permute-start.11) | collective-permute-done | bytes 14624 | tf_op jit(solution)/shard_map/ppermute | solution.py:35
  243.9 3.7 %collective-permute-start.13 = (bf16[18,1,304]{2,0,1:T(8,128)(2,1)S(1)}, bf16[18,1,304]{2,0,1:T(8,128)(2,1)S(1)}, u32[]{:S(2)}, u32[]{:S(2)}) collective-permute-start(bf16[18,1,304]{2,0,1:T(8,128)(2,1)S(1)} %get-tuple-element.46), channel_id=1, source_target_pairs={{1,0},{2,1},{3,2},{4,3},{5,4},{6,5},{7,6},{9,8},{10,9},{11,10},{12... | collective-permute-start | bytes 32840 | tf_op jit(solution)/shard_map/ppermute | solution.py:35
  247.6 2.3 collective-permute-start.12
  250.4 2.9 collective-permute-done.12
  255.2 4.9 %concatenate.122 = bf16[384,2736]{1,0:T(8,128)(2,1)} concatenate(bf16[384,304]{1,0:T(8,128)(2,1)S(1)} %bitcast.104, bf16[384,304]{1,0:T(8,128)(2,1)S(1)} %bitcast.100, bf16[384,304]{1,0:T(8,128)(2,1)S(1)} %bitcast.103, bf16[384,304]{1,0:T(8,128)(2,1)S(1)} %bitcast.105, bf16[384,256]{1,0:T(8,128)(2,1)} %convert_element_type.76, bf16[384,48]{1,0:T(8,128)(2,1)} %copy-done.6, ...), dimensions={1} | concatenate | bytes 4202496 | tf_op jit(solution)/shard_map/concatenate | solution.py:63
  260.1 2.3 fusion.6
  262.5 5.0 %collective-permute-start.14 = (bf16[1,24,256]{2,1,0:T(8,128)(2,1)S(1)}, bf16[1,24,256]{2,1,0:T(8,128)(2,1)S(1)}, u32[]{:S(2)}, u32[]{:S(2)}) collective-permute-start(bf16[1,24,256]{2,1,0:T(8,128)(2,1)S(1)} %get-tuple-element.66), channel_id=1, source_target_pairs={{0,8},{8,16},{16,24},{24,32},{32,40},{40,48},{48,56},{56,64},{64,7... | collective-permute-start | bytes 36872 | tf_op jit(solution)/shard_map/ppermute | solution.py:34
  267.5 1.3 collective-permute-start.15
  268.9 4.2 %collective-permute-done.15 = bf16[1,24,256]{2,1,0:T(8,128)(2,1)S(1)} collective-permute-done((bf16[1,24,256]{2,1,0:T(8,128)(2,1)S(1)}, bf16[1,24,256]{2,1,0:T(8,128)(2,1)S(1)}, u32[]{:S(2)}, u32[]{:S(2)}) %collective-permute-start.15) | collective-permute-done | bytes 12320 | tf_op jit(solution)/shard_map/ppermute | solution.py:35
  273.2 1.9 collective-permute-start.17
  275.1 3.9 %collective-permute-start.16 = (bf16[18,1,256]{2,1,0:T(2,128)(2,1)S(1)}, bf16[18,1,256]{2,1,0:T(2,128)(2,1)S(1)}, u32[]{:S(2)}, u32[]{:S(2)}) collective-permute-start(bf16[18,1,256]{2,1,0:T(2,128)(2,1)S(1)} %get-tuple-element.63), channel_id=1, source_target_pairs={{0,1},{1,2},{2,3},{3,4},{4,5},{5,6},{6,7},{8,9},{9,10},{10,11},{11... | collective-permute-start | bytes 27656 | tf_op jit(solution)/shard_map/ppermute | solution.py:34
  279.1 1.7 collective-permute-done.16
  281.3 1.0 copy-done.18
  282.3 1.3 fusion.5
  (123 shorter events, 13.2 us)
Async XLA Ops:
  6.5 253.6 %copy-start = (bf16[3,3,304,256]{3,2,1,0:T(8,128)(2,1)S(1)}, bf16[3,3,304,256]{3,2,1,0:T(8,128)(2,1)}, u32[]{:S(2)}) copy-start(bf16[3,3,304,256]{3,2,1,0:T(8,128)(2,1)} %param.24) | copy-start | bytes 4202500
  6.5 72.2 %all-gather.2.cloned.1.call-start = ((), (), s32[]{:S(2)}) async-start(), calls=%async_computation.1 | async-start | bytes 6684672 | tf_op jit(solution)/shard_map/all_gather | solution.py:136
  88.4 10.8 %copy-start.17 = (bf16[3,3,3,2048,16]{3,4,2,1,0:T(8,128)(2,1)S(1)}, bf16[3,3,3,2048,16]{3,4,2,1,0:T(8,128)(2,1)}, u32[]{:S(2)}) copy-start(bf16[3,3,3,2048,16]{3,4,2,1,0:T(8,128)(2,1)} %param.17) | copy-start | bytes 5308420
  88.4 10.8 %copy-start.19 = (bf16[2048,16]{0,1:T(8,128)(2,1)S(1)}, bf16[2048,16]{0,1:T(8,128)(2,1)}, u32[]{:S(2)}) copy-start(bf16[2048,16]{0,1:T(8,128)(2,1)} %param.16) | copy-start | bytes 196612
  144.3 1.2 copy-start.1
  154.2 2.7 copy-start.5
  156.8 1.2 copy-start.4
  157.8 5.6 %copy-start.3 = (f32[128,12,16]{2,1,0:T(8,128)S(1)}, f32[128,12,16]{2,1,0:T(8,128)}, u32[]{:S(2)}) copy-start(f32[128,12,16]{2,1,0:T(8,128)} %get-tuple-element.35) | copy-start | bytes 294916
  159.0 27.5 %copy-start.2 = (f32[128,12,16]{2,1,0:T(8,128)S(1)}, f32[128,12,16]{2,1,0:T(8,128)}, u32[]{:S(2)}) copy-start(f32[128,12,16]{2,1,0:T(8,128)} %get-tuple-element.31) | copy-start | bytes 294916
  164.4 31.8 %copy-start.10 = (f32[128,12,16]{0,2,1:T(8,128)S(1)}, f32[128,12,16]{0,2,1:T(8,128)}, u32[]{:S(2)}) copy-start(f32[128,12,16]{0,2,1:T(8,128)} %copy.223) | copy-start | bytes 294916
  164.4 33.5 %copy-start.8 = (f32[128,12,16]{0,2,1:T(8,128)S(1)}, f32[128,12,16]{0,2,1:T(8,128)}, u32[]{:S(2)}) copy-start(f32[128,12,16]{0,2,1:T(8,128)} %copy.224) | copy-start | bytes 294916
  164.4 33.5 %copy-start.9 = (f32[128,12,16]{0,2,1:T(8,128)S(1)}, f32[128,12,16]{0,2,1:T(8,128)}, u32[]{:S(2)}) copy-start(f32[128,12,16]{0,2,1:T(8,128)} %copy.225) | copy-start | bytes 294916
  164.4 33.5 %collective-permute-start.5 = (f32[128,12,16]{0,2,1:T(8,128)}, f32[128,12,16]{0,2,1:T(8,128)}, u32[]{:S(2)}, u32[]{:S(2)}) collective-permute-start(f32[128,12,16]{0,2,1:T(8,128)} %copy.197), channel_id=1, source_target_pairs={{3,0},{4,1},{5,2},{6,3},{7,4},{11,8},{12,9},{13,10},{14,11},{15,12... | collective-permute-start | bytes 294920 | tf_op jit(solution)/shard_map/ppermute | solution.py:18
  165.8 21.7 %collective-permute-start.1 = (f32[128,12,16]{0,2,1:T(8,128)}, f32[128,12,16]{0,2,1:T(8,128)S(1)}, u32[]{:S(2)}, u32[]{:S(2)}) collective-permute-start(f32[128,12,16]{0,2,1:T(8,128)} %copy.187), channel_id=1, source_target_pairs={{1,0},{2,1},{3,2},{4,3},{5,4},{6,5},{7,6},{9,8},{10,9},{11,10},{12... | collective-permute-start | bytes 294920 | tf_op jit(solution)/shard_map/ppermute | solution.py:18
  168.2 23.2 %collective-permute-start.2 = (f32[128,12,16]{0,2,1:T(8,128)}, f32[128,12,16]{0,2,1:T(8,128)}, u32[]{:S(2)}, u32[]{:S(2)}) collective-permute-start(f32[128,12,16]{0,2,1:T(8,128)} %copy.188), channel_id=1, source_target_pairs={{0,2},{1,3},{2,4},{3,5},{4,6},{5,7},{8,10},{9,11},{10,12},{11,13},... | collective-permute-start | bytes 294920 | tf_op jit(solution)/shard_map/ppermute | solution.py:18
  173.8 24.2 %collective-permute-start.4 = (f32[128,12,16]{0,2,1:T(8,128)}, f32[128,12,16]{0,2,1:T(8,128)}, u32[]{:S(2)}, u32[]{:S(2)}) collective-permute-start(f32[128,12,16]{0,2,1:T(8,128)} %copy.193), channel_id=1, source_target_pairs={{0,3},{1,4},{2,5},{3,6},{4,7},{8,11},{9,12},{10,13},{11,14},{12,15... | collective-permute-start | bytes 294920 | tf_op jit(solution)/shard_map/ppermute | solution.py:18
  181.5 7.3 %collective-permute-start = (f32[128,12,16]{0,2,1:T(8,128)}, f32[128,12,16]{0,2,1:T(8,128)S(1)}, u32[]{:S(2)}, u32[]{:S(2)}) collective-permute-start(f32[128,12,16]{0,2,1:T(8,128)} %copy.183), channel_id=1, source_target_pairs={{0,1},{1,2},{2,3},{3,4},{4,5},{5,6},{6,7},{8,9},{9,10},{10,11},{11... | collective-permute-start | bytes 294920 | tf_op jit(solution)/shard_map/ppermute | solution.py:18
  187.5 1.3 copy-start.12
  187.5 8.7 %collective-permute-start.3 = (f32[128,12,16]{0,2,1:T(8,128)}, f32[128,12,16]{0,2,1:T(8,128)S(1)}, u32[]{:S(2)}, u32[]{:S(2)}) collective-permute-start(f32[128,12,16]{0,2,1:T(8,128)} %copy.192), channel_id=1, source_target_pairs={{2,0},{3,1},{4,2},{5,3},{6,4},{7,5},{10,8},{11,9},{12,10},{13,11},... | collective-permute-start | bytes 294920 | tf_op jit(solution)/shard_map/ppermute | solution.py:18
  188.8 0.6 copy-start.13
  189.5 19.1 %copy-start.7 = (bf16[1280,256]{1,0:T(8,128)(2,1)S(1)}, bf16[1280,256]{1,0:T(8,128)(2,1)}, u32[]{:S(2)}) copy-start(bf16[1280,256]{1,0:T(8,128)(2,1)} %param.20) | copy-start | bytes 1966084
  203.3 13.9 %all-to-all-start = ((bf16[16,2,3840]{2,1,0:T(2,128)(2,1)}), bf16[16,2,3840]{2,1,0:T(2,128)(2,1)S(1)}, u32[]{:S(2)}, u32[]{:S(2)}) async-start(bf16[16,2,3840]{2,1,0:T(2,128)(2,1)} %reshape.102), calls=%async_computation | async-start | bytes 491520 | tf_op jit(solution)/shard_map/all_to_all | solution.py:179
  208.5 10.1 %copy-start.15 = (f32[256]{0:T(256)S(1)}, f32[256]{0:T(256)}, u32[]{:S(2)}) copy-start(f32[256]{0:T(256)} %param.21) | copy-start | bytes 3076
  208.6 24.2 %copy-start.11 = (bf16[16,24,256]{2,1,0:T(8,128)(2,1)S(1)}, bf16[16,24,256]{2,1,0:T(8,128)(2,1)}, u32[]{:S(2)}) copy-start(bf16[16,24,256]{2,1,0:T(8,128)(2,1)} %param.15) | copy-start | bytes 589828
  208.6 24.2 %copy-start.14 = (bf16[256,48]{0,1:T(8,128)(2,1)S(1)}, bf16[256,48]{0,1:T(8,128)(2,1)}, u32[]{:S(2)}) copy-start(bf16[256,48]{0,1:T(8,128)(2,1)} %param.22) | copy-start | bytes 73732
  208.6 24.2 %copy-start.16 = (f32[48]{0:T(128)S(1)}, f32[48]{0:T(128)}, u32[]{:S(2)}) copy-start(f32[48]{0:T(128)} %param.23) | copy-start | bytes 580
  218.9 3.8 %collective-permute-start.6 = (bf16[1,12,256]{2,1,0:T(8,128)(2,1)S(1)}, bf16[1,12,256]{2,1,0:T(8,128)(2,1)S(1)}, u32[]{:S(2)}, u32[]{:S(2)}) collective-permute-start(bf16[1,12,256]{2,1,0:T(8,128)(2,1)S(1)} %get-tuple-element.77), channel_id=1, source_target_pairs={{0,8},{8,16},{16,24},{24,32},{32,40},{40,48},{48,56},{56,64},{64,7... | collective-permute-start | bytes 18440 | tf_op jit(solution)/shard_map/ppermute | solution.py:34
  221.4 5.5 %collective-permute-start.7 = (bf16[1,12,256]{2,1,0:T(8,128)(2,1)S(1)}, bf16[1,12,256]{2,1,0:T(8,128)(2,1)S(1)}, u32[]{:S(2)}, u32[]{:S(2)}) collective-permute-start(bf16[1,12,256]{2,1,0:T(8,128)(2,1)S(1)} %get-tuple-element.76), channel_id=1, source_target_pairs={{8,0},{16,8},{24,16},{32,24},{40,32},{48,40},{56,48},{64,56},{72,6... | collective-permute-start | bytes 18440 | tf_op jit(solution)/shard_map/ppermute | solution.py:35
  227.0 6.3 %collective-permute-start.8 = (bf16[10,1,256]{2,1,0:T(2,128)(2,1)S(1)}, bf16[10,1,256]{2,1,0:T(2,128)(2,1)S(1)}, u32[]{:S(2)}, u32[]{:S(2)}) collective-permute-start(bf16[10,1,256]{2,1,0:T(2,128)(2,1)S(1)} %get-tuple-element.74), channel_id=1, source_target_pairs={{0,1},{1,2},{2,3},{3,4},{4,5},{5,6},{6,7},{8,9},{9,10},{10,11},{11... | collective-permute-start | bytes 15368 | tf_op jit(solution)/shard_map/ppermute | solution.py:34
  229.3 5.6 %collective-permute-start.9 = (bf16[10,1,256]{2,1,0:T(2,128)(2,1)S(1)}, bf16[10,1,256]{2,1,0:T(2,128)(2,1)S(1)}, u32[]{:S(2)}, u32[]{:S(2)}) collective-permute-start(bf16[10,1,256]{2,1,0:T(2,128)(2,1)S(1)} %get-tuple-element.75), channel_id=1, source_target_pairs={{1,0},{2,1},{3,2},{4,3},{5,4},{6,5},{7,6},{9,8},{10,9},{11,10},{12... | collective-permute-start | bytes 15368 | tf_op jit(solution)/shard_map/ppermute | solution.py:35
  233.2 2.0 copy-start.6
  235.7 4.6 %collective-permute-start.10 = (bf16[1,24,304]{2,0,1:T(2,128)(2,1)S(1)}, bf16[1,24,304]{2,0,1:T(2,128)(2,1)S(1)}, u32[]{:S(2)}, u32[]{:S(2)}) collective-permute-start(bf16[1,24,304]{2,0,1:T(2,128)(2,1)S(1)} %get-tuple-element.56), channel_id=1, source_target_pairs={{0,8},{8,16},{16,24},{24,32},{32,40},{40,48},{48,56},{56,64},{64,7... | collective-permute-start | bytes 43784 | tf_op jit(solution)/shard_map/ppermute | solution.py:34
  238.0 5.9 %collective-permute-start.11 = (bf16[1,24,304]{2,0,1:T(2,128)(2,1)S(1)}, bf16[1,24,304]{2,0,1:T(2,128)(2,1)S(1)}, u32[]{:S(2)}, u32[]{:S(2)}) collective-permute-start(bf16[1,24,304]{2,0,1:T(2,128)(2,1)S(1)} %get-tuple-element.57), channel_id=1, source_target_pairs={{8,0},{16,8},{24,16},{32,24},{40,32},{48,40},{56,48},{64,56},{72,6... | collective-permute-start | bytes 43784 | tf_op jit(solution)/shard_map/ppermute | solution.py:35
  243.9 6.5 %collective-permute-start.13 = (bf16[18,1,304]{2,0,1:T(8,128)(2,1)S(1)}, bf16[18,1,304]{2,0,1:T(8,128)(2,1)S(1)}, u32[]{:S(2)}, u32[]{:S(2)}) collective-permute-start(bf16[18,1,304]{2,0,1:T(8,128)(2,1)S(1)} %get-tuple-element.46), channel_id=1, source_target_pairs={{1,0},{2,1},{3,2},{4,3},{5,4},{6,5},{7,6},{9,8},{10,9},{11,10},{12... | collective-permute-start | bytes 32840 | tf_op jit(solution)/shard_map/ppermute | solution.py:35
  247.6 5.7 %collective-permute-start.12 = (bf16[18,1,304]{2,0,1:T(8,128)(2,1)S(1)}, bf16[18,1,304]{2,0,1:T(8,128)(2,1)S(1)}, u32[]{:S(2)}, u32[]{:S(2)}) collective-permute-start(bf16[18,1,304]{2,0,1:T(8,128)(2,1)S(1)} %get-tuple-element.47), channel_id=1, source_target_pairs={{0,1},{1,2},{2,3},{3,4},{4,5},{5,6},{6,7},{8,9},{9,10},{10,11},{11... | collective-permute-start | bytes 32840 | tf_op jit(solution)/shard_map/ppermute | solution.py:34
  255.2 5.0 %copy-start.20 = (f32[256]{0:T(256)S(1)}, f32[256]{0:T(256)}, u32[]{:S(2)}) copy-start(f32[256]{0:T(256)} %param.25) | copy-start | bytes 3076
  262.5 6.4 %collective-permute-start.14 = (bf16[1,24,256]{2,1,0:T(8,128)(2,1)S(1)}, bf16[1,24,256]{2,1,0:T(8,128)(2,1)S(1)}, u32[]{:S(2)}, u32[]{:S(2)}) collective-permute-start(bf16[1,24,256]{2,1,0:T(8,128)(2,1)S(1)} %get-tuple-element.66), channel_id=1, source_target_pairs={{0,8},{8,16},{16,24},{24,32},{32,40},{40,48},{48,56},{56,64},{64,7... | collective-permute-start | bytes 36872 | tf_op jit(solution)/shard_map/ppermute | solution.py:34
  267.5 5.6 %collective-permute-start.15 = (bf16[1,24,256]{2,1,0:T(8,128)(2,1)S(1)}, bf16[1,24,256]{2,1,0:T(8,128)(2,1)S(1)}, u32[]{:S(2)}, u32[]{:S(2)}) collective-permute-start(bf16[1,24,256]{2,1,0:T(8,128)(2,1)S(1)} %get-tuple-element.67), channel_id=1, source_target_pairs={{8,0},{16,8},{24,16},{32,24},{40,32},{48,40},{56,48},{64,56},{72,6... | collective-permute-start | bytes 36872 | tf_op jit(solution)/shard_map/ppermute | solution.py:35
  273.2 5.9 %collective-permute-start.17 = (bf16[18,1,256]{2,1,0:T(2,128)(2,1)S(1)}, bf16[18,1,256]{2,1,0:T(2,128)(2,1)S(1)}, u32[]{:S(2)}, u32[]{:S(2)}) collective-permute-start(bf16[18,1,256]{2,1,0:T(2,128)(2,1)S(1)} %get-tuple-element.62), channel_id=1, source_target_pairs={{1,0},{2,1},{3,2},{4,3},{5,4},{6,5},{7,6},{9,8},{10,9},{11,10},{12... | collective-permute-start | bytes 27656 | tf_op jit(solution)/shard_map/ppermute | solution.py:35
  275.1 5.7 %collective-permute-start.16 = (bf16[18,1,256]{2,1,0:T(2,128)(2,1)S(1)}, bf16[18,1,256]{2,1,0:T(2,128)(2,1)S(1)}, u32[]{:S(2)}, u32[]{:S(2)}) collective-permute-start(bf16[18,1,256]{2,1,0:T(2,128)(2,1)S(1)} %get-tuple-element.63), channel_id=1, source_target_pairs={{0,1},{1,2},{2,3},{3,4},{4,5},{5,6},{6,7},{8,9},{9,10},{10,11},{11... | collective-permute-start | bytes 27656 | tf_op jit(solution)/shard_map/ppermute | solution.py:34
  281.1 1.3 copy-start.18
  281.1 1.3 copy-start.21
Sparse Core Ops, SparseCore 0:
  9.8 68.8 all-gather.1
where the time goes:
time: 295 us; the launch traced here: 290 us
  local copies, waits for them, and re-layouts  84.2 us (29%)
  blocking collectives  63.6 us (22%)
  starting transfers between devices  58.4 us (20%)
  waiting for transfers between devices  37.3 us (13%)
  other arithmetic  20.4 us (7%)
  between operations  14.2 us (5%)
  matrix products  12.4 us (4%)
    psum x3, blocking collectives, one_axis_at_a_time(): value = lax.psum(value, axis)  63.6 us
    unnamed x66, local copies, waits for them, and re-layouts  22.7 us
    ppermute x6, starting transfers between devices, from_behind(): return lax.ppermute(value, axis, pairs)  21.8 us
    ppermute x6, starting transfers between devices, padded_2(): before = lax.ppermute(last, axis, up)  18.3 us
    ppermute x6, waiting for transfers between devices, padded_2(): after = lax.ppermute(first, axis, down)  13.6 us
    slice x1, local copies, waits for them, and re-layouts, group(): return products[:, :, number * own_width:(number + 1) * own_width]  13.5 us
    ppermute x6, starting transfers between devices, padded_2(): after = lax.ppermute(first, axis, down)  13 us
    reshape x1, local copies, waits for them, and re-layouts, on_device(): piece.reshape(-1, in_width)  10.8 us
  transfers between devices with their start and end apart: 20, of which 10 were waited for; matrix products, arithmetic and copies ran while one was open for 4% of the time, Pallas kernels for 0%

commit v1 on v0

v1 whole, which is shorter than its diff:
```python
import jax
import jax.numpy as jnp
from jax import lax
from jax.experimental import pallas as pl
from jax.experimental.pallas import tpu as pltpu
from jax.sharding import Mesh
from jax.sharding import PartitionSpec as P

ROW = ("row_0", "row_1")
DP_ROW = ("dp", "row_0", "row_1")
RATES = (12, 24, 36)
MAP_ROWS = 128
MAP_COLS = 96
BF = jnp.bfloat16
F32 = jnp.float32
VMEM_BYTES = 56 * 1024 * 1024


def around(value, axis, by):
    devices = lax.axis_size(axis)
    return lax.ppermute(value, axis, [(i, (i + by) % devices) for i in range(devices)])


def next_to(value, axis, by):
    devices = lax.axis_size(axis)
    pairs = [(i, i + by) for i in range(devices) if 0 <= i + by < devices]
    return lax.ppermute(value, axis, pairs)


def gather_strip(half, first, second):
    behind = around(half, first, 1)
    ahead = around(half, first, -1)
    far_low = around(behind[:3], first, 1)
    far_high = around(ahead[3:], first, -1)
    line = jnp.concatenate([half, behind, ahead, far_low, far_high], axis=0)
    line_behind = around(line, second, 1)
    line_ahead = around(line, second, -1)
    far_behind = around(line_behind[:12], second, 1)
    far_ahead = around(line_ahead[12:], second, -1)
    return [line, line_behind, line_ahead, far_behind, far_ahead]


LINE = ((0, 6, 0, 0), (6, 6, 0, -1), (12, 6, 0, 1), (18, 3, 0, 2), (21, 3, 3, 2))
PIECES = (
    [(0, *piece, 0) for piece in LINE]
    + [(1, *piece, -1) for piece in LINE]
    + [(2, *piece, 1) for piece in LINE]
    + [(3, *piece, 2) for piece in LINE[:2]]
    + [(4, start - 12, count, col, step, 2) for start, count, col, step in LINE[2:]]
)


def products_kernel(*refs):
    place = refs[0]
    parts = (refs[1:6], refs[6:11])
    atrous, point, pool = refs[11:14]
    centre = refs[14]
    sides = refs[15:21]
    pooled = refs[21]
    feats, weights, total, feat_sems, weight_sems = refs[22:27]
    own_y, own_x = place[0], place[1]
    copies = []
    for colour in range(2):
        group = []
        for number, (which, start, count, col, first, second) in enumerate(PIECES):
            step_y, step_x = (second, first) if colour == 0 else (first, second)
            tile = ((own_y + step_y + 4) % 4) * 4 + (own_x + step_x + 4) % 4
            group.append(
                pltpu.make_async_copy(
                    parts[colour][which].at[pl.ds(start, count)],
                    feats.at[pl.ds(6 * colour + col, count), tile],
                    feat_sems.at[colour * len(PIECES) + number],
                )
            )
        copies.append(group)
    loads = [
        pltpu.make_async_copy(atrous, weights.at[pl.ds(0, 432)], weight_sems.at[0]),
        pltpu.make_async_copy(point, weights.at[pl.ds(432, 16)], weight_sems.at[1]),
        pltpu.make_async_copy(pool, weights.at[pl.ds(448, 16)], weight_sems.at[2]),
    ]
    for copy in loads + copies[0] + copies[1]:
        copy.start()
    total[...] = jnp.zeros_like(total)
    lane = lax.broadcasted_iota(jnp.int32, (16, MAP_ROWS), 1)

    def shifted(value, offset):
        if offset == 0:
            return value
        moved = pltpu.roll(value, (-offset) % MAP_ROWS, 1)
        inside = (lane + offset >= 0) & (lane + offset < MAP_ROWS)
        return jnp.where(inside, moved, 0.0)

    def pair(index, carry):
        block = feats[pl.ds(2 * index, 2)].reshape(2 * MAP_ROWS, feats.shape[-1])
        result = lax.dot_general(
            weights[...], block, (((1,), (1,)), ((), ())), preferred_element_type=F32
        )
        for side in range(2):
            col = 2 * index + side
            columns = result[:, side * MAP_ROWS : (side + 1) * MAP_ROWS]

            def group(number, columns=columns):
                return columns[number * 16 : (number + 1) * 16]

            centre[col, 0:16] = group(27)
            for rate in range(3):
                for col_tap in range(3):
                    summed = group(rate * 9 + 3 + col_tap)
                    summed = summed + shifted(group(rate * 9 + col_tap), -RATES[rate])
                    summed = summed + shifted(group(rate * 9 + 6 + col_tap), RATES[rate])
                    if col_tap == 1:
                        centre[col, 16 * (rate + 1) : 16 * (rate + 2)] = summed
                    else:
                        sides[2 * rate + col_tap // 2][col] = summed.astype(BF)
            total[...] += group(28)
        return carry

    for copy in loads + copies[0]:
        copy.wait()
    lax.fori_loop(0, 3, pair, 0)
    for copy in copies[1]:
        copy.wait()
    lax.fori_loop(3, 6, pair, 0)
    strip = jnp.sum(total[...], axis=1, keepdims=True)
    high = strip.astype(BF).astype(F32)
    middle = (strip - high).astype(BF).astype(F32)
    low = strip - high - middle
    terms = jnp.where(lane == 0, high, jnp.where(lane == 1, middle, jnp.where(lane == 2, low, 0.0)))
    terms = terms.astype(BF)
    for side in sides:
        side[12] = terms
    pooled[...] = terms


def products(place, pieces, atrous, point, pool):
    depth = atrous.shape[1]
    side = jax.ShapeDtypeStruct((13, 16, MAP_ROWS), BF)
    anywhere = pl.BlockSpec(memory_space=pl.ANY)
    return pl.pallas_call(
        products_kernel,
        out_shape=[jax.ShapeDtypeStruct((12, 64, MAP_ROWS), F32)]
        + [side] * 6
        + [jax.ShapeDtypeStruct((16, MAP_ROWS), BF)],
        in_specs=[pl.BlockSpec(memory_space=pltpu.SMEM)] + [anywhere] * 13,
        scratch_shapes=[
            pltpu.VMEM((12, 16, 8, depth), BF),
            pltpu.VMEM((464, depth), BF),
            pltpu.VMEM((16, MAP_ROWS), F32),
            pltpu.SemaphoreType.DMA((2 * len(PIECES),)),
            pltpu.SemaphoreType.DMA((3,)),
        ],
        compiler_params=pltpu.CompilerParams(vmem_limit_bytes=VMEM_BYTES),
        name="products",
    )(place, *pieces, atrous, point, pool)


def branches_kernel(place, centre, *refs):
    sides = refs[0:6]
    pooled, opposite, bias, out, rows, slots = refs[6:12]
    strip = place[2]
    for c6 in range(6):
        halves = []
        for half in range(2):
            col = half * 6 + c6
            values = [centre[col, 0:16] + bias[0:16]]
            for rate in range(3):
                running = centre[col, 16 * (rate + 1) : 16 * (rate + 2)]
                for tap in range(2):
                    source = strip + (rate + 1) * (2 * tap - 1)
                    inside = (source >= 0) & (source < 8)
                    running = running + jnp.where(
                        inside, sides[2 * rate + tap][col].astype(F32), 0.0
                    )
                values.append(running + bias[16 * (rate + 1) : 16 * (rate + 2)])
            halves.extend(values)
        block = jnp.maximum(jnp.concatenate(halves, axis=0), 0.0)
        rows[c6, 0:8] = jnp.zeros((8, 128), F32)
        rows[c6, 8:136] = block.T
        rows[c6, 136:144] = jnp.zeros((8, 128), F32)
    terms = pooled[...].astype(F32) + opposite[...].astype(F32)
    for side in sides:
        terms = terms + side[12].astype(F32)
    mean = jnp.sum(terms, axis=1, keepdims=True) / (MAP_ROWS * MAP_COLS)
    branch = jnp.maximum(mean + bias[64:80], 0.0)
    wide = jnp.concatenate(
        [jnp.broadcast_to(branch, (16, 128)), jnp.zeros((112, 128), F32)], axis=0
    ).T
    for slot in range(16):
        for c6 in range(6):
            slots[slot, c6 * 12 : c6 * 12 + 12] = rows[c6, 8 * slot + 6 : 8 * slot + 18]
        slots[slot, 72:80] = wide[0:8]
        out[slot] = slots[slot].astype(BF)


def branches(place, centre, sides, pooled, opposite, bias):
    smem = pl.BlockSpec(memory_space=pltpu.SMEM)
    vmem = pl.BlockSpec(memory_space=pltpu.VMEM)
    return pl.pallas_call(
        branches_kernel,
        out_shape=jax.ShapeDtypeStruct((16, 80, 128), BF),
        in_specs=[smem] + [vmem] * 10,
        scratch_shapes=[pltpu.VMEM((6, 144, 128), F32), pltpu.VMEM((16, 80, 128), F32)],
        compiler_params=pltpu.CompilerParams(vmem_limit_bytes=VMEM_BYTES),
        name="branches",
    )(place, centre, *sides, pooled, opposite, bias)


def project_kernel(received, weight, pool_weight, bias, out, first, last):
    lane = lax.broadcasted_iota(jnp.int32, (80, 128), 1)
    blocks = [received[source].astype(F32) for source in range(16)]
    turned = [pltpu.roll(block, 64, 1) for block in blocks]
    halves = []
    for half in range(2):
        pieces = []
        for source in range(0, 16, 2):
            left = blocks[source] if half == 0 else turned[source]
            right = turned[source + 1] if half == 0 else blocks[source + 1]
            pieces.append(jnp.where(lane < 64, left, right)[0:72])
        halves.append(jnp.concatenate(pieces, axis=1))
    stacked = jnp.concatenate(halves, axis=0).astype(BF)
    low = blocks[0][72:80]
    high = blocks[8][72:80]
    for source in range(1, 8):
        low = low + pltpu.roll(blocks[source][72:80], 16 * source, 1)
        high = high + pltpu.roll(blocks[source + 8][72:80], 16 * source, 1)
    vector = jnp.concatenate([low, high], axis=1).astype(BF)
    constant = jnp.dot(vector, pool_weight[...], preferred_element_type=F32)[0:1]
    summed = jnp.dot(stacked, weight[...], preferred_element_type=F32)
    coarse = jnp.maximum(summed + constant + bias[...], 0.0).astype(BF)
    out[...] = coarse
    first[...] = coarse[0:24]
    last[...] = coarse[120:144]


def project(received, weight, pool_weight, bias):
    return pl.pallas_call(
        project_kernel,
        out_shape=[
            jax.ShapeDtypeStruct((144, 256), BF),
            jax.ShapeDtypeStruct((24, 256), BF),
            jax.ShapeDtypeStruct((24, 256), BF),
        ],
        compiler_params=pltpu.CompilerParams(vmem_limit_bytes=VMEM_BYTES),
        name="project",
    )(received, weight, pool_weight, bias)


def decode_kernel(
    place, before, coarse, after, spread, low, w1, b1, w2, b2, out, fine, fine_cols, mid, mid_cols
):
    wide = jnp.concatenate([before[...], coarse[...], after[...]], axis=0)
    fine[0:640] = jnp.dot(spread[...], wide, preferred_element_type=F32)
    fine[640:656] = jnp.zeros((16, 256), F32)
    for tap in range(3):
        fine_cols[tap] = fine[tap : tap + 640].astype(BF)
    acc = jnp.zeros((576, 256), F32)
    for row_tap in range(3):
        rows = slice(row_tap * 32, row_tap * 32 + 576)
        for tap in range(3):
            acc = acc + jnp.dot(
                fine_cols[tap, rows], w1[row_tap, tap, 0:256], preferred_element_type=F32
            )
        small = jnp.concatenate([w1[row_tap, tap, 256:304] for tap in range(3)], axis=0)
        acc = acc + jnp.dot(low[rows], small, preferred_element_type=F32)
    position = lax.broadcasted_iota(jnp.int32, (576, 256), 0)
    y = 16 * (place[0] * 4 + place[1]) - 1 + (position >> 5)
    x = 24 * place[2] - 1 + (position & 31)
    inside = (y >= 0) & (y < 2 * MAP_ROWS) & (x >= 0) & (x < 2 * MAP_COLS)
    mid[0:576] = jnp.where(inside, jnp.maximum(acc + b1[...], 0.0), 0.0)
    mid[576:592] = jnp.zeros((16, 256), F32)
    for tap in range(3):
        mid_cols[tap] = mid[tap : tap + 576].astype(BF)
    acc = jnp.zeros((512, 256), F32)
    for row_tap in range(3):
        for tap in range(3):
            acc = acc + jnp.dot(
                mid_cols[tap, row_tap * 32 : row_tap * 32 + 512],
                w2[row_tap, tap],
                preferred_element_type=F32,
            )
    result = jnp.maximum(acc + b2[...], 0.0).astype(BF).reshape(16, 32, 256)
    out[...] = result[:, 0:24]


def decode(place, before, coarse, after, spread, low, w1, b1, w2, b2):
    smem = pl.BlockSpec(memory_space=pltpu.SMEM)
    vmem = pl.BlockSpec(memory_space=pltpu.VMEM)
    return pl.pallas_call(
        decode_kernel,
        out_shape=jax.ShapeDtypeStruct((16, 24, 256), BF),
        in_specs=[smem] + [vmem] * 9,
        scratch_shapes=[
            pltpu.VMEM((656, 256), F32),
            pltpu.VMEM((3, 640, 256), BF),
            pltpu.VMEM((592, 256), F32),
            pltpu.VMEM((3, 576, 256), BF),
        ],
        compiler_params=pltpu.CompilerParams(vmem_limit_bytes=VMEM_BYTES),
        name="decode",
    )(place, before, coarse, after, spread, low, w1, b1, w2, b2)


def spread_matrix(row_index, col_index):
    n = lax.broadcasted_iota(jnp.int32, (640, 192), 0)
    m = lax.broadcasted_iota(jnp.int32, (640, 192), 1)

    def weights(fine, size, coarse):
        near = fine >> 1
        other = jnp.where((fine & 1) == 1, near + 1, near - 1)
        other = jnp.clip(other, 0, size - 1)
        value = jnp.where(coarse == near, 0.75, 0.0) + jnp.where(coarse == other, 0.25, 0.0)
        return jnp.where((fine >= 0) & (fine < 2 * size), value, 0.0)

    rows = weights(16 * row_index - 2 + (n >> 5), MAP_ROWS, 8 * row_index - 2 + m % 12)
    cols = weights(24 * col_index - 2 + (n & 31), MAP_COLS, 12 * col_index - 2 + m // 12)
    return (rows * cols).astype(BF)


def low_columns(low_level, weight, bias):
    reduced = jnp.dot(
        low_level.reshape(-1, low_level.shape[2]), weight, preferred_element_type=F32
    )
    reduced = jnp.maximum(reduced + bias, 0.0).astype(BF).reshape(16, 24, -1)
    above = next_to(reduced[14:16], ROW, 1)
    below = next_to(reduced[0:2], ROW, -1)
    tall = jnp.concatenate([above, reduced, below], axis=0)
    before = next_to(tall[:, 22:24], "col", 1)
    after = next_to(tall[:, 0:2], "col", -1)
    full = jnp.concatenate([before, tall, after], axis=1)
    full = jnp.pad(full, ((0, 1), (0, 4), (0, 0))).reshape(672, -1)
    return jnp.concatenate([full[tap : tap + 640] for tap in range(3)], axis=1)


def on_device(
    features,
    low_level,
    point_weight,
    atrous_weight,
    pool_weight,
    aspp_bias,
    proj_weight,
    proj_bias,
    low_weight,
    low_bias,
    conv1_weight,
    conv1_bias,
    conv2_weight,
    conv2_bias,
):
    in_width = features.shape[2]
    own_y, own_x = lax.axis_index("row_0"), lax.axis_index("row_1")
    row_index, col_index = lax.axis_index(ROW), lax.axis_index("col")
    place = jnp.stack([own_y, own_x, col_index]).astype(jnp.int32)
    tile = jnp.transpose(features, (1, 0, 2))
    pieces = gather_strip(tile[:6], "row_1", "row_0") + gather_strip(tile[6:], "row_0", "row_1")
    low = low_columns(low_level, low_weight, low_bias)
    spread = spread_matrix(row_index, col_index)
    atrous = jnp.transpose(atrous_weight, (0, 1, 2, 4, 3)).reshape(432, in_width)
    centre, *sides, pooled = products(place, pieces, atrous, point_weight.T, pool_weight.T)
    moved = [None] * 6
    for rate in (2, 1, 0):
        moved[2 * rate] = around(sides[2 * rate], "col", rate + 1)
        moved[2 * rate + 1] = around(sides[2 * rate + 1], "col", -rate - 1)
    opposite = around(pooled, "col", 4)
    mine = branches(place, centre, moved, pooled, opposite, aspp_bias.reshape(80, 1))
    received = lax.all_to_all(mine, ROW, split_axis=0, concat_axis=0, tiled=True)
    blocks = proj_weight.reshape(5, 16, 16, 256)
    ordered = jnp.transpose(blocks[:4], (1, 0, 2, 3)).reshape(1024, 256)
    coarse, first, last = project(received, ordered, proj_weight[1024:], proj_bias.reshape(1, 256))
    before = next_to(last, "col", 1)
    after = next_to(first, "col", -1)
    return decode(
        place,
        before,
        coarse,
        after,
        spread,
        low,
        conv1_weight,
        conv1_bias.reshape(1, 256),
        conv2_weight,
        conv2_bias.reshape(1, 256),
    )


def solution(mesh):
    torus = Mesh(
        mesh.devices.reshape(mesh.shape["dp"], 4, 4, mesh.shape["col"]),
        ("dp", "row_0", "row_1", "col"),
    )
    placed = (
        P(DP_ROW, "col", None),
        P(DP_ROW, "col", None),
        P(None, ROW),
        P(None, None, None, None, ROW),
        P(None, ROW),
        P(None, ROW),
        P(),
        P(),
        P(),
        P(),
        P(),
        P(),
        P(),
        P(),
    )
    return jax.shard_map(
        on_device, mesh=torus, in_specs=placed, out_specs=P(DP_ROW, "col", None), check_vma=False
    )
```

time: 295 us -> 133 us (0.45); the launches traced: 290 us -> 132 us
  local copies, waits for them, and re-layouts: 84.2 us -> 15.5 us
  blocking collectives: 63.6 us -> 0 us
  Pallas kernels: 0 us -> 20.2 us
  between operations: 14.2 us -> 0.42 us
  other arithmetic: 20.4 us -> 6.82 us
  waiting for transfers between devices: 37.3 us -> 25 us
  matrix products: 12.4 us -> 0.93 us
  starting transfers between devices: 58.4 us -> 63.4 us
    psum x3 -> x0, blocking collectives: 63.6 us -> none  [one_axis_at_a_time(): value = lax.psum(value, axis)]
    pallas_call x0 -> x4, Pallas kernels: none -> 20.2 us  [the longest x1 9.92 us: products(): pl.pallas_call(products_kernel, out_shape=[jax.ShapeDtypeStruct((12, 64,...]
    unnamed x66 -> x58, local copies, waits for them, and re-layouts: 22.7 us -> 6.14 us
    reshape x6 -> x1, local copies, waits for them, and re-layouts: 16 us -> 0.7 us  [on_device(): aspp_bias.reshape(80, 1)]
    dot_general x6 -> x1, matrix products: 12.4 us -> 0.93 us  [low_columns(): jnp.dot(low_level.reshape(-1, low_level.shape[2]), weight, preferred_elem...]
    all_gather x1 -> x0, local copies, waits for them, and re-layouts: 9.74 us -> none  [on_device(): piece = lax.all_gather(features, ROW, axis=0, tiled=True)]
    slice x2 -> x1, other arithmetic: 8.77 us -> 0.03 us  [low_columns(): before = next_to(tall[:, 22:24], 'col', 1)]
    add x7 -> x0, local copies, waits for them, and re-layouts: 8.31 us -> none  [the longest x6 8.3 us: on_device(): column_sum = column_sum + local_rows(row_values, offset)]
  transfers between devices with their start and end apart: 20 -> 30, of which waited for: 10 -> 8; matrix products, arithmetic and copies ran while one was open for 4% -> 15% of each run, Pallas kernels for 0% -> 9%
where the time goes in v1:
time: 133 us; the launch traced here: 132 us
  starting transfers between devices  63.4 us (48%)
  waiting for transfers between devices  25 us (19%)
  Pallas kernels  20.2 us (15%)
  local copies, waits for them, and re-layouts  15.5 us (12%)
  other arithmetic  6.82 us (5%)
    ppermute x23, starting transfers between devices, around(): lax.ppermute(value, axis, [(i, (i + by) % devices) for i in range(devices)])  44.8 us
    ppermute x6, starting transfers between devices, next_to(): return lax.ppermute(value, axis, pairs)  13.5 us
    ppermute x23, waiting for transfers between devices, around(): lax.ppermute(value, axis, [(i, (i + by) % devices) for i in range(devices)])  13.3 us
    pallas_call x1, Pallas kernels, products(): pl.pallas_call(products_kernel, out_shape=[jax.ShapeDtypeStruct((12, 64,...  9.92 us
    all_to_all x1, waiting for transfers between devices, on_device(): lax.all_to_all(mine, ROW, split_axis=0, concat_axis=0, tiled=True)  8.81 us
    unnamed x58, local copies, waits for them, and re-layouts  6.14 us
    pallas_call x1, Pallas kernels, decode(): pl.pallas_call(decode_kernel, out_shape=jax.ShapeDtypeStruct((16, 24, 256...  5.85 us
    all_to_all x1, starting transfers between devices, on_device(): lax.all_to_all(mine, ROW, split_axis=0, concat_axis=0, tiled=True)  5.08 us
  transfers between devices with their start and end apart: 30, of which 8 were waited for; matrix products, arithmetic and copies ran while one was open for 15% of the time, Pallas kernels for 9%

profile of v1, /device:TPU:32, one launch (start us, length us, event | category | flops | bytes accessed | tf_op | source)
XLA Modules:
  0.0 132.4 jit_solution(17275874184019574692)
XLA Ops:
  0.0 1.9 %fusion.33 = (bf16[6,8,2048]{2,1,0:T(8,128)(2,1)S(1)}, bf16[24,8,2048]{2,1,0:T(8,128)(2,1)}, bf16[24,8,2048]{2,1,0:T(8,128)(2,1)}, bf16[6,8,2048]{2,1,0:T(8,128)(2,1)S(1)}) fusion(bf16[12,8,2048]{2,1,0:T(8,128)(2,1)} %bitcast.32), kind=kLoop, calls=%fused_computation.66 | loop fusion | bytes 1179648 | tf_op jit(solution)/shard_map/slice | solution.py:355
  1.9 1.6 %collective-permute-start.8 = (bf16[6,8,2048]{2,1,0:T(8,128)(2,1)S(1)}, bf16[6,8,2048]{2,1,0:T(8,128)(2,1)S(1)}, u32[]{:S(2)}, u32[]{:S(2)}) collective-permute-start(bf16[6,8,2048]{2,1,0:T(8,128)(2,1)S(1)} %get-tuple-element.27), channel_id=1, source_target_pairs={{0,32},{32,64},{64,96},{96,0},{1,33},{33,65},{65,97},{97,1},{2,34}... | collective-permute-start | bytes 589832 | tf_op jit(solution)/shard_map/ppermute | solution.py:21
  3.5 1.7 %collective-permute-start.9 = (bf16[6,8,2048]{2,1,0:T(8,128)(2,1)S(1)}, bf16[6,8,2048]{2,1,0:T(8,128)(2,1)S(1)}, u32[]{:S(2)}, u32[]{:S(2)}) collective-permute-start(bf16[6,8,2048]{2,1,0:T(8,128)(2,1)S(1)} %get-tuple-element.27), channel_id=1, source_target_pairs={{0,96},{32,0},{64,32},{96,64},{1,97},{33,1},{65,33},{97,65},{2,98}... | collective-permute-start | bytes 589832 | tf_op jit(solution)/shard_map/ppermute | solution.py:21
  5.2 1.5 %collective-permute-start = (bf16[6,8,2048]{2,1,0:T(8,128)(2,1)S(1)}, bf16[6,8,2048]{2,1,0:T(8,128)(2,1)S(1)}, u32[]{:S(2)}, u32[]{:S(2)}) collective-permute-start(bf16[6,8,2048]{2,1,0:T(8,128)(2,1)S(1)} %get-tuple-element.30), channel_id=1, source_target_pairs={{0,8},{8,16},{16,24},{24,0},{1,9},{9,17},{17,25},{25,1},{2,10},{10... | collective-permute-start | bytes 589832 | tf_op jit(solution)/shard_map/ppermute | solution.py:21
  6.7 1.7 %collective-permute-start.1 = (bf16[6,8,2048]{2,1,0:T(8,128)(2,1)S(1)}, bf16[6,8,2048]{2,1,0:T(8,128)(2,1)S(1)}, u32[]{:S(2)}, u32[]{:S(2)}) collective-permute-start(bf16[6,8,2048]{2,1,0:T(8,128)(2,1)S(1)} %get-tuple-element.30), channel_id=1, source_target_pairs={{0,24},{8,0},{16,8},{24,16},{1,25},{9,1},{17,9},{25,17},{2,26},{10... | collective-permute-start | bytes 589832 | tf_op jit(solution)/shard_map/ppermute | solution.py:21
  8.4 0.9 fusion.1
  9.4 0.5 collective-permute-done.8
  10.3 3.0 %collective-permute-start.11 = (bf16[3,8,2048]{2,1,0:T(8,128)(2,1)S(1)}, bf16[3,8,2048]{2,1,0:T(8,128)(2,1)S(1)}, u32[]{:S(2)}, u32[]{:S(2)}) collective-permute-start(bf16[3,8,2048]{2,1,0:T(8,128)(2,1)S(1)} %slice.99), channel_id=1, source_target_pairs={{0,96},{32,0},{64,32},{96,64},{1,97},{33,1},{65,33},{97,65},{2,98}... | collective-permute-start | bytes 294920 | tf_op jit(solution)/shard_map/ppermute | solution.py:21
  13.3 1.6 %collective-permute-start.2 = (bf16[3,8,2048]{2,1,0:T(8,128)(2,1)S(1)}, bf16[3,8,2048]{2,1,0:T(8,128)(2,1)S(1)}, u32[]{:S(2)}, u32[]{:S(2)}) collective-permute-start(bf16[3,8,2048]{2,1,0:T(8,128)(2,1)S(1)} %slice.93), channel_id=1, source_target_pairs={{0,8},{8,16},{16,24},{24,0},{1,9},{9,17},{17,25},{25,1},{2,10},{10... | collective-permute-start | bytes 294920 | tf_op jit(solution)/shard_map/ppermute | solution.py:21
  14.9 1.8 %collective-permute-start.3 = (bf16[3,8,2048]{2,1,0:T(8,128)(2,1)S(1)}, bf16[3,8,2048]{2,1,0:T(8,128)(2,1)S(1)}, u32[]{:S(2)}, u32[]{:S(2)}) collective-permute-start(bf16[3,8,2048]{2,1,0:T(8,128)(2,1)S(1)} %slice.94), channel_id=1, source_target_pairs={{0,24},{8,0},{16,8},{24,16},{1,25},{9,1},{17,9},{25,17},{2,26},{10... | collective-permute-start | bytes 294920 | tf_op jit(solution)/shard_map/ppermute | solution.py:21
  16.7 0.7 constant_dynamic-update-slice_fusion.8
  17.4 0.7 constant_dynamic-update-slice_fusion.7
  18.1 0.7 constant_dynamic-update-slice_fusion.3
  18.8 0.7 constant_dynamic-update-slice_fusion.2
  19.5 0.6 constant_dynamic-update-slice_fusion.6
  20.1 0.7 constant_dynamic-update-slice_fusion.5.refs_6_
  21.1 3.0 %collective-permute-start.13 = (bf16[24,8,2048]{2,1,0:T(8,128)(2,1)}, bf16[24,8,2048]{2,1,0:T(8,128)(2,1)S(1)}, u32[]{:S(2)}, u32[]{:S(2)}) collective-permute-start(bf16[24,8,2048]{2,1,0:T(8,128)(2,1)} %constant_dynamic-update-slice_fusion.5.refs_6_), channel_id=1, source_target_pairs={{0,24},{8,0},{16,8},{24,16},{1,25},{9,1},{17,9},{25,17},{2,26},{10... | collective-permute-start | bytes 2359304 | tf_op jit(solution)/shard_map/ppermute | solution.py:21
  24.0 0.6 constant_dynamic-update-slice_fusion.1
  24.7 0.6 constant_dynamic-update-slice_fusion.refs_1_
  25.3 3.2 %collective-permute-start.5 = (bf16[24,8,2048]{2,1,0:T(8,128)(2,1)}, bf16[24,8,2048]{2,1,0:T(8,128)(2,1)S(1)}, u32[]{:S(2)}, u32[]{:S(2)}) collective-permute-start(bf16[24,8,2048]{2,1,0:T(8,128)(2,1)} %constant_dynamic-update-slice_fusion.refs_1_), channel_id=1, source_target_pairs={{0,96},{32,0},{64,32},{96,64},{1,97},{33,1},{65,33},{97,65},{2,98}... | collective-permute-start | bytes 2359304 | tf_op jit(solution)/shard_map/ppermute | solution.py:21
  28.7 1.3 collective-permute-start.25
  30.1 0.6 iota_divide_fusion
  30.6 0.6 and_compare_fusion.1
  31.2 0.6 and_compare_fusion
  31.8 7.9 %collective-permute-done.12.refs_7_ = bf16[24,8,2048]{2,1,0:T(8,128)(2,1)S(1)} collective-permute-done((bf16[24,8,2048]{2,1,0:T(8,128)(2,1)}, bf16[24,8,2048]{2,1,0:T(8,128)(2,1)S(1)}, u32[]{:S(2)}, u32[]{:S(2)}) %collective-permute-start.12) | collective-permute-done | bytes 786464 | tf_op jit(solution)/shard_map/ppermute | solution.py:21
  39.7 0.8 slice.100
  40.6 0.5 fusion.31
  41.1 0.8 slice.101
  42.0 3.2 %collective-permute-start.15 = (bf16[12,8,2048]{2,1,0:T(8,128)(2,1)}, bf16[12,8,2048]{2,1,0:T(8,128)(2,1)}, u32[]{:S(2)}, u32[]{:S(2)}) collective-permute-start(bf16[12,8,2048]{2,1,0:T(8,128)(2,1)} %slice.101), channel_id=1, source_target_pairs={{0,24},{8,0},{16,8},{24,16},{1,25},{9,1},{17,9},{25,17},{2,26},{10... | collective-permute-start | bytes 1179656 | tf_op jit(solution)/shard_map/ppermute | solution.py:21
  45.2 0.9 slice.95
  46.1 0.8 slice.96
  46.9 3.2 %collective-permute-start.7 = (bf16[12,8,2048]{2,1,0:T(8,128)(2,1)}, bf16[12,8,2048]{2,1,0:T(8,128)(2,1)}, u32[]{:S(2)}, u32[]{:S(2)}) collective-permute-start(bf16[12,8,2048]{2,1,0:T(8,128)(2,1)} %slice.96), channel_id=1, source_target_pairs={{0,96},{32,0},{64,32},{96,64},{1,97},{33,1},{65,33},{97,65},{2,98}... | collective-permute-start | bytes 1179656 | tf_op jit(solution)/shard_map/ppermute | solution.py:21
  50.2 0.6 compare_and_fusion
  50.9 1.3 collective-permute-start.26
  52.2 0.6 pad_add_fusion.refs_0_.place
  52.9 2.5 %collective-permute-done.6.refs_4_ = bf16[12,8,2048]{2,1,0:T(8,128)(2,1)} collective-permute-done((bf16[12,8,2048]{2,1,0:T(8,128)(2,1)}, bf16[12,8,2048]{2,1,0:T(8,128)(2,1)}, u32[]{:S(2)}, u32[]{:S(2)}) %collective-permute-start.6) | collective-permute-done | bytes 393248 | tf_op jit(solution)/shard_map/ppermute | solution.py:21
  55.4 0.4 collective-permute-done.7.refs_5_
  55.9 9.9 %products.1 = (f32[12,64,128]{2,1,0:T(8,128)}, bf16[13,16,128]{2,1,0:T(8,128)(2,1)}, bf16[13,16,128]{2,1,0:T(8,128)(2,1)}, bf16[13,16,128]{2,1,0:T(8,128)(2,1)},...) custom-call(s32[3]{0:T(128)} %pad_add_fusion.refs_0_.place, ...), custom_call_target="tpu_custom_call" | custom-call | tf_op jit(solution)/shard_map/products/pallas_call | solution.py:139
  65.8 2.0 %collective-permute-start.16 = (bf16[13,16,128]{2,1,0:T(8,128)(2,1)}, bf16[13,16,128]{2,1,0:T(8,128)(2,1)S(1)}, u32[]{:S(2)}, u32[]{:S(2)}) collective-permute-start(bf16[13,16,128]{2,1,0:T(8,128)(2,1)} %get-tuple-element.17), channel_id=1, source_target_pairs={{0,1},{1,2},{2,3},{3,4},{4,5},{5,6},{6,7},{7,0},{8,9},{9,10},{10,1... | collective-permute-start | bytes 159752 | tf_op jit(solution)/shard_map/ppermute | solution.py:21
  67.9 4.4 %collective-permute-start.18 = (bf16[13,16,128]{2,1,0:T(8,128)(2,1)}, bf16[13,16,128]{2,1,0:T(8,128)(2,1)S(1)}, u32[]{:S(2)}, u32[]{:S(2)}) collective-permute-start(bf16[13,16,128]{2,1,0:T(8,128)(2,1)} %get-tuple-element.19), channel_id=1, source_target_pairs={{0,2},{1,3},{2,4},{3,5},{4,6},{5,7},{6,0},{7,1},{8,10},{9,11},{10,... | collective-permute-start | bytes 159752 | tf_op jit(solution)/shard_map/ppermute | solution.py:21
  72.3 3.4 %collective-permute-start.22 = (bf16[16,128]{1,0:T(8,128)(2,1)}, bf16[16,128]{1,0:T(8,128)(2,1)S(1)}, u32[]{:S(2)}, u32[]{:S(2)}) collective-permute-start(bf16[16,128]{1,0:T(8,128)(2,1)} %get-tuple-element.23.refs_6_), channel_id=1, source_target_pairs={{0,4},{1,5},{2,6},{3,7},{4,0},{5,1},{6,2},{7,3},{8,12},{9,13},{10,... | collective-permute-start | bytes 12296 | tf_op jit(solution)/shard_map/ppermute | solution.py:21
  75.7 3.2 %collective-permute-start.27 = (bf16[20,2,48]{2,1,0:T(2,128)(2,1)S(1)}, bf16[20,2,48]{2,1,0:T(2,128)(2,1)S(1)}, u32[]{:S(2)}, u32[]{:S(2)}) collective-permute-start(bf16[20,2,48]{2,1,0:T(2,128)(2,1)S(1)} %get-tuple-element.33), channel_id=1, source_target_pairs={{0,1},{1,2},{2,3},{3,4},{4,5},{5,6},{6,7},{8,9},{9,10},{10,11},{11... | collective-permute-start | bytes 11528 | tf_op jit(solution)/shard_map/ppermute | solution.py:27
  79.0 1.2 collective-permute-done.22.refs_7_
  80.2 1.9 %collective-permute-start.28 = (bf16[20,2,48]{2,1,0:T(2,128)(2,1)S(1)}, bf16[20,2,48]{2,1,0:T(2,128)(2,1)S(1)}, u32[]{:S(2)}, u32[]{:S(2)}) collective-permute-start(bf16[20,2,48]{2,1,0:T(2,128)(2,1)S(1)} %get-tuple-element.34), channel_id=1, source_target_pairs={{1,0},{2,1},{3,2},{4,3},{5,4},{6,5},{7,6},{9,8},{10,9},{11,10},{12... | collective-permute-start | bytes 11528 | tf_op jit(solution)/shard_map/ppermute | solution.py:27
  82.1 3.7 %collective-permute-start.19 = (bf16[13,16,128]{2,1,0:T(8,128)(2,1)}, bf16[13,16,128]{2,1,0:T(8,128)(2,1)S(1)}, u32[]{:S(2)}, u32[]{:S(2)}) collective-permute-start(bf16[13,16,128]{2,1,0:T(8,128)(2,1)} %get-tuple-element.20), channel_id=1, source_target_pairs={{0,6},{1,7},{2,0},{3,1},{4,2},{5,3},{6,4},{7,5},{8,14},{9,15},{10,... | collective-permute-start | bytes 159752 | tf_op jit(solution)/shard_map/ppermute | solution.py:21
  85.8 3.0 %collective-permute-start.20 = (bf16[13,16,128]{2,1,0:T(8,128)(2,1)}, bf16[13,16,128]{2,1,0:T(8,128)(2,1)S(1)}, u32[]{:S(2)}, u32[]{:S(2)}) collective-permute-start(bf16[13,16,128]{2,1,0:T(8,128)(2,1)} %get-tuple-element.21), channel_id=1, source_target_pairs={{0,3},{1,4},{2,5},{3,6},{4,7},{5,0},{6,1},{7,2},{8,11},{9,12},{10,... | collective-permute-start | bytes 159752 | tf_op jit(solution)/shard_map/ppermute | solution.py:21
  88.9 2.0 %collective-permute-start.21 = (bf16[13,16,128]{2,1,0:T(8,128)(2,1)}, bf16[13,16,128]{2,1,0:T(8,128)(2,1)S(1)}, u32[]{:S(2)}, u32[]{:S(2)}) collective-permute-start(bf16[13,16,128]{2,1,0:T(8,128)(2,1)} %get-tuple-element.22), channel_id=1, source_target_pairs={{0,5},{1,6},{2,7},{3,0},{4,1},{5,2},{6,3},{7,4},{8,13},{9,14},{10,... | collective-permute-start | bytes 159752 | tf_op jit(solution)/shard_map/ppermute | solution.py:21
  90.9 2.2 %multiply_convert_fusion.spread = bf16[640,192]{1,0:T(8,128)(2,1)} fusion(s32[640]{0:T(1024)S(1)} %get-tuple-element.40, s32[640]{0:T(1024)S(1)} %get-tuple-element.46, s32[640]{0:T(1024)S(1)} %get-tuple-element.39, s32[192]{0:T(256)S(1)} %get-tuple-element.49, s32[192]{0:T(256)S(1)} %copy-done.22, s32[]{:T(128)S(6)} %sub.30, s32[640]{0:T(1024)S(1)} %get-tuple-element.44, ...), kind=kLoop, calls=%fused_computation.3 | loop fusion | flops 2703360 | bytes 267144 | tf_op jit(solution)/shard_map/convert_element_type | solution.py:316
  93.1 0.7 slice.81.pool_weight
  93.8 0.7 reshape.42.refs_8_
  94.5 0.9 copy.21
  95.4 0.8 collective-permute-done.21.refs_5_
  96.3 0.6 copy-done.12
  96.9 2.3 %branches.1 = bf16[16,80,128]{2,1,0:T(8,128)(2,1)} custom-call(s32[3]{0:T(128)} %pad_add_fusion.refs_0_.place, f32[12,64,128]{2,1,0:T(8,128)} %get-tuple-element.16.centre, bf16[13,16,128]{2,1,0:T(8,128)(2,1)} %copy-done.7, bf16[13,16,128]{2,1,0:T(8,128)(2,1)} %copy-done.8, bf16[13,16,128]{2,1,0:T(8,128)(2,1)} %copy-done.9, bf16[13,16,128]{2,1,0:T(8,128)(2,1)} %copy-done.10, ...), custom_call_target="tpu_custom_call" | custom-call | tf_op jit(solution)/shard_map/branches/pallas_call | solution.py:198
  99.2 5.1 %all-to-all-start = ((bf16[16,80,128]{2,1,0:T(8,128)(2,1)}), bf16[16,80,128]{2,1,0:T(8,128)(2,1)S(1)}, u32[]{:S(2)}, u32[]{:S(2)}) async-start(bf16[16,80,128]{2,1,0:T(8,128)(2,1)} %branches.1), calls=%async_computation | async-start | bytes 655360 | tf_op jit(solution)/shard_map/all_to_all | solution.py:366
  104.5 8.8 %all-to-all-done.received = bf16[16,80,128]{2,1,0:T(8,128)(2,1)S(1)} async-done(((bf16[16,80,128]{2,1,0:T(8,128)(2,1)}), bf16[16,80,128]{2,1,0:T(8,128)(2,1)S(1)}, u32[]{:S(2)}, u32[]{:S(2)}) %all-to-all-start) | async-done | bytes 327712 | tf_op jit(solution)/shard_map/all_to_all | solution.py:366
  113.3 0.8 copy-done.6
  114.1 2.1 %project.1 = (bf16[144,256]{1,0:T(8,128)(2,1)}, bf16[24,256]{1,0:T(8,128)(2,1)}, bf16[24,256]{1,0:T(8,128)(2,1)}) custom-call(bf16[16,80,128]{2,1,0:T(8,128)(2,1)} %copy-done.6, bf16[1024,256]{1,0:T(8,128)(2,1)} %bitcast.26, bf16[256,256]{1,0:T(8,128)(2,1)} %slice.81.pool_weight, f32[1,256]{1,0:T(1,128)} %bitcast.37), custom_call_target="tpu_custom_call" | custom-call | tf_op jit(solution)/shard_map/project/pallas_call | solution.py:236
  116.2 3.9 %collective-permute-start.23 = (bf16[24,256]{1,0:T(8,128)(2,1)}, bf16[24,256]{1,0:T(8,128)(2,1)S(1)}, u32[]{:S(2)}, u32[]{:S(2)}) collective-permute-start(bf16[24,256]{1,0:T(8,128)(2,1)} %get-tuple-element.24), channel_id=1, source_target_pairs={{0,1},{1,2},{2,3},{3,4},{4,5},{5,6},{6,7},{8,9},{9,10},{10,11},{11... | collective-permute-start | bytes 36872 | tf_op jit(solution)/shard_map/ppermute | solution.py:27
  120.1 1.9 %collective-permute-start.24 = (bf16[24,256]{1,0:T(8,128)(2,1)}, bf16[24,256]{1,0:T(8,128)(2,1)S(1)}, u32[]{:S(2)}, u32[]{:S(2)}) collective-permute-start(bf16[24,256]{1,0:T(8,128)(2,1)} %get-tuple-element.26), channel_id=1, source_target_pairs={{1,0},{2,1},{3,2},{4,3},{5,4},{6,5},{7,6},{9,8},{10,9},{11,10},{12... | collective-permute-start | bytes 36872 | tf_op jit(solution)/shard_map/ppermute | solution.py:27
  122.0 1.0 pad_maximum_fusion.low
  123.1 2.9 %collective-permute-done.24.after = bf16[24,256]{1,0:T(8,128)(2,1)S(1)} collective-permute-done((bf16[24,256]{1,0:T(8,128)(2,1)}, bf16[24,256]{1,0:T(8,128)(2,1)S(1)}, u32[]{:S(2)}, u32[]{:S(2)}) %collective-permute-start.24) | collective-permute-done | bytes 12320 | tf_op jit(solution)/shard_map/ppermute | solution.py:27
  125.9 0.6 copy-done.14
  126.5 5.9 %decode.1 = bf16[16,24,256]{2,1,0:T(8,128)(2,1)} custom-call(s32[3]{0:T(128)} %pad_add_fusion.refs_0_.place, bf16[24,256]{1,0:T(8,128)(2,1)} %copy-done.13, bf16[144,256]{1,0:T(8,128)(2,1)} %get-tuple-element.25.coarse, bf16[24,256]{1,0:T(8,128)(2,1)} %copy-done.14, bf16[640,192]{1,0:T(8,128)(2,1)} %multiply_convert_fusion.spread, ...), custom_call_target="tpu_custom_call" | custom-call | tf_op jit(solution)/shard_map/decode/pallas_call | solution.py:288
  (94 shorter events, 1.6 us)
Async XLA Ops:
  0.0 8.4 %copy-start = (bf16[16,24,256]{2,1,0:T(8,128)(2,1)S(1)}, bf16[16,24,256]{2,1,0:T(8,128)(2,1)}, u32[]{:S(2)}) copy-start(bf16[16,24,256]{2,1,0:T(8,128)(2,1)} %param.15) | copy-start | bytes 589828
  1.9 7.9 %collective-permute-start.8 = (bf16[6,8,2048]{2,1,0:T(8,128)(2,1)S(1)}, bf16[6,8,2048]{2,1,0:T(8,128)(2,1)S(1)}, u32[]{:S(2)}, u32[]{:S(2)}) collective-permute-start(bf16[6,8,2048]{2,1,0:T(8,128)(2,1)S(1)} %get-tuple-element.27), channel_id=1, source_target_pairs={{0,32},{32,64},{64,96},{96,0},{1,33},{33,65},{65,97},{97,1},{2,34}... | collective-permute-start | bytes 589832 | tf_op jit(solution)/shard_map/ppermute | solution.py:21
  3.5 6.7 %collective-permute-start.9 = (bf16[6,8,2048]{2,1,0:T(8,128)(2,1)S(1)}, bf16[6,8,2048]{2,1,0:T(8,128)(2,1)S(1)}, u32[]{:S(2)}, u32[]{:S(2)}) collective-permute-start(bf16[6,8,2048]{2,1,0:T(8,128)(2,1)S(1)} %get-tuple-element.27), channel_id=1, source_target_pairs={{0,96},{32,0},{64,32},{96,64},{1,97},{33,1},{65,33},{97,65},{2,98}... | collective-permute-start | bytes 589832 | tf_op jit(solution)/shard_map/ppermute | solution.py:21
  5.2 8.1 %collective-permute-start = (bf16[6,8,2048]{2,1,0:T(8,128)(2,1)S(1)}, bf16[6,8,2048]{2,1,0:T(8,128)(2,1)S(1)}, u32[]{:S(2)}, u32[]{:S(2)}) collective-permute-start(bf16[6,8,2048]{2,1,0:T(8,128)(2,1)S(1)} %get-tuple-element.30), channel_id=1, source_target_pairs={{0,8},{8,16},{16,24},{24,0},{1,9},{9,17},{17,25},{25,1},{2,10},{10... | collective-permute-start | bytes 589832 | tf_op jit(solution)/shard_map/ppermute | solution.py:21
  6.7 8.2 %collective-permute-start.1 = (bf16[6,8,2048]{2,1,0:T(8,128)(2,1)S(1)}, bf16[6,8,2048]{2,1,0:T(8,128)(2,1)S(1)}, u32[]{:S(2)}, u32[]{:S(2)}) collective-permute-start(bf16[6,8,2048]{2,1,0:T(8,128)(2,1)S(1)} %get-tuple-element.30), channel_id=1, source_target_pairs={{0,24},{8,0},{16,8},{24,16},{1,25},{9,1},{17,9},{25,17},{2,26},{10... | collective-permute-start | bytes 589832 | tf_op jit(solution)/shard_map/ppermute | solution.py:21
  9.9 9.6 %collective-permute-start.10 = (bf16[3,8,2048]{2,1,0:T(8,128)(2,1)S(1)}, bf16[3,8,2048]{2,1,0:T(8,128)(2,1)S(1)}, u32[]{:S(2)}, u32[]{:S(2)}) collective-permute-start(bf16[3,8,2048]{2,1,0:T(8,128)(2,1)S(1)} %slice.98), channel_id=1, source_target_pairs={{0,32},{32,64},{64,96},{96,0},{1,33},{33,65},{65,97},{97,1},{2,34}... | collective-permute-start | bytes 294920 | tf_op jit(solution)/shard_map/ppermute | solution.py:21
  10.3 9.9 %collective-permute-start.11 = (bf16[3,8,2048]{2,1,0:T(8,128)(2,1)S(1)}, bf16[3,8,2048]{2,1,0:T(8,128)(2,1)S(1)}, u32[]{:S(2)}, u32[]{:S(2)}) collective-permute-start(bf16[3,8,2048]{2,1,0:T(8,128)(2,1)S(1)} %slice.99), channel_id=1, source_target_pairs={{0,96},{32,0},{64,32},{96,64},{1,97},{33,1},{65,33},{97,65},{2,98}... | collective-permute-start | bytes 294920 | tf_op jit(solution)/shard_map/ppermute | solution.py:21
  13.3 10.8 %collective-permute-start.2 = (bf16[3,8,2048]{2,1,0:T(8,128)(2,1)S(1)}, bf16[3,8,2048]{2,1,0:T(8,128)(2,1)S(1)}, u32[]{:S(2)}, u32[]{:S(2)}) collective-permute-start(bf16[3,8,2048]{2,1,0:T(8,128)(2,1)S(1)} %slice.93), channel_id=1, source_target_pairs={{0,8},{8,16},{16,24},{24,0},{1,9},{9,17},{17,25},{25,1},{2,10},{10... | collective-permute-start | bytes 294920 | tf_op jit(solution)/shard_map/ppermute | solution.py:21
  14.9 9.8 %collective-permute-start.3 = (bf16[3,8,2048]{2,1,0:T(8,128)(2,1)S(1)}, bf16[3,8,2048]{2,1,0:T(8,128)(2,1)S(1)}, u32[]{:S(2)}, u32[]{:S(2)}) collective-permute-start(bf16[3,8,2048]{2,1,0:T(8,128)(2,1)S(1)} %slice.94), channel_id=1, source_target_pairs={{0,24},{8,0},{16,8},{24,16},{1,25},{9,1},{17,9},{25,17},{2,26},{10... | collective-permute-start | bytes 294920 | tf_op jit(solution)/shard_map/ppermute | solution.py:21
  20.8 18.9 %collective-permute-start.12 = (bf16[24,8,2048]{2,1,0:T(8,128)(2,1)}, bf16[24,8,2048]{2,1,0:T(8,128)(2,1)S(1)}, u32[]{:S(2)}, u32[]{:S(2)}) collective-permute-start(bf16[24,8,2048]{2,1,0:T(8,128)(2,1)} %constant_dynamic-update-slice_fusion.5.refs_6_), channel_id=1, source_target_pairs={{0,8},{8,16},{16,24},{24,0},{1,9},{9,17},{17,25},{25,1},{2,10},{10... | collective-permute-start | bytes 2359304 | tf_op jit(solution)/shard_map/ppermute | solution.py:21
  21.1 20.0 %collective-permute-start.13 = (bf16[24,8,2048]{2,1,0:T(8,128)(2,1)}, bf16[24,8,2048]{2,1,0:T(8,128)(2,1)S(1)}, u32[]{:S(2)}, u32[]{:S(2)}) collective-permute-start(bf16[24,8,2048]{2,1,0:T(8,128)(2,1)} %constant_dynamic-update-slice_fusion.5.refs_6_), channel_id=1, source_target_pairs={{0,24},{8,0},{16,8},{24,16},{1,25},{9,1},{17,9},{25,17},{2,26},{10... | collective-permute-start | bytes 2359304 | tf_op jit(solution)/shard_map/ppermute | solution.py:21
  25.3 19.9 %collective-permute-start.4 = (bf16[24,8,2048]{2,1,0:T(8,128)(2,1)}, bf16[24,8,2048]{2,1,0:T(8,128)(2,1)S(1)}, u32[]{:S(2)}, u32[]{:S(2)}) collective-permute-start(bf16[24,8,2048]{2,1,0:T(8,128)(2,1)} %constant_dynamic-update-slice_fusion.refs_1_), channel_id=1, source_target_pairs={{0,32},{32,64},{64,96},{96,0},{1,33},{33,65},{65,97},{97,1},{2,34}... | collective-permute-start | bytes 2359304 | tf_op jit(solution)/shard_map/ppermute | solution.py:21
  25.3 20.8 %collective-permute-start.5 = (bf16[24,8,2048]{2,1,0:T(8,128)(2,1)}, bf16[24,8,2048]{2,1,0:T(8,128)(2,1)S(1)}, u32[]{:S(2)}, u32[]{:S(2)}) collective-permute-start(bf16[24,8,2048]{2,1,0:T(8,128)(2,1)} %constant_dynamic-update-slice_fusion.refs_1_), channel_id=1, source_target_pairs={{0,96},{32,0},{64,32},{96,64},{1,97},{33,1},{65,33},{97,65},{2,98}... | collective-permute-start | bytes 2359304 | tf_op jit(solution)/shard_map/ppermute | solution.py:21
  28.7 43.6 %collective-permute-start.25 = (bf16[2,24,48]{2,1,0:T(8,128)(2,1)S(1)}, bf16[2,24,48]{2,1,0:T(8,128)(2,1)S(1)}, u32[]{:S(2)}, u32[]{:S(2)}) collective-permute-start(bf16[2,24,48]{2,1,0:T(8,128)(2,1)S(1)} %bitcast.35), channel_id=1, source_target_pairs={{0,8},{8,16},{16,24},{24,32},{32,40},{40,48},{48,56},{56,64},{64,7... | collective-permute-start | bytes 13832 | tf_op jit(solution)/shard_map/ppermute | solution.py:27
  39.7 7.2 %copy-start.2 = (bf16[24,8,2048]{2,1,0:T(8,128)(2,1)}, bf16[24,8,2048]{2,1,0:T(8,128)(2,1)S(1)}, u32[]{:S(2)}) copy-start(bf16[24,8,2048]{2,1,0:T(8,128)(2,1)S(1)} %collective-permute-done.12.refs_7_) | copy-start | bytes 2359300
  40.6 10.3 %collective-permute-start.14 = (bf16[12,8,2048]{2,1,0:T(8,128)(2,1)}, bf16[12,8,2048]{2,1,0:T(8,128)(2,1)}, u32[]{:S(2)}, u32[]{:S(2)}) collective-permute-start(bf16[12,8,2048]{2,1,0:T(8,128)(2,1)} %slice.100), channel_id=1, source_target_pairs={{0,8},{8,16},{16,24},{24,0},{1,9},{9,17},{17,25},{25,1},{2,10},{10... | collective-permute-start | bytes 1179656 | tf_op jit(solution)/shard_map/ppermute | solution.py:21
  41.1 14.7 %copy-start.3 = (bf16[24,8,2048]{2,1,0:T(8,128)(2,1)}, bf16[24,8,2048]{2,1,0:T(8,128)(2,1)S(1)}, u32[]{:S(2)}) copy-start(bf16[24,8,2048]{2,1,0:T(8,128)(2,1)S(1)} %collective-permute-done.13.refs_8_) | copy-start | bytes 2359300
  42.0 11.0 %collective-permute-start.15 = (bf16[12,8,2048]{2,1,0:T(8,128)(2,1)}, bf16[12,8,2048]{2,1,0:T(8,128)(2,1)}, u32[]{:S(2)}, u32[]{:S(2)}) collective-permute-start(bf16[12,8,2048]{2,1,0:T(8,128)(2,1)} %slice.101), channel_id=1, source_target_pairs={{0,24},{8,0},{16,8},{24,16},{1,25},{9,1},{17,9},{25,17},{2,26},{10... | collective-permute-start | bytes 1179656 | tf_op jit(solution)/shard_map/ppermute | solution.py:21
  45.2 10.6 %copy-start.4 = (bf16[24,8,2048]{2,1,0:T(8,128)(2,1)}, bf16[24,8,2048]{2,1,0:T(8,128)(2,1)S(1)}, u32[]{:S(2)}) copy-start(bf16[24,8,2048]{2,1,0:T(8,128)(2,1)S(1)} %collective-permute-done.4.refs_2_) | copy-start | bytes 2359300
  46.1 9.3 %collective-permute-start.6 = (bf16[12,8,2048]{2,1,0:T(8,128)(2,1)}, bf16[12,8,2048]{2,1,0:T(8,128)(2,1)}, u32[]{:S(2)}, u32[]{:S(2)}) collective-permute-start(bf16[12,8,2048]{2,1,0:T(8,128)(2,1)} %slice.95), channel_id=1, source_target_pairs={{0,32},{32,64},{64,96},{96,0},{1,33},{33,65},{65,97},{97,1},{2,34}... | collective-permute-start | bytes 1179656 | tf_op jit(solution)/shard_map/ppermute | solution.py:21
  46.1 9.7 %copy-start.5 = (bf16[24,8,2048]{2,1,0:T(8,128)(2,1)}, bf16[24,8,2048]{2,1,0:T(8,128)(2,1)S(1)}, u32[]{:S(2)}) copy-start(bf16[24,8,2048]{2,1,0:T(8,128)(2,1)S(1)} %collective-permute-done.5.refs_3_) | copy-start | bytes 2359300
  46.9 8.8 %collective-permute-start.7 = (bf16[12,8,2048]{2,1,0:T(8,128)(2,1)}, bf16[12,8,2048]{2,1,0:T(8,128)(2,1)}, u32[]{:S(2)}, u32[]{:S(2)}) collective-permute-start(bf16[12,8,2048]{2,1,0:T(8,128)(2,1)} %slice.96), channel_id=1, source_target_pairs={{0,96},{32,0},{64,32},{96,64},{1,97},{33,1},{65,33},{97,65},{2,98}... | collective-permute-start | bytes 1179656 | tf_op jit(solution)/shard_map/ppermute | solution.py:21
  50.9 24.8 %collective-permute-start.26 = (bf16[2,24,48]{2,1,0:T(8,128)(2,1)S(1)}, bf16[2,24,48]{2,1,0:T(8,128)(2,1)S(1)}, u32[]{:S(2)}, u32[]{:S(2)}) collective-permute-start(bf16[2,24,48]{2,1,0:T(8,128)(2,1)S(1)} %bitcast.36), channel_id=1, source_target_pairs={{8,0},{16,8},{24,16},{32,24},{40,32},{48,40},{56,48},{64,56},{72,6... | collective-permute-start | bytes 13832 | tf_op jit(solution)/shard_map/ppermute | solution.py:27
  55.8 35.1 %copy-start.16 = (s32[192]{0:T(256)S(1)}, s32[192]{0:T(256)}, u32[]{:S(2)}) copy-start(s32[192]{0:T(256)} %get-tuple-element.50) | copy-start | bytes 2308
  55.8 35.1 %copy-start.17 = (pred[640]{0:T(1024)(128)(4,1)S(1)}, pred[640]{0:T(1024)(128)(4,1)}, u32[]{:S(2)}) copy-start(pred[640]{0:T(1024)(128)(4,1)} %get-tuple-element.41) | copy-start | bytes 1924
  55.8 35.1 %copy-start.18 = (pred[640]{0:T(1024)(128)(4,1)S(1)}, pred[640]{0:T(1024)(128)(4,1)}, u32[]{:S(2)}) copy-start(pred[640]{0:T(1024)(128)(4,1)} %get-tuple-element.42) | copy-start | bytes 1924
  55.8 35.1 %copy-start.19 = (pred[640]{0:T(1024)(128)(4,1)S(1)}, pred[640]{0:T(1024)(128)(4,1)}, u32[]{:S(2)}) copy-start(pred[640]{0:T(1024)(128)(4,1)} %get-tuple-element.37) | copy-start | bytes 1924
  55.8 35.1 %copy-start.20 = (pred[640]{0:T(1024)(128)(4,1)S(1)}, pred[640]{0:T(1024)(128)(4,1)}, u32[]{:S(2)}) copy-start(pred[640]{0:T(1024)(128)(4,1)} %get-tuple-element.38) | copy-start | bytes 1924
  55.8 35.1 %copy-start.21 = (s32[192]{0:T(256)S(1)}, s32[192]{0:T(256)}, u32[]{:S(2)}) copy-start(s32[192]{0:T(256)} %get-tuple-element.51) | copy-start | bytes 2308
  55.8 35.1 %copy-start.22 = (s32[192]{0:T(256)S(1)}, s32[192]{0:T(256)}, u32[]{:S(2)}) copy-start(s32[192]{0:T(256)} %get-tuple-element.52) | copy-start | bytes 2308
  55.9 35.1 %copy-start.24 = (pred[192]{0:T(512)(128)(4,1)S(1)}, pred[192]{0:T(512)(128)(4,1)}, u32[]{:S(2)}) copy-start(pred[192]{0:T(512)(128)(4,1)} %get-tuple-element.47) | copy-start | bytes 580
  55.9 35.1 %copy-start.25 = (pred[192]{0:T(512)(128)(4,1)S(1)}, pred[192]{0:T(512)(128)(4,1)}, u32[]{:S(2)}) copy-start(pred[192]{0:T(512)(128)(4,1)} %get-tuple-element.48) | copy-start | bytes 580
  65.8 27.3 %copy-start.1 = (bf16[1280,256]{1,0:T(8,128)(2,1)S(1)}, bf16[1280,256]{1,0:T(8,128)(2,1)}, u32[]{:S(2)}) copy-start(bf16[1280,256]{1,0:T(8,128)(2,1)} %param.20) | copy-start | bytes 1966084
  65.8 28.0 %copy-start.23 = (f32[5,16]{1,0:T(8,128)S(1)}, f32[5,16]{1,0:T(8,128)}, u32[]{:S(2)}) copy-start(f32[5,16]{1,0:T(8,128)} %param.19) | copy-start | bytes 964
  65.8 28.7 %slice-start = ((bf16[1280,256]{1,0:T(8,128)(2,1)}), bf16[1024,256]{1,0:T(8,128)(2,1)S(1)}, s32[]{:S(2)}) async-start(bf16[1280,256]{1,0:T(8,128)(2,1)} %param.20), calls=%async_computation.1 | async-start | bytes 1048576 | tf_op jit(solution)/shard_map/slice | solution.py:368
  65.8 16.2 %collective-permute-start.16 = (bf16[13,16,128]{2,1,0:T(8,128)(2,1)}, bf16[13,16,128]{2,1,0:T(8,128)(2,1)S(1)}, u32[]{:S(2)}, u32[]{:S(2)}) collective-permute-start(bf16[13,16,128]{2,1,0:T(8,128)(2,1)} %get-tuple-element.17), channel_id=1, source_target_pairs={{0,1},{1,2},{2,3},{3,4},{4,5},{5,6},{6,7},{7,0},{8,9},{9,10},{10,1... | collective-permute-start | bytes 159752 | tf_op jit(solution)/shard_map/ppermute | solution.py:21
  67.8 18.0 %collective-permute-start.17 = (bf16[13,16,128]{2,1,0:T(8,128)(2,1)}, bf16[13,16,128]{2,1,0:T(8,128)(2,1)S(1)}, u32[]{:S(2)}, u32[]{:S(2)}) collective-permute-start(bf16[13,16,128]{2,1,0:T(8,128)(2,1)} %get-tuple-element.18), channel_id=1, source_target_pairs={{0,7},{1,0},{2,1},{3,2},{4,3},{5,4},{6,5},{7,6},{8,15},{9,8},{10,9... | collective-permute-start | bytes 159752 | tf_op jit(solution)/shard_map/ppermute | solution.py:21
  67.9 20.9 %collective-permute-start.18 = (bf16[13,16,128]{2,1,0:T(8,128)(2,1)}, bf16[13,16,128]{2,1,0:T(8,128)(2,1)S(1)}, u32[]{:S(2)}, u32[]{:S(2)}) collective-permute-start(bf16[13,16,128]{2,1,0:T(8,128)(2,1)} %get-tuple-element.19), channel_id=1, source_target_pairs={{0,2},{1,3},{2,4},{3,5},{4,6},{5,7},{6,0},{7,1},{8,10},{9,11},{10,... | collective-permute-start | bytes 159752 | tf_op jit(solution)/shard_map/ppermute | solution.py:21
  72.3 7.8 %collective-permute-start.22 = (bf16[16,128]{1,0:T(8,128)(2,1)}, bf16[16,128]{1,0:T(8,128)(2,1)S(1)}, u32[]{:S(2)}, u32[]{:S(2)}) collective-permute-start(bf16[16,128]{1,0:T(8,128)(2,1)} %get-tuple-element.23.refs_6_), channel_id=1, source_target_pairs={{0,4},{1,5},{2,6},{3,7},{4,0},{5,1},{6,2},{7,3},{8,12},{9,13},{10,... | collective-permute-start | bytes 12296 | tf_op jit(solution)/shard_map/ppermute | solution.py:21
  75.7 28.5 %collective-permute-start.27 = (bf16[20,2,48]{2,1,0:T(2,128)(2,1)S(1)}, bf16[20,2,48]{2,1,0:T(2,128)(2,1)S(1)}, u32[]{:S(2)}, u32[]{:S(2)}) collective-permute-start(bf16[20,2,48]{2,1,0:T(2,128)(2,1)S(1)} %get-tuple-element.33), channel_id=1, source_target_pairs={{0,1},{1,2},{2,3},{3,4},{4,5},{5,6},{6,7},{8,9},{9,10},{10,11},{11... | collective-permute-start | bytes 11528 | tf_op jit(solution)/shard_map/ppermute | solution.py:27
  80.2 15.2 %copy-start.15 = (bf16[16,128]{1,0:T(8,128)(2,1)}, bf16[16,128]{1,0:T(8,128)(2,1)S(1)}, u32[]{:S(2)}) copy-start(bf16[16,128]{1,0:T(8,128)(2,1)S(1)} %collective-permute-done.22.refs_7_) | copy-start | bytes 12292
  80.2 24.1 %collective-permute-start.28 = (bf16[20,2,48]{2,1,0:T(2,128)(2,1)S(1)}, bf16[20,2,48]{2,1,0:T(2,128)(2,1)S(1)}, u32[]{:S(2)}, u32[]{:S(2)}) collective-permute-start(bf16[20,2,48]{2,1,0:T(2,128)(2,1)S(1)} %get-tuple-element.34), channel_id=1, source_target_pairs={{1,0},{2,1},{3,2},{4,3},{5,4},{6,5},{7,6},{9,8},{10,9},{11,10},{12... | collective-permute-start | bytes 11528 | tf_op jit(solution)/shard_map/ppermute | solution.py:27
  82.1 13.3 %copy-start.7 = (bf16[13,16,128]{2,1,0:T(8,128)(2,1)}, bf16[13,16,128]{2,1,0:T(8,128)(2,1)S(1)}, u32[]{:S(2)}) copy-start(bf16[13,16,128]{2,1,0:T(8,128)(2,1)S(1)} %collective-permute-done.16.refs_0_) | copy-start | bytes 159748
  82.1 13.3 %collective-permute-start.19 = (bf16[13,16,128]{2,1,0:T(8,128)(2,1)}, bf16[13,16,128]{2,1,0:T(8,128)(2,1)S(1)}, u32[]{:S(2)}, u32[]{:S(2)}) collective-permute-start(bf16[13,16,128]{2,1,0:T(8,128)(2,1)} %get-tuple-element.20), channel_id=1, source_target_pairs={{0,6},{1,7},{2,0},{3,1},{4,2},{5,3},{6,4},{7,5},{8,14},{9,15},{10,... | collective-permute-start | bytes 159752 | tf_op jit(solution)/shard_map/ppermute | solution.py:21
  85.8 9.5 %copy-start.8 = (bf16[13,16,128]{2,1,0:T(8,128)(2,1)}, bf16[13,16,128]{2,1,0:T(8,128)(2,1)S(1)}, u32[]{:S(2)}) copy-start(bf16[13,16,128]{2,1,0:T(8,128)(2,1)S(1)} %collective-permute-done.17.refs_1_) | copy-start | bytes 159748
  85.8 9.5 %collective-permute-start.20 = (bf16[13,16,128]{2,1,0:T(8,128)(2,1)}, bf16[13,16,128]{2,1,0:T(8,128)(2,1)S(1)}, u32[]{:S(2)}, u32[]{:S(2)}) collective-permute-start(bf16[13,16,128]{2,1,0:T(8,128)(2,1)} %get-tuple-element.21), channel_id=1, source_target_pairs={{0,3},{1,4},{2,5},{3,6},{4,7},{5,0},{6,1},{7,2},{8,11},{9,12},{10,... | collective-permute-start | bytes 159752 | tf_op jit(solution)/shard_map/ppermute | solution.py:21
  88.9 6.5 %copy-start.9 = (bf16[13,16,128]{2,1,0:T(8,128)(2,1)}, bf16[13,16,128]{2,1,0:T(8,128)(2,1)S(1)}, u32[]{:S(2)}) copy-start(bf16[13,16,128]{2,1,0:T(8,128)(2,1)S(1)} %collective-permute-done.18.refs_2_) | copy-start | bytes 159748
  88.9 7.4 %collective-permute-start.21 = (bf16[13,16,128]{2,1,0:T(8,128)(2,1)}, bf16[13,16,128]{2,1,0:T(8,128)(2,1)S(1)}, u32[]{:S(2)}, u32[]{:S(2)}) collective-permute-start(bf16[13,16,128]{2,1,0:T(8,128)(2,1)} %get-tuple-element.22), channel_id=1, source_target_pairs={{0,5},{1,6},{2,7},{3,0},{4,1},{5,2},{6,3},{7,4},{8,13},{9,14},{10,... | collective-permute-start | bytes 159752 | tf_op jit(solution)/shard_map/ppermute | solution.py:21
  95.4 0.9 copy-start.10
  95.4 0.9 copy-start.11
  96.2 0.6 copy-start.12
  99.2 14.1 %all-to-all-start = ((bf16[16,80,128]{2,1,0:T(8,128)(2,1)}), bf16[16,80,128]{2,1,0:T(8,128)(2,1)S(1)}, u32[]{:S(2)}, u32[]{:S(2)}) async-start(bf16[16,80,128]{2,1,0:T(8,128)(2,1)} %branches.1), calls=%async_computation | async-start | bytes 655360 | tf_op jit(solution)/shard_map/all_to_all | solution.py:366
  113.3 0.8 copy-start.6
  116.2 6.9 %collective-permute-start.23 = (bf16[24,256]{1,0:T(8,128)(2,1)}, bf16[24,256]{1,0:T(8,128)(2,1)S(1)}, u32[]{:S(2)}, u32[]{:S(2)}) collective-permute-start(bf16[24,256]{1,0:T(8,128)(2,1)} %get-tuple-element.24), channel_id=1, source_target_pairs={{0,1},{1,2},{2,3},{3,4},{4,5},{5,6},{6,7},{8,9},{9,10},{10,11},{11... | collective-permute-start | bytes 36872 | tf_op jit(solution)/shard_map/ppermute | solution.py:27
  120.1 5.8 %collective-permute-start.24 = (bf16[24,256]{1,0:T(8,128)(2,1)}, bf16[24,256]{1,0:T(8,128)(2,1)S(1)}, u32[]{:S(2)}, u32[]{:S(2)}) collective-permute-start(bf16[24,256]{1,0:T(8,128)(2,1)} %get-tuple-element.26), channel_id=1, source_target_pairs={{1,0},{2,1},{3,2},{4,3},{5,4},{6,5},{7,6},{9,8},{10,9},{11,10},{12... | collective-permute-start | bytes 36872 | tf_op jit(solution)/shard_map/ppermute | solution.py:27
  123.1 2.9 %copy-start.13 = (bf16[24,256]{1,0:T(8,128)(2,1)}, bf16[24,256]{1,0:T(8,128)(2,1)S(1)}, u32[]{:S(2)}) copy-start(bf16[24,256]{1,0:T(8,128)(2,1)S(1)} %collective-permute-done.23.before) | copy-start | bytes 36868
  125.9 0.6 copy-start.14

commit v2 on v1

v2 whole, which is shorter than its diff:
```python
import jax
import jax.numpy as jnp
from jax import lax
from jax.experimental import pallas as pl
from jax.experimental.pallas import tpu as pltpu
from jax.sharding import Mesh
from jax.sharding import PartitionSpec as P

ROW = ("row_0", "row_1")
DP_ROW = ("dp", "row_0", "row_1")
RATES = (12, 24, 36)
MAP_ROWS = 128
MAP_COLS = 96
BF = jnp.bfloat16
F32 = jnp.float32
VMEM_BYTES = 56 * 1024 * 1024


def around(value, axis, by):
    devices = lax.axis_size(axis)
    return lax.ppermute(value, axis, [(i, (i + by) % devices) for i in range(devices)])


def next_to(value, axis, by):
    devices = lax.axis_size(axis)
    pairs = [(i, i + by) for i in range(devices) if 0 <= i + by < devices]
    return lax.ppermute(value, axis, pairs)


def swap(value, axis, near):
    pairs = ((0, 1), (2, 3)) if near else ((0, 3), (1, 2))
    return lax.ppermute(value, axis, [way for a, b in pairs for way in ((a, b), (b, a))])


OWN, NEAR, WRAP, FAR = range(4)


def position(index, kind):
    if kind == OWN:
        return index
    if kind == NEAR:
        return index + 1 - 2 * (index % 2)
    if kind == WRAP:
        return 3 - index
    return (index + 2) % 4


def gather_strip(half, first, second):
    near = swap(half, first, True)
    wrap = swap(half, first, False)
    far_low = swap(near[:3], first, False)
    far_high = swap(wrap[3:], first, True)
    low = jnp.concatenate([half, near], axis=0)
    high = jnp.concatenate([wrap, far_low, far_high], axis=0)
    low_near = swap(low, second, True)
    low_wrap = swap(low, second, False)
    high_wrap = swap(high, second, False)
    high_near = swap(high, second, True)
    low_far = swap(low_near, second, False)
    high_far = swap(high_wrap, second, True)
    return [low, high, low_near, high_near, low_wrap, high_wrap, low_far, high_far]


LOW = ((0, 6, 0, OWN), (6, 6, 0, NEAR))
HIGH = ((0, 6, 0, WRAP), (6, 3, 0, FAR), (9, 3, 3, FAR))
PIECES = [
    (2 * which + part, *piece, kind)
    for which, kind in enumerate((OWN, NEAR, WRAP, FAR))
    for part, pieces in enumerate((LOW, HIGH))
    for piece in pieces
]
SIZES = (23, 17, 15)


def products_kernel(*refs):
    refs = (None, *refs)
    parts = (refs[1:9], refs[9:17])
    atrous, point, pool = refs[17:20]
    centre = refs[20]
    sides = refs[21:27]
    opposite = refs[27]
    feats, weights, total, feat_sems, weight_sems = refs[28:33]
    own_y, own_x = lax.axis_index("row_0"), lax.axis_index("row_1")
    copies = []
    for colour in range(2):
        group = []
        for number, (which, start, count, col, first, second) in enumerate(PIECES):
            kind_y, kind_x = (second, first) if colour == 0 else (first, second)
            tile = position(own_y, kind_y) * 4 + position(own_x, kind_x)
            group.append(
                pltpu.make_async_copy(
                    parts[colour][which].at[pl.ds(start, count)],
                    feats.at[pl.ds(6 * colour + col, count), tile],
                    feat_sems.at[colour * len(PIECES) + number],
                )
            )
        copies.append(group)
    loads = [
        pltpu.make_async_copy(atrous, weights.at[pl.ds(0, 432)], weight_sems.at[0]),
        pltpu.make_async_copy(point, weights.at[pl.ds(432, 16)], weight_sems.at[1]),
        pltpu.make_async_copy(pool, weights.at[pl.ds(448, 16)], weight_sems.at[2]),
    ]
    for copy in loads + copies[0] + copies[1]:
        copy.start()
    total[...] = jnp.zeros_like(total)
    lane = lax.broadcasted_iota(jnp.int32, (16, MAP_ROWS), 1)

    def shifted(value, offset):
        if offset == 0:
            return value
        moved = pltpu.roll(value, (-offset) % MAP_ROWS, 1)
        inside = (lane + offset >= 0) & (lane + offset < MAP_ROWS)
        return jnp.where(inside, moved, 0.0)

    def pair(index, carry):
        block = feats[pl.ds(2 * index, 2)].reshape(2 * MAP_ROWS, feats.shape[-1])
        result = lax.dot_general(
            weights[...], block, (((1,), (1,)), ((), ())), preferred_element_type=F32
        )
        for side in range(2):
            col = 2 * index + side
            columns = result[:, side * MAP_ROWS : (side + 1) * MAP_ROWS]

            def group(number, columns=columns):
                return columns[number * 16 : (number + 1) * 16]

            centre[col, 0:16] = group(27)
            for rate in range(3):
                for col_tap in range(3):
                    summed = group(rate * 9 + 3 + col_tap)
                    summed = summed + shifted(group(rate * 9 + col_tap), -RATES[rate])
                    summed = summed + shifted(group(rate * 9 + 6 + col_tap), RATES[rate])
                    if col_tap == 1:
                        centre[col, 16 * (rate + 1) : 16 * (rate + 2)] = summed
                    else:
                        sides[2 * rate + col_tap // 2][col] = summed.astype(BF)
            total[...] += group(28)
        return carry

    for copy in loads + copies[0]:
        copy.wait()
    lax.fori_loop(0, 3, pair, 0)
    for copy in copies[1]:
        copy.wait()
    lax.fori_loop(3, 6, pair, 0)
    strip = jnp.sum(total[...], axis=1, keepdims=True)
    high = strip.astype(BF).astype(F32)
    middle = (strip - high).astype(BF).astype(F32)
    low = strip - high - middle
    terms = jnp.where(lane == 0, high, jnp.where(lane == 1, middle, jnp.where(lane == 2, low, 0.0)))
    terms = terms.astype(BF)
    for rate in range(3):
        for way in range(2):
            sides[2 * rate + way][SIZES[rate] - 1] = terms
    opposite[4] = terms
    for edge in range(2):
        for way in range(2):
            near, middle_rate, far = sides[way], sides[2 + way], sides[4 + way]
            here, there = (edge, 10 + edge) if way == 0 else (10 + edge, edge)
            for branch in range(4):
                piece = centre[there, 16 * branch : 16 * (branch + 1)]
                near[12 + 2 * branch + edge] = piece.astype(BF)
            near[20 + edge] = middle_rate[here]
            middle_rate[12 + edge] = near[there]
            middle_rate[14 + edge] = far[here]
            far[12 + edge] = middle_rate[there]
            opposite[2 - 2 * way + edge] = far[there]


def products(pieces, atrous, point, pool):
    depth = atrous.shape[1]
    sides = [jax.ShapeDtypeStruct((size, 16, MAP_ROWS), BF) for size in SIZES for _ in range(2)]
    anywhere = pl.BlockSpec(memory_space=pl.ANY)
    return pl.pallas_call(
        products_kernel,
        out_shape=[jax.ShapeDtypeStruct((12, 64, MAP_ROWS), F32)]
        + sides
        + [jax.ShapeDtypeStruct((5, 16, MAP_ROWS), BF)],
        in_specs=[anywhere] * 19,
        scratch_shapes=[
            pltpu.VMEM((12, 16, 8, depth), BF),
            pltpu.VMEM((464, depth), BF),
            pltpu.VMEM((16, MAP_ROWS), F32),
            pltpu.SemaphoreType.DMA((2 * len(PIECES),)),
            pltpu.SemaphoreType.DMA((3,)),
        ],
        compiler_params=pltpu.CompilerParams(vmem_limit_bytes=VMEM_BYTES),
        name="products",
    )(*pieces, atrous, point, pool)


def branches_kernel(centre, *refs):
    sides = refs[0:6]
    opposite, own_left, own_right, own_terms, bias, out, rows, slots = refs[6:14]
    strip = lax.axis_index("col")

    diagonal = lax.broadcasted_iota(jnp.int32, (16, 16), 0) == lax.broadcasted_iota(
        jnp.int32, (16, 16), 1
    )

    def bias_column(branch):
        row = jnp.broadcast_to(bias[branch : branch + 1], (16, 16))
        return jnp.sum(jnp.where(diagonal, row, 0.0), axis=1, keepdims=True)

    def brought(distance, index):
        ref = opposite
        if abs(distance) < 4:
            ref = sides[2 * (abs(distance) - 1) + (1 if distance > 0 else 0)]
        source = strip + distance
        inside = (source >= 0) & (source < 8)
        return jnp.where(inside, ref[index].astype(F32), 0.0)

    def column(c16):
        if 2 <= c16 < 14:
            col = c16 - 2
            values = [centre[col, 0:16]]
            for rate in range(3):
                running = centre[col, 16 * (rate + 1) : 16 * (rate + 2)]
                values.append(running + brought(-rate - 1, col) + brought(rate + 1, col))
            return values
        edge = c16 % 2
        side = -1 if c16 < 2 else 1
        own = own_right[10 + edge] if side < 0 else own_left[edge]
        values = [brought(side, 12 + 2 * branch + edge) for branch in range(4)]
        last = 2 + edge if side < 0 else edge
        values[1] = values[1] + brought(2 * side, 12 + edge) + own.astype(F32)
        values[2] = values[2] + brought(3 * side, 12 + edge) + brought(-side, 20 + edge)
        values[3] = values[3] + brought(4 * side, last) + brought(-2 * side, 14 + edge)
        return values

    for c8 in range(8):
        values = column(c8) + column(c8 + 8)
        biases = [bias_column(k % 4) for k in range(8)]
        block = jnp.concatenate([v + b for v, b in zip(values, biases)], axis=0)
        rows[c8, 0:8] = jnp.zeros((8, 128), F32)
        rows[c8, 8:136] = jnp.maximum(block, 0.0).T
        rows[c8, 136:144] = jnp.zeros((8, 128), F32)
    terms = own_terms[4].astype(F32) + opposite[4].astype(F32)
    for rate in range(3):
        for way in range(2):
            terms = terms + sides[2 * rate + way][SIZES[rate] - 1].astype(F32)
    mean = jnp.sum(terms, axis=1, keepdims=True) / (MAP_ROWS * MAP_COLS)
    branch = jnp.maximum(mean + bias_column(4), 0.0)
    wide = jnp.concatenate(
        [jnp.broadcast_to(branch, (16, 128)), jnp.zeros((112, 128), F32)], axis=0
    ).T
    for slot in range(16):
        for c8 in range(8):
            slots[slot, c8 * 12 : c8 * 12 + 12] = rows[c8, 8 * slot + 6 : 8 * slot + 18]
        slots[slot, 96:104] = wide[0:8]
        out[slot] = slots[slot].astype(BF)


def branches(centre, moved, opposite, own_left, own_right, own_terms, bias):
    vmem = pl.BlockSpec(memory_space=pltpu.VMEM)
    return pl.pallas_call(
        branches_kernel,
        out_shape=jax.ShapeDtypeStruct((16, 104, 128), BF),
        in_specs=[vmem] * 12,
        scratch_shapes=[pltpu.VMEM((8, 144, 128), F32), pltpu.VMEM((16, 104, 128), F32)],
        compiler_params=pltpu.CompilerParams(vmem_limit_bytes=VMEM_BYTES),
        name="branches",
    )(centre, *moved, opposite, own_left, own_right, own_terms, bias)


def coarse_tile(received, weight, pool_weight, bias):
    lane = lax.broadcasted_iota(jnp.int32, (104, 128), 1)
    blocks = [received[source].astype(F32) for source in range(16)]
    turned = [pltpu.roll(block, 64, 1) for block in blocks]
    halves = []
    for half in range(2):
        pieces = []
        for source in range(0, 16, 2):
            left = blocks[source] if half == 0 else turned[source]
            right = turned[source + 1] if half == 0 else blocks[source + 1]
            pieces.append(jnp.where(lane < 64, left, right)[0:96])
        halves.append(jnp.concatenate(pieces, axis=1))
    stacked = jnp.concatenate(halves, axis=0).astype(BF)
    low = blocks[0][96:104]
    high = blocks[8][96:104]
    for source in range(1, 8):
        low = low + pltpu.roll(blocks[source][96:104], 16 * source, 1)
        high = high + pltpu.roll(blocks[source + 8][96:104], 16 * source, 1)
    vector = jnp.concatenate([low, high], axis=1).astype(BF)
    constant = jnp.dot(vector, pool_weight, preferred_element_type=F32)[0:1]
    summed = jnp.dot(stacked, weight, preferred_element_type=F32)
    return jnp.maximum(summed + constant + bias[...], 0.0).astype(BF)


def decode_kernel(*refs):
    received, proj, bias, spread, low, w1_hbm, b1, w2_hbm, b2 = refs[0:9]
    out, fine, fine_cols, mid, mid_cols, w1, w2, weight, last, sems = refs[9:]
    loads = [
        pltpu.make_async_copy(w1_hbm, w1, sems.at[0]),
        pltpu.make_async_copy(w2_hbm, w2, sems.at[1]),
    ]
    small_loads = [
        pltpu.make_async_copy(proj.at[branch], weight.at[:, branch], sems.at[2 + branch])
        for branch in range(4)
    ]
    small_loads.append(pltpu.make_async_copy(proj.at[4], last, sems.at[6]))
    for load in small_loads + loads:
        load.start()
    for load in small_loads:
        load.wait()
    coarse = coarse_tile(
        received, weight[...].reshape(1024, 256), last[...].reshape(256, 256), bias
    )
    fine[0:640] = jnp.dot(spread[...], coarse, preferred_element_type=F32)
    fine[640:656] = jnp.zeros((16, 256), F32)
    for tap in range(3):
        fine_cols[tap] = fine[tap : tap + 640].astype(BF)
    loads[0].wait()
    acc = jnp.zeros((576, 256), F32)
    for row_tap in range(3):
        rows = slice(row_tap * 32, row_tap * 32 + 576)
        for tap in range(3):
            acc = acc + jnp.dot(
                fine_cols[tap, rows], w1[row_tap, tap, 0:256], preferred_element_type=F32
            )
        small = jnp.concatenate([w1[row_tap, tap, 256:304] for tap in range(3)], axis=0)
        acc = acc + jnp.dot(low[rows], small, preferred_element_type=F32)
    at = lax.broadcasted_iota(jnp.int32, (576, 256), 0)
    y = 16 * (lax.axis_index("row_0") * 4 + lax.axis_index("row_1")) - 1 + (at >> 5)
    x = 24 * lax.axis_index("col") - 1 + (at & 31)
    inside = (y >= 0) & (y < 2 * MAP_ROWS) & (x >= 0) & (x < 2 * MAP_COLS)
    mid[0:576] = jnp.where(inside, jnp.maximum(acc + b1[...], 0.0), 0.0)
    mid[576:592] = jnp.zeros((16, 256), F32)
    for tap in range(3):
        mid_cols[tap] = mid[tap : tap + 576].astype(BF)
    loads[1].wait()
    acc = jnp.zeros((512, 256), F32)
    for row_tap in range(3):
        for tap in range(3):
            acc = acc + jnp.dot(
                mid_cols[tap, row_tap * 32 : row_tap * 32 + 512],
                w2[row_tap, tap],
                preferred_element_type=F32,
            )
    result = jnp.maximum(acc + b2[...], 0.0).astype(BF).reshape(16, 32, 256)
    out[...] = result[:, 0:24]


def decode(received, proj, bias, spread, low, w1, b1, w2, b2):
    vmem = pl.BlockSpec(memory_space=pltpu.VMEM)
    hbm = pl.BlockSpec(memory_space=pl.ANY)
    return pl.pallas_call(
        decode_kernel,
        out_shape=jax.ShapeDtypeStruct((16, 24, 256), BF),
        in_specs=[vmem, hbm, vmem, vmem, vmem, hbm, vmem, hbm, vmem],
        scratch_shapes=[
            pltpu.VMEM((656, 256), F32),
            pltpu.VMEM((3, 640, 256), BF),
            pltpu.VMEM((592, 256), F32),
            pltpu.VMEM((3, 576, 256), BF),
            pltpu.VMEM(w1.shape, BF),
            pltpu.VMEM(w2.shape, BF),
            pltpu.VMEM((16, 4, 16, 256), BF),
            pltpu.VMEM((16, 16, 256), BF),
            pltpu.SemaphoreType.DMA((7,)),
        ],
        compiler_params=pltpu.CompilerParams(vmem_limit_bytes=VMEM_BYTES),
        name="decode",
    )(received, proj, bias, spread, low, w1, b1, w2, b2)


def spread_kernel(out):
    n = lax.broadcasted_iota(jnp.int32, (640, 192), 0)
    m = lax.broadcasted_iota(jnp.int32, (640, 192), 1)
    col = (m * 683) >> 13
    row_index = lax.axis_index("row_0") * 4 + lax.axis_index("row_1")
    strip = lax.axis_index("col")

    def weights(fine, size, coarse):
        near = fine >> 1
        other = jnp.where((fine & 1) == 1, near + 1, near - 1)
        other = jnp.clip(other, 0, size - 1)
        value = jnp.where(coarse == near, 0.75, 0.0) + jnp.where(coarse == other, 0.25, 0.0)
        return jnp.where((fine >= 0) & (fine < 2 * size), value, 0.0)

    rows = weights(16 * row_index - 2 + (n >> 5), MAP_ROWS, 8 * row_index - 2 + m - 12 * col)
    cols = weights(24 * strip - 2 + (n & 31), MAP_COLS, 12 * strip - 2 + col)
    out[...] = (rows * cols).astype(BF)


def spread_matrix():
    return pl.pallas_call(
        spread_kernel,
        out_shape=jax.ShapeDtypeStruct((640, 192), BF),
        name="spread",
    )()


def reduce_low(low_level, weight, bias):
    reduced = jnp.dot(
        low_level.reshape(-1, low_level.shape[2]), weight, preferred_element_type=F32
    )
    reduced = jnp.maximum(reduced + bias, 0.0).astype(BF).reshape(16, 24, -1)
    return reduced


def low_columns(above, wide, below):
    full = jnp.concatenate([above, wide, below], axis=0)
    full = jnp.pad(full, ((0, 1), (0, 4), (0, 0))).reshape(672, -1)
    return jnp.concatenate([full[tap : tap + 640] for tap in range(3)], axis=1)


def on_device(
    features,
    low_level,
    point_weight,
    atrous_weight,
    pool_weight,
    aspp_bias,
    proj_weight,
    proj_bias,
    low_weight,
    low_bias,
    conv1_weight,
    conv1_bias,
    conv2_weight,
    conv2_bias,
):
    in_width = features.shape[2]
    tile = jnp.transpose(features, (1, 0, 2))
    reduced = reduce_low(low_level, low_weight, low_bias)
    before = next_to(reduced[:, 22:24], "col", 1)
    after = next_to(reduced[:, 0:2], "col", -1)
    wide = jnp.concatenate([before, reduced, after], axis=1)
    above = next_to(wide[14:16], ROW, 1)
    below = next_to(wide[0:2], ROW, -1)
    low = low_columns(above, wide, below)
    pieces = gather_strip(tile[:6], "row_1", "row_0")
    pieces += gather_strip(tile[6:], "row_0", "row_1")
    spread = spread_matrix()
    atrous = jnp.transpose(atrous_weight, (0, 1, 2, 4, 3)).reshape(432, in_width)
    centre, *sides, opposite = products(pieces, atrous, point_weight.T, pool_weight.T)
    moved = []
    for rate in range(3):
        moved.append(around(sides[2 * rate], "col", rate + 1))
        moved.append(around(sides[2 * rate + 1], "col", -rate - 1))
    across = around(opposite, "col", 4)
    mine = branches(centre, moved, across, sides[0], sides[1], opposite, aspp_bias)
    received = lax.all_to_all(mine, ROW, split_axis=0, concat_axis=0, tiled=True)
    return decode(
        received,
        proj_weight.reshape(5, 16, 16, 256),
        proj_bias.reshape(1, 256),
        spread,
        low,
        conv1_weight,
        conv1_bias.reshape(1, 256),
        conv2_weight,
        conv2_bias.reshape(1, 256),
    )


def solution(mesh):
    torus = Mesh(
        mesh.devices.reshape(mesh.shape["dp"], 4, 4, mesh.shape["col"]),
        ("dp", "row_0", "row_1", "col"),
    )
    placed = (
        P(DP_ROW, "col", None),
        P(DP_ROW, "col", None),
        P(None, ROW),
        P(None, None, None, None, ROW),
        P(None, ROW),
        P(None, ROW),
        P(),
        P(),
        P(),
        P(),
        P(),
        P(),
        P(),
        P(),
    )
    return jax.shard_map(
        on_device, mesh=torus, in_specs=placed, out_specs=P(DP_ROW, "col", None), check_vma=False
    )
```

time: 133 us -> 137 us (1.030)
  waiting for transfers between devices: 25 us -> 53.8 us
  local copies, waits for them, and re-layouts: 15.5 us -> 3.64 us
  starting transfers between devices: 63.4 us -> 56.5 us
  other arithmetic: 6.82 us -> 1.18 us
    ppermute x0 -> x20, waiting for transfers between devices: none -> 39.4 us  [swap(): lax.ppermute(value, axis, [way for a, b in pairs for way in ((a, b), (b,...]
    ppermute x23 -> x7, starting transfers between devices: 44.8 us -> 16.8 us  [around(): lax.ppermute(value, axis, [(i, (i + by) % devices) for i in range(devices)])]
    ppermute x0 -> x20, starting transfers between devices: none -> 21.6 us  [swap(): lax.ppermute(value, axis, [way for a, b in pairs for way in ((a, b), (b,...]
    ppermute x23 -> x7, waiting for transfers between devices: 13.3 us -> 5.63 us  [around(): lax.ppermute(value, axis, [(i, (i + by) % devices) for i in range(devices)])]
    slice x16 -> x6, local copies, waits for them, and re-layouts: 7.16 us -> 1.14 us  [the longest x1 1.09 us: on_device(): pieces += gather_strip(tile[6:], 'row_0', 'row_1')]
    unnamed x58 -> x46, local copies, waits for them, and re-layouts: 6.14 us -> 2.27 us
    ppermute x6 -> x4, starting transfers between devices: 13.5 us -> 10.7 us  [next_to(): return lax.ppermute(value, axis, pairs)]
    ppermute x6 -> x4, waiting for transfers between devices: 2.86 us -> 0.42 us  [next_to(): return lax.ppermute(value, axis, pairs)]
  transfers between devices with their start and end apart: 30 -> 32, of which waited for: 8 -> 15; matrix products, arithmetic and copies ran while one was open for 15% -> 1% of each run, Pallas kernels for 9% -> 3%
where the time goes in v2:
time: 137 us; the launch traced here: 136 us
  starting transfers between devices  56.5 us (41%)
  waiting for transfers between devices  53.8 us (39%)
  Pallas kernels  20.3 us (15%)
  local copies, waits for them, and re-layouts  3.64 us (3%)
    ppermute x20, waiting for transfers between devices, swap(): lax.ppermute(value, axis, [way for a, b in pairs for way in ((a, b), (b,...  39.4 us
    ppermute x20, starting transfers between devices, swap(): lax.ppermute(value, axis, [way for a, b in pairs for way in ((a, b), (b,...  21.6 us
    ppermute x7, starting transfers between devices, around(): lax.ppermute(value, axis, [(i, (i + by) % devices) for i in range(devices)])  16.8 us
    ppermute x4, starting transfers between devices, next_to(): return lax.ppermute(value, axis, pairs)  10.7 us
    pallas_call x1, Pallas kernels, products(): pl.pallas_call(products_kernel, out_shape=[jax.ShapeDtypeStruct((12, 64,...  9.37 us
    all_to_all x1, waiting for transfers between devices, on_device(): lax.all_to_all(mine, ROW, split_axis=0, concat_axis=0, tiled=True)  8.34 us
    all_to_all x1, starting transfers between devices, on_device(): lax.all_to_all(mine, ROW, split_axis=0, concat_axis=0, tiled=True)  7.44 us
    pallas_call x1, Pallas kernels, decode(): pl.pallas_call(decode_kernel, out_shape=jax.ShapeDtypeStruct((16, 24, 256...  7.18 us
  transfers between devices with their start and end apart: 32, of which 15 were waited for; matrix products, arithmetic and copies ran while one was open for 1% of the time, Pallas kernels for 3%

profile of v2, /device:TPU:32, one launch (start us, length us, event | category | flops | bytes accessed | tf_op | source)
XLA Modules:
  0.0 136.2 jit_solution(8581724833258704319)
XLA Ops:
  0.0 1.1 fusion.17
  1.1 1.7 %collective-permute-start.10 = (bf16[6,8,2048]{2,1,0:T(8,128)(2,1)S(1)}, bf16[6,8,2048]{2,1,0:T(8,128)(2,1)S(1)}, u32[]{:S(2)}, u32[]{:S(2)}) collective-permute-start(bf16[6,8,2048]{2,1,0:T(8,128)(2,1)S(1)} %get-tuple-element.21), channel_id=1, source_target_pairs={{0,32},{32,0},{64,96},{96,64},{1,33},{33,1},{65,97},{97,65},{2,34}... | collective-permute-start | bytes 589832 | tf_op jit(solution)/shard_map/ppermute | solution.py:32
  2.8 2.2 %collective-permute-start.11 = (bf16[6,8,2048]{2,1,0:T(8,128)(2,1)S(1)}, bf16[6,8,2048]{2,1,0:T(8,128)(2,1)S(1)}, u32[]{:S(2)}, u32[]{:S(2)}) collective-permute-start(bf16[6,8,2048]{2,1,0:T(8,128)(2,1)S(1)} %get-tuple-element.21), channel_id=1, source_target_pairs={{0,96},{96,0},{32,64},{64,32},{1,97},{97,1},{33,65},{65,33},{2,98}... | collective-permute-start | bytes 589832 | tf_op jit(solution)/shard_map/ppermute | solution.py:32
  4.9 2.8 %collective-permute-start.1 = (bf16[6,8,2048]{2,1,0:T(8,128)(2,1)S(1)}, bf16[6,8,2048]{2,1,0:T(8,128)(2,1)S(1)}, u32[]{:S(2)}, u32[]{:S(2)}) collective-permute-start(bf16[6,8,2048]{2,1,0:T(8,128)(2,1)S(1)} %get-tuple-element.22), channel_id=1, source_target_pairs={{0,24},{24,0},{8,16},{16,8},{1,25},{25,1},{9,17},{17,9},{2,26},{26... | collective-permute-start | bytes 589832 | tf_op jit(solution)/shard_map/ppermute | solution.py:32
  7.7 0.2 collective-permute-start
  8.0 0.0 copy-start.18
  8.0 0.0 copy-start.20
  8.0 1.9 %collective-permute-start.14 = (bf16[12,8,2048]{2,1,0:T(8,128)(2,1)S(1)}, bf16[12,8,2048]{2,1,0:T(8,128)(2,1)S(1)}, u32[]{:S(2)}, u32[]{:S(2)}) collective-permute-start(bf16[12,8,2048]{2,1,0:T(8,128)(2,1)S(1)} %pad_maximum_fusion.1.refs_8_), channel_id=1, source_target_pairs={{0,8},{8,0},{16,24},{24,16},{1,9},{9,1},{17,25},{25,17},{2,10},{10... | collective-permute-start | bytes 1179656 | tf_op jit(solution)/shard_map/ppermute | solution.py:32
  9.9 1.7 %collective-permute-start.16 = (bf16[12,8,2048]{2,1,0:T(8,128)(2,1)S(1)}, bf16[12,8,2048]{2,1,0:T(8,128)(2,1)S(1)}, u32[]{:S(2)}, u32[]{:S(2)}) collective-permute-start(bf16[12,8,2048]{2,1,0:T(8,128)(2,1)S(1)} %pad_maximum_fusion.1.refs_8_), channel_id=1, source_target_pairs={{0,24},{24,0},{8,16},{16,8},{1,25},{25,1},{9,17},{17,9},{2,26},{26... | collective-permute-start | bytes 1179656 | tf_op jit(solution)/shard_map/ppermute | solution.py:32
  11.6 3.9 %collective-permute-done = bf16[6,8,2048]{2,1,0:T(8,128)(2,1)S(1)} collective-permute-done((bf16[6,8,2048]{2,1,0:T(8,128)(2,1)S(1)}, bf16[6,8,2048]{2,1,0:T(8,128)(2,1)S(1)}, u32[]{:S(2)}, u32[]{:S(2)}) %collective-permute-start) | collective-permute-done | bytes 196640 | tf_op jit(solution)/shard_map/ppermute | solution.py:32
  15.5 0.8 collective-permute-start.4
  16.3 0.7 collective-permute-start.6
  17.0 0.0 collective-permute-done.1
  17.0 2.7 %collective-permute-start.12 = (bf16[3,8,2048]{2,1,0:T(8,128)(2,1)S(1)}, bf16[3,8,2048]{2,1,0:T(8,128)(2,1)S(1)}, u32[]{:S(2)}, u32[]{:S(2)}) collective-permute-start(bf16[3,8,2048]{2,1,0:T(8,128)(2,1)S(1)} %slice.60), channel_id=1, source_target_pairs={{0,96},{96,0},{32,64},{64,32},{1,97},{97,1},{33,65},{65,33},{2,98}... | collective-permute-start | bytes 294920 | tf_op jit(solution)/shard_map/ppermute | solution.py:32
  19.8 6.8 %collective-permute-done.12 = bf16[3,8,2048]{2,1,0:T(8,128)(2,1)S(1)} collective-permute-done((bf16[3,8,2048]{2,1,0:T(8,128)(2,1)S(1)}, bf16[3,8,2048]{2,1,0:T(8,128)(2,1)S(1)}, u32[]{:S(2)}, u32[]{:S(2)}) %collective-permute-start.12) | collective-permute-done | bytes 98336 | tf_op jit(solution)/shard_map/ppermute | solution.py:32
  26.6 0.1 collective-permute-start.13
  26.8 4.5 %collective-permute-done.13 = bf16[3,8,2048]{2,1,0:T(8,128)(2,1)S(1)} collective-permute-done((bf16[3,8,2048]{2,1,0:T(8,128)(2,1)S(1)}, bf16[3,8,2048]{2,1,0:T(8,128)(2,1)S(1)}, u32[]{:S(2)}, u32[]{:S(2)}) %collective-permute-start.13) | collective-permute-done | bytes 98336 | tf_op jit(solution)/shard_map/ppermute | solution.py:32
  31.2 0.5 collective-permute-start.2
  31.7 5.3 %collective-permute-done.2 = bf16[3,8,2048]{2,1,0:T(8,128)(2,1)S(1)} collective-permute-done((bf16[3,8,2048]{2,1,0:T(8,128)(2,1)S(1)}, bf16[3,8,2048]{2,1,0:T(8,128)(2,1)S(1)}, u32[]{:S(2)}, u32[]{:S(2)}) %collective-permute-start.2) | collective-permute-done | bytes 98336 | tf_op jit(solution)/shard_map/ppermute | solution.py:32
  37.1 0.0 collective-permute-start.3
  37.1 5.6 %collective-permute-done.3 = bf16[3,8,2048]{2,1,0:T(8,128)(2,1)S(1)} collective-permute-done((bf16[3,8,2048]{2,1,0:T(8,128)(2,1)S(1)}, bf16[3,8,2048]{2,1,0:T(8,128)(2,1)S(1)}, u32[]{:S(2)}, u32[]{:S(2)}) %collective-permute-start.3) | collective-permute-done | bytes 98336 | tf_op jit(solution)/shard_map/ppermute | solution.py:32
  42.7 0.4 collective-permute-start.17
  43.1 0.0 collective-permute-done.14.refs_10_
  43.1 2.3 %collective-permute-start.7 = (bf16[12,8,2048]{2,1,0:T(8,128)(2,1)S(1)}, bf16[12,8,2048]{2,1,0:T(8,128)(2,1)}, u32[]{:S(2)}, u32[]{:S(2)}) collective-permute-start(bf16[12,8,2048]{2,1,0:T(8,128)(2,1)S(1)} %constant_dynamic-update-slice_fusion.refs_1_), channel_id=1, source_target_pairs={{0,96},{96,0},{32,64},{64,32},{1,97},{97,1},{33,65},{65,33},{2,98}... | collective-permute-start | bytes 1179656 | tf_op jit(solution)/shard_map/ppermute | solution.py:32
  45.4 0.0 collective-permute-done.4.refs_2_
  45.5 0.1 collective-permute-start.5
  45.6 2.2 %collective-permute-start.18 = (bf16[12,8,2048]{2,1,0:T(8,128)(2,1)S(1)}, bf16[12,8,2048]{2,1,0:T(8,128)(2,1)}, u32[]{:S(2)}, u32[]{:S(2)}) collective-permute-start(bf16[12,8,2048]{2,1,0:T(8,128)(2,1)S(1)} %collective-permute-done.14.refs_10_), channel_id=1, source_target_pairs={{0,24},{24,0},{8,16},{16,8},{1,25},{25,1},{9,17},{17,9},{2,26},{26... | collective-permute-start | bytes 1179656 | tf_op jit(solution)/shard_map/ppermute | solution.py:32
  47.8 4.1 %collective-permute-done.17.refs_13_ = bf16[12,8,2048]{2,1,0:T(8,128)(2,1)} collective-permute-done((bf16[12,8,2048]{2,1,0:T(8,128)(2,1)S(1)}, bf16[12,8,2048]{2,1,0:T(8,128)(2,1)}, u32[]{:S(2)}, u32[]{:S(2)}) %collective-permute-start.17) | collective-permute-done | bytes 393248 | tf_op jit(solution)/shard_map/ppermute | solution.py:32
  51.8 1.4 %collective-permute-start.8 = (bf16[12,8,2048]{2,1,0:T(8,128)(2,1)S(1)}, bf16[12,8,2048]{2,1,0:T(8,128)(2,1)}, u32[]{:S(2)}, u32[]{:S(2)}) collective-permute-start(bf16[12,8,2048]{2,1,0:T(8,128)(2,1)S(1)} %collective-permute-done.4.refs_2_), channel_id=1, source_target_pairs={{0,96},{96,0},{32,64},{64,32},{1,97},{97,1},{33,65},{65,33},{2,98}... | collective-permute-start | bytes 1179656 | tf_op jit(solution)/shard_map/ppermute | solution.py:32
  53.3 0.6 collective-permute-done.7.refs_5_
  53.8 0.9 collective-permute-done.15.refs_11_
  54.7 0.7 copy-done.10
  55.5 0.0 collective-permute-start.9
  55.5 0.2 fusion.1
  55.7 0.1 copy.18
  55.8 1.5 %collective-permute-done.5.refs_3_ = bf16[12,8,2048]{2,1,0:T(8,128)(2,1)S(1)} collective-permute-done((bf16[12,8,2048]{2,1,0:T(8,128)(2,1)S(1)}, bf16[12,8,2048]{2,1,0:T(8,128)(2,1)S(1)}, u32[]{:S(2)}, u32[]{:S(2)}) %collective-permute-start.5) | collective-permute-done | bytes 393248 | tf_op jit(solution)/shard_map/ppermute | solution.py:32
  57.3 3.6 %collective-permute-done.8.refs_6_ = bf16[12,8,2048]{2,1,0:T(8,128)(2,1)} collective-permute-done((bf16[12,8,2048]{2,1,0:T(8,128)(2,1)S(1)}, bf16[12,8,2048]{2,1,0:T(8,128)(2,1)}, u32[]{:S(2)}, u32[]{:S(2)}) %collective-permute-start.8) | collective-permute-done | bytes 393248 | tf_op jit(solution)/shard_map/ppermute | solution.py:32
  60.9 1.0 collective-permute-done.19.refs_15_
  61.9 1.6 %collective-permute-done.9.refs_7_ = bf16[12,8,2048]{2,1,0:T(8,128)(2,1)} collective-permute-done((bf16[12,8,2048]{2,1,0:T(8,128)(2,1)}, bf16[12,8,2048]{2,1,0:T(8,128)(2,1)}, u32[]{:S(2)}, u32[]{:S(2)}) %collective-permute-start.9) | collective-permute-done | bytes 393248 | tf_op jit(solution)/shard_map/ppermute | solution.py:32
  63.6 9.4 %products.1 = (f32[12,64,128]{2,1,0:T(8,128)}, bf16[23,16,128]{2,1,0:T(8,128)(2,1)}, bf16[23,16,128]{2,1,0:T(8,128)(2,1)}, bf16[17,16,128]{2,1,0:T(8,128)(2,1)},...) custom-call(bf16[12,8,2048]{2,1,0:T(8,128)(2,1)} %copy-done.3, ...), custom_call_target="tpu_custom_call" | custom-call | tf_op jit(solution)/shard_map/products/pallas_call | solution.py:174
  73.0 5.9 %collective-permute-start.24 = (bf16[15,16,128]{2,1,0:T(8,128)(2,1)}, bf16[15,16,128]{2,1,0:T(8,128)(2,1)S(1)}, u32[]{:S(2)}, u32[]{:S(2)}) collective-permute-start(bf16[15,16,128]{2,1,0:T(8,128)(2,1)} %get-tuple-element.18), channel_id=1, source_target_pairs={{0,3},{1,4},{2,5},{3,6},{4,7},{5,0},{6,1},{7,2},{8,11},{9,12},{10,... | collective-permute-start | bytes 184328 | tf_op jit(solution)/shard_map/ppermute | solution.py:21
  78.9 0.5 collective-permute-start.26
  79.5 2.9 %collective-permute-start.27 = (bf16[16,2,48]{2,1,0:T(2,128)(2,1)S(1)}, bf16[16,2,48]{2,1,0:T(2,128)(2,1)S(1)}, u32[]{:S(2)}, u32[]{:S(2)}) collective-permute-start(bf16[16,2,48]{2,1,0:T(2,128)(2,1)S(1)} %get-tuple-element.27), channel_id=1, source_target_pairs={{0,1},{1,2},{2,3},{3,4},{4,5},{5,6},{6,7},{8,9},{9,10},{10,11},{11... | collective-permute-start | bytes 9224 | tf_op jit(solution)/shard_map/ppermute | solution.py:27
  82.4 3.1 %collective-permute-start.28 = (bf16[16,2,48]{2,1,0:T(2,128)(2,1)S(1)}, bf16[16,2,48]{2,1,0:T(2,128)(2,1)S(1)}, u32[]{:S(2)}, u32[]{:S(2)}) collective-permute-start(bf16[16,2,48]{2,1,0:T(2,128)(2,1)S(1)} %get-tuple-element.28), channel_id=1, source_target_pairs={{1,0},{2,1},{3,2},{4,3},{5,4},{6,5},{7,6},{9,8},{10,9},{11,10},{12... | collective-permute-start | bytes 9224 | tf_op jit(solution)/shard_map/ppermute | solution.py:27
  85.5 0.9 collective-permute-start.20
  86.4 1.2 collective-permute-start.21
  87.6 0.4 collective-permute-done.28
  88.0 4.9 %collective-permute-start.22 = (bf16[17,16,128]{2,1,0:T(8,128)(2,1)}, bf16[17,16,128]{2,1,0:T(8,128)(2,1)S(1)}, u32[]{:S(2)}, u32[]{:S(2)}) collective-permute-start(bf16[17,16,128]{2,1,0:T(8,128)(2,1)} %get-tuple-element.16), channel_id=1, source_target_pairs={{0,2},{1,3},{2,4},{3,5},{4,6},{5,7},{6,0},{7,1},{8,10},{9,11},{10,... | collective-permute-start | bytes 208904 | tf_op jit(solution)/shard_map/ppermute | solution.py:21
  93.0 3.3 %collective-permute-start.25 = (bf16[15,16,128]{2,1,0:T(8,128)(2,1)}, bf16[15,16,128]{2,1,0:T(8,128)(2,1)S(1)}, u32[]{:S(2)}, u32[]{:S(2)}) collective-permute-start(bf16[15,16,128]{2,1,0:T(8,128)(2,1)} %get-tuple-element.19), channel_id=1, source_target_pairs={{0,5},{1,6},{2,7},{3,0},{4,1},{5,2},{6,3},{7,4},{8,13},{9,14},{10,... | collective-permute-start | bytes 184328 | tf_op jit(solution)/shard_map/ppermute | solution.py:21
  96.3 5.6 %collective-permute-done.25.refs_5_ = bf16[15,16,128]{2,1,0:T(8,128)(2,1)S(1)} collective-permute-done((bf16[15,16,128]{2,1,0:T(8,128)(2,1)}, bf16[15,16,128]{2,1,0:T(8,128)(2,1)S(1)}, u32[]{:S(2)}, u32[]{:S(2)}) %collective-permute-start.25) | collective-permute-done | bytes 61472 | tf_op jit(solution)/shard_map/ppermute | solution.py:21
  101.9 3.4 %collective-permute-start.29 = (bf16[2,28,48]{2,1,0:T(8,128)(2,1)S(1)}, bf16[2,28,48]{2,1,0:T(8,128)(2,1)S(1)}, u32[]{:S(2)}, u32[]{:S(2)}) collective-permute-start(bf16[2,28,48]{2,1,0:T(8,128)(2,1)S(1)} %get-tuple-element.25), channel_id=1, source_target_pairs={{0,8},{8,16},{16,24},{24,32},{32,40},{40,48},{48,56},{56,64},{64,7... | collective-permute-start | bytes 16136 | tf_op jit(solution)/shard_map/ppermute | solution.py:27
  105.3 1.3 collective-permute-start.30
  106.6 1.3 spread.1.refs_3_
  108.0 0.6 copy-done.15
  108.6 0.1 copy-done.12
  108.6 0.0 copy-done.13
  108.6 2.4 %branches.1 = bf16[16,104,128]{2,1,0:T(8,128)(2,1)} custom-call(f32[12,64,128]{2,1,0:T(8,128)} %get-tuple-element.13.centre, bf16[23,16,128]{2,1,0:T(8,128)(2,1)} %copy-done.12, bf16[23,16,128]{2,1,0:T(8,128)(2,1)} %copy-done.13, bf16[17,16,128]{2,1,0:T(8,128)(2,1)} %copy-done.14, bf16[17,16,128]{2,1,0:T(8,128)(2,1)} %copy-done.15, ...), custom_call_target="tpu_custom_call" | custom-call | tf_op jit(solution)/shard_map/branches/pallas_call | solution.py:256
  111.1 7.4 %all-to-all-start = ((bf16[16,104,128]{2,1,0:T(8,128)(2,1)}), bf16[16,104,128]{2,1,0:T(8,128)(2,1)S(1)}, u32[]{:S(2)}, u32[]{:S(2)}) async-start(bf16[16,104,128]{2,1,0:T(8,128)(2,1)} %branches.1), calls=%async_computation | async-start | bytes 851968 | tf_op jit(solution)/shard_map/all_to_all | solution.py:444
  118.5 0.1 fusion.10
  118.7 0.1 fusion.18
  118.7 1.0 pad_maximum_fusion.2.refs_4_
  119.7 8.3 %all-to-all-done.refs_0_ = bf16[16,104,128]{2,1,0:T(8,128)(2,1)S(1)} async-done(((bf16[16,104,128]{2,1,0:T(8,128)(2,1)}), bf16[16,104,128]{2,1,0:T(8,128)(2,1)S(1)}, u32[]{:S(2)}, u32[]{:S(2)}) %all-to-all-start) | async-done | bytes 426016 | tf_op jit(solution)/shard_map/all_to_all | solution.py:444
  128.1 0.8 copy-done.1
  128.9 7.2 %decode.1 = bf16[16,24,256]{2,1,0:T(8,128)(2,1)} custom-call(bf16[16,104,128]{2,1,0:T(8,128)(2,1)} %copy-done.1, bf16[5,16,16,256]{3,2,1,0:T(8,128)(2,1)} %bitcast.22, f32[1,256]{1,0:T(1,128)} %bitcast.27, bf16[640,192]{1,0:T(8,128)(2,1)} %spread.1.refs_3_, bf16[640,144]{1,0:T(8,128)(2,1)} %pad_maximum_fusion.2.refs_4_, bf16[3,3,304,256]{3,2,1,0:T(8,128)(2,1)} %refs_5_.1, ...), custom_call_target="tpu_custom_call" | custom-call | tf_op jit(solution)/shard_map/decode/pallas_call | solution.py:347
  (67 shorter events, 0.3 us)
Async XLA Ops:
  0.0 55.5 %copy-start = (bf16[16,24,256]{2,1,0:T(8,128)(2,1)S(1)}, bf16[16,24,256]{2,1,0:T(8,128)(2,1)}, u32[]{:S(2)}) copy-start(bf16[16,24,256]{2,1,0:T(8,128)(2,1)} %param.15) | copy-start | bytes 589828
  1.1 6.8 %collective-permute-start.10 = (bf16[6,8,2048]{2,1,0:T(8,128)(2,1)S(1)}, bf16[6,8,2048]{2,1,0:T(8,128)(2,1)S(1)}, u32[]{:S(2)}, u32[]{:S(2)}) collective-permute-start(bf16[6,8,2048]{2,1,0:T(8,128)(2,1)S(1)} %get-tuple-element.21), channel_id=1, source_target_pairs={{0,32},{32,0},{64,96},{96,64},{1,33},{33,1},{65,97},{97,65},{2,34}... | collective-permute-start | bytes 589832 | tf_op jit(solution)/shard_map/ppermute | solution.py:32
  2.8 13.5 %collective-permute-start.11 = (bf16[6,8,2048]{2,1,0:T(8,128)(2,1)S(1)}, bf16[6,8,2048]{2,1,0:T(8,128)(2,1)S(1)}, u32[]{:S(2)}, u32[]{:S(2)}) collective-permute-start(bf16[6,8,2048]{2,1,0:T(8,128)(2,1)S(1)} %get-tuple-element.21), channel_id=1, source_target_pairs={{0,96},{96,0},{32,64},{64,32},{1,97},{97,1},{33,65},{65,33},{2,98}... | collective-permute-start | bytes 589832 | tf_op jit(solution)/shard_map/ppermute | solution.py:32
  4.9 12.1 %collective-permute-start.1 = (bf16[6,8,2048]{2,1,0:T(8,128)(2,1)S(1)}, bf16[6,8,2048]{2,1,0:T(8,128)(2,1)S(1)}, u32[]{:S(2)}, u32[]{:S(2)}) collective-permute-start(bf16[6,8,2048]{2,1,0:T(8,128)(2,1)S(1)} %get-tuple-element.22), channel_id=1, source_target_pairs={{0,24},{24,0},{8,16},{16,8},{1,25},{25,1},{9,17},{17,9},{2,26},{26... | collective-permute-start | bytes 589832 | tf_op jit(solution)/shard_map/ppermute | solution.py:32
  7.7 7.8 %collective-permute-start = (bf16[6,8,2048]{2,1,0:T(8,128)(2,1)S(1)}, bf16[6,8,2048]{2,1,0:T(8,128)(2,1)S(1)}, u32[]{:S(2)}, u32[]{:S(2)}) collective-permute-start(bf16[6,8,2048]{2,1,0:T(8,128)(2,1)S(1)} %get-tuple-element.22), channel_id=1, source_target_pairs={{0,8},{8,0},{16,24},{24,16},{1,9},{9,1},{17,25},{25,17},{2,10},{10... | collective-permute-start | bytes 589832 | tf_op jit(solution)/shard_map/ppermute | solution.py:32
  8.0 29.1 %copy-start.2 = (bf16[12,8,2048]{2,1,0:T(8,128)(2,1)}, bf16[12,8,2048]{2,1,0:T(8,128)(2,1)S(1)}, u32[]{:S(2)}) copy-start(bf16[12,8,2048]{2,1,0:T(8,128)(2,1)S(1)} %pad_maximum_fusion.1.refs_8_) | copy-start | bytes 1179652
  8.0 47.5 %copy-start.18 = (bf16[256,48]{0,1:T(8,128)(2,1)S(1)}, bf16[256,48]{0,1:T(8,128)(2,1)}, u32[]{:S(2)}) copy-start(bf16[256,48]{0,1:T(8,128)(2,1)} %param.22) | copy-start | bytes 73732
  8.0 47.5 %copy-start.20 = (f32[48]{0:T(128)S(1)}, f32[48]{0:T(128)}, u32[]{:S(2)}) copy-start(f32[48]{0:T(128)} %param.23) | copy-start | bytes 580
  8.0 35.1 %collective-permute-start.14 = (bf16[12,8,2048]{2,1,0:T(8,128)(2,1)S(1)}, bf16[12,8,2048]{2,1,0:T(8,128)(2,1)S(1)}, u32[]{:S(2)}, u32[]{:S(2)}) collective-permute-start(bf16[12,8,2048]{2,1,0:T(8,128)(2,1)S(1)} %pad_maximum_fusion.1.refs_8_), channel_id=1, source_target_pairs={{0,8},{8,0},{16,24},{24,16},{1,9},{9,1},{17,25},{25,17},{2,10},{10... | collective-permute-start | bytes 1179656 | tf_op jit(solution)/shard_map/ppermute | solution.py:32
  9.9 35.5 %collective-permute-start.16 = (bf16[12,8,2048]{2,1,0:T(8,128)(2,1)S(1)}, bf16[12,8,2048]{2,1,0:T(8,128)(2,1)S(1)}, u32[]{:S(2)}, u32[]{:S(2)}) collective-permute-start(bf16[12,8,2048]{2,1,0:T(8,128)(2,1)S(1)} %pad_maximum_fusion.1.refs_8_), channel_id=1, source_target_pairs={{0,24},{24,0},{8,16},{16,8},{1,25},{25,1},{9,17},{17,9},{2,26},{26... | collective-permute-start | bytes 1179656 | tf_op jit(solution)/shard_map/ppermute | solution.py:32
  15.5 48.0 %copy-start.3 = (bf16[12,8,2048]{2,1,0:T(8,128)(2,1)}, bf16[12,8,2048]{2,1,0:T(8,128)(2,1)S(1)}, u32[]{:S(2)}) copy-start(bf16[12,8,2048]{2,1,0:T(8,128)(2,1)S(1)} %pad_maximum_fusion.refs_0_) | copy-start | bytes 1179652
  15.5 29.9 %collective-permute-start.4 = (bf16[12,8,2048]{2,1,0:T(8,128)(2,1)S(1)}, bf16[12,8,2048]{2,1,0:T(8,128)(2,1)S(1)}, u32[]{:S(2)}, u32[]{:S(2)}) collective-permute-start(bf16[12,8,2048]{2,1,0:T(8,128)(2,1)S(1)} %pad_maximum_fusion.refs_0_), channel_id=1, source_target_pairs={{0,32},{32,0},{64,96},{96,64},{1,33},{33,1},{65,97},{97,65},{2,34}... | collective-permute-start | bytes 1179656 | tf_op jit(solution)/shard_map/ppermute | solution.py:32
  16.3 29.3 %collective-permute-start.6 = (bf16[12,8,2048]{2,1,0:T(8,128)(2,1)S(1)}, bf16[12,8,2048]{2,1,0:T(8,128)(2,1)S(1)}, u32[]{:S(2)}, u32[]{:S(2)}) collective-permute-start(bf16[12,8,2048]{2,1,0:T(8,128)(2,1)S(1)} %pad_maximum_fusion.refs_0_), channel_id=1, source_target_pairs={{0,96},{96,0},{32,64},{64,32},{1,97},{97,1},{33,65},{65,33},{2,98}... | collective-permute-start | bytes 1179656 | tf_op jit(solution)/shard_map/ppermute | solution.py:32
  17.0 9.6 %collective-permute-start.12 = (bf16[3,8,2048]{2,1,0:T(8,128)(2,1)S(1)}, bf16[3,8,2048]{2,1,0:T(8,128)(2,1)S(1)}, u32[]{:S(2)}, u32[]{:S(2)}) collective-permute-start(bf16[3,8,2048]{2,1,0:T(8,128)(2,1)S(1)} %slice.60), channel_id=1, source_target_pairs={{0,96},{96,0},{32,64},{64,32},{1,97},{97,1},{33,65},{65,33},{2,98}... | collective-permute-start | bytes 294920 | tf_op jit(solution)/shard_map/ppermute | solution.py:32
  26.6 4.6 %collective-permute-start.13 = (bf16[3,8,2048]{2,1,0:T(8,128)(2,1)S(1)}, bf16[3,8,2048]{2,1,0:T(8,128)(2,1)S(1)}, u32[]{:S(2)}, u32[]{:S(2)}) collective-permute-start(bf16[3,8,2048]{2,1,0:T(8,128)(2,1)S(1)} %slice.61), channel_id=1, source_target_pairs={{0,32},{32,0},{64,96},{96,64},{1,33},{33,1},{65,97},{97,65},{2,34}... | collective-permute-start | bytes 294920 | tf_op jit(solution)/shard_map/ppermute | solution.py:32
  31.2 5.8 %collective-permute-start.2 = (bf16[3,8,2048]{2,1,0:T(8,128)(2,1)S(1)}, bf16[3,8,2048]{2,1,0:T(8,128)(2,1)S(1)}, u32[]{:S(2)}, u32[]{:S(2)}) collective-permute-start(bf16[3,8,2048]{2,1,0:T(8,128)(2,1)S(1)} %slice.57), channel_id=1, source_target_pairs={{0,24},{24,0},{8,16},{16,8},{1,25},{25,1},{9,17},{17,9},{2,26},{26... | collective-permute-start | bytes 294920 | tf_op jit(solution)/shard_map/ppermute | solution.py:32
  31.7 31.8 %copy-start.5 = (bf16[12,8,2048]{2,1,0:T(8,128)(2,1)}, bf16[12,8,2048]{2,1,0:T(8,128)(2,1)S(1)}, u32[]{:S(2)}) copy-start(bf16[12,8,2048]{2,1,0:T(8,128)(2,1)S(1)} %constant_dynamic-update-slice_fusion.3.refs_9_) | copy-start | bytes 1179652
  37.1 5.7 %collective-permute-start.3 = (bf16[3,8,2048]{2,1,0:T(8,128)(2,1)S(1)}, bf16[3,8,2048]{2,1,0:T(8,128)(2,1)S(1)}, u32[]{:S(2)}, u32[]{:S(2)}) collective-permute-start(bf16[3,8,2048]{2,1,0:T(8,128)(2,1)S(1)} %slice.58), channel_id=1, source_target_pairs={{0,8},{8,0},{16,24},{24,16},{1,9},{9,1},{17,25},{25,17},{2,10},{10... | collective-permute-start | bytes 294920 | tf_op jit(solution)/shard_map/ppermute | solution.py:32
  42.7 9.1 %collective-permute-start.17 = (bf16[12,8,2048]{2,1,0:T(8,128)(2,1)S(1)}, bf16[12,8,2048]{2,1,0:T(8,128)(2,1)}, u32[]{:S(2)}, u32[]{:S(2)}) collective-permute-start(bf16[12,8,2048]{2,1,0:T(8,128)(2,1)S(1)} %constant_dynamic-update-slice_fusion.3.refs_9_), channel_id=1, source_target_pairs={{0,24},{24,0},{8,16},{16,8},{1,25},{25,1},{9,17},{17,9},{2,26},{26... | collective-permute-start | bytes 1179656 | tf_op jit(solution)/shard_map/ppermute | solution.py:32
  43.1 20.5 %copy-start.4 = (bf16[12,8,2048]{2,1,0:T(8,128)(2,1)}, bf16[12,8,2048]{2,1,0:T(8,128)(2,1)S(1)}, u32[]{:S(2)}) copy-start(bf16[12,8,2048]{2,1,0:T(8,128)(2,1)S(1)} %constant_dynamic-update-slice_fusion.refs_1_) | copy-start | bytes 1179652
  43.1 20.5 %copy-start.6 = (bf16[12,8,2048]{2,1,0:T(8,128)(2,1)}, bf16[12,8,2048]{2,1,0:T(8,128)(2,1)S(1)}, u32[]{:S(2)}) copy-start(bf16[12,8,2048]{2,1,0:T(8,128)(2,1)S(1)} %collective-permute-done.14.refs_10_) | copy-start | bytes 1179652
  43.1 10.7 %collective-permute-start.7 = (bf16[12,8,2048]{2,1,0:T(8,128)(2,1)S(1)}, bf16[12,8,2048]{2,1,0:T(8,128)(2,1)}, u32[]{:S(2)}, u32[]{:S(2)}) collective-permute-start(bf16[12,8,2048]{2,1,0:T(8,128)(2,1)S(1)} %constant_dynamic-update-slice_fusion.refs_1_), channel_id=1, source_target_pairs={{0,96},{96,0},{32,64},{64,32},{1,97},{97,1},{33,65},{65,33},{2,98}... | collective-permute-start | bytes 1179656 | tf_op jit(solution)/shard_map/ppermute | solution.py:32
  45.4 18.1 %copy-start.8 = (bf16[12,8,2048]{2,1,0:T(8,128)(2,1)}, bf16[12,8,2048]{2,1,0:T(8,128)(2,1)S(1)}, u32[]{:S(2)}) copy-start(bf16[12,8,2048]{2,1,0:T(8,128)(2,1)S(1)} %collective-permute-done.4.refs_2_) | copy-start | bytes 1179652
  45.4 9.3 %collective-permute-start.15 = (bf16[12,8,2048]{2,1,0:T(8,128)(2,1)S(1)}, bf16[12,8,2048]{2,1,0:T(8,128)(2,1)S(1)}, u32[]{:S(2)}, u32[]{:S(2)}) collective-permute-start(bf16[12,8,2048]{2,1,0:T(8,128)(2,1)S(1)} %constant_dynamic-update-slice_fusion.3.refs_9_), channel_id=1, source_target_pairs={{0,8},{8,0},{16,24},{24,16},{1,9},{9,1},{17,25},{25,17},{2,10},{10... | collective-permute-start | bytes 1179656 | tf_op jit(solution)/shard_map/ppermute | solution.py:32
  45.4 18.1 %copy-start.7 = (bf16[12,8,2048]{2,1,0:T(8,128)(2,1)}, bf16[12,8,2048]{2,1,0:T(8,128)(2,1)S(1)}, u32[]{:S(2)}) copy-start(bf16[12,8,2048]{2,1,0:T(8,128)(2,1)S(1)} %collective-permute-done.16.refs_12_) | copy-start | bytes 1179652
  45.5 11.9 %collective-permute-start.5 = (bf16[12,8,2048]{2,1,0:T(8,128)(2,1)S(1)}, bf16[12,8,2048]{2,1,0:T(8,128)(2,1)S(1)}, u32[]{:S(2)}, u32[]{:S(2)}) collective-permute-start(bf16[12,8,2048]{2,1,0:T(8,128)(2,1)S(1)} %constant_dynamic-update-slice_fusion.refs_1_), channel_id=1, source_target_pairs={{0,32},{32,0},{64,96},{96,64},{1,33},{33,1},{65,97},{97,65},{2,34}... | collective-permute-start | bytes 1179656 | tf_op jit(solution)/shard_map/ppermute | solution.py:32
  45.6 18.0 %copy-start.9 = (bf16[12,8,2048]{2,1,0:T(8,128)(2,1)}, bf16[12,8,2048]{2,1,0:T(8,128)(2,1)S(1)}, u32[]{:S(2)}) copy-start(bf16[12,8,2048]{2,1,0:T(8,128)(2,1)S(1)} %collective-permute-done.6.refs_4_) | copy-start | bytes 1179652
  45.6 11.7 %collective-permute-start.18 = (bf16[12,8,2048]{2,1,0:T(8,128)(2,1)S(1)}, bf16[12,8,2048]{2,1,0:T(8,128)(2,1)}, u32[]{:S(2)}, u32[]{:S(2)}) collective-permute-start(bf16[12,8,2048]{2,1,0:T(8,128)(2,1)S(1)} %collective-permute-done.14.refs_10_), channel_id=1, source_target_pairs={{0,24},{24,0},{8,16},{16,8},{1,25},{25,1},{9,17},{17,9},{2,26},{26... | collective-permute-start | bytes 1179656 | tf_op jit(solution)/shard_map/ppermute | solution.py:32
  51.8 9.1 %collective-permute-start.8 = (bf16[12,8,2048]{2,1,0:T(8,128)(2,1)S(1)}, bf16[12,8,2048]{2,1,0:T(8,128)(2,1)}, u32[]{:S(2)}, u32[]{:S(2)}) collective-permute-start(bf16[12,8,2048]{2,1,0:T(8,128)(2,1)S(1)} %collective-permute-done.4.refs_2_), channel_id=1, source_target_pairs={{0,96},{96,0},{32,64},{64,32},{1,97},{97,1},{33,65},{65,33},{2,98}... | collective-permute-start | bytes 1179656 | tf_op jit(solution)/shard_map/ppermute | solution.py:32
  53.8 8.1 %collective-permute-start.19 = (bf16[12,8,2048]{2,1,0:T(8,128)(2,1)}, bf16[12,8,2048]{2,1,0:T(8,128)(2,1)}, u32[]{:S(2)}, u32[]{:S(2)}) collective-permute-start(bf16[12,8,2048]{2,1,0:T(8,128)(2,1)} %collective-permute-done.17.refs_13_), channel_id=1, source_target_pairs={{0,8},{8,0},{16,24},{24,16},{1,9},{9,1},{17,25},{25,17},{2,10},{10... | collective-permute-start | bytes 1179656 | tf_op jit(solution)/shard_map/ppermute | solution.py:32
  54.7 0.7 copy-start.10
  55.5 8.1 %collective-permute-start.9 = (bf16[12,8,2048]{2,1,0:T(8,128)(2,1)}, bf16[12,8,2048]{2,1,0:T(8,128)(2,1)}, u32[]{:S(2)}, u32[]{:S(2)}) collective-permute-start(bf16[12,8,2048]{2,1,0:T(8,128)(2,1)} %collective-permute-done.7.refs_5_), channel_id=1, source_target_pairs={{0,32},{32,0},{64,96},{96,64},{1,33},{33,1},{65,97},{97,65},{2,34}... | collective-permute-start | bytes 1179656 | tf_op jit(solution)/shard_map/ppermute | solution.py:32
  57.3 6.3 %copy-start.11 = (bf16[12,8,2048]{2,1,0:T(8,128)(2,1)}, bf16[12,8,2048]{2,1,0:T(8,128)(2,1)S(1)}, u32[]{:S(2)}) copy-start(bf16[12,8,2048]{2,1,0:T(8,128)(2,1)S(1)} %collective-permute-done.5.refs_3_) | copy-start | bytes 1179652
  73.0 20.0 %collective-permute-start.24 = (bf16[15,16,128]{2,1,0:T(8,128)(2,1)}, bf16[15,16,128]{2,1,0:T(8,128)(2,1)S(1)}, u32[]{:S(2)}, u32[]{:S(2)}) collective-permute-start(bf16[15,16,128]{2,1,0:T(8,128)(2,1)} %get-tuple-element.18), channel_id=1, source_target_pairs={{0,3},{1,4},{2,5},{3,6},{4,7},{5,0},{6,1},{7,2},{8,11},{9,12},{10,... | collective-permute-start | bytes 184328 | tf_op jit(solution)/shard_map/ppermute | solution.py:21
  78.9 14.0 %collective-permute-start.26 = (bf16[5,16,128]{2,1,0:T(8,128)(2,1)}, bf16[5,16,128]{2,1,0:T(8,128)(2,1)S(1)}, u32[]{:S(2)}, u32[]{:S(2)}) collective-permute-start(bf16[5,16,128]{2,1,0:T(8,128)(2,1)} %get-tuple-element.20.refs_9_), channel_id=1, source_target_pairs={{0,4},{1,5},{2,6},{3,7},{4,0},{5,1},{6,2},{7,3},{8,12},{9,13},{10,... | collective-permute-start | bytes 61448 | tf_op jit(solution)/shard_map/ppermute | solution.py:21
  79.5 7.0 %collective-permute-start.27 = (bf16[16,2,48]{2,1,0:T(2,128)(2,1)S(1)}, bf16[16,2,48]{2,1,0:T(2,128)(2,1)S(1)}, u32[]{:S(2)}, u32[]{:S(2)}) collective-permute-start(bf16[16,2,48]{2,1,0:T(2,128)(2,1)S(1)} %get-tuple-element.27), channel_id=1, source_target_pairs={{0,1},{1,2},{2,3},{3,4},{4,5},{5,6},{6,7},{8,9},{9,10},{10,11},{11... | collective-permute-start | bytes 9224 | tf_op jit(solution)/shard_map/ppermute | solution.py:27
  82.4 5.6 %collective-permute-start.28 = (bf16[16,2,48]{2,1,0:T(2,128)(2,1)S(1)}, bf16[16,2,48]{2,1,0:T(2,128)(2,1)S(1)}, u32[]{:S(2)}, u32[]{:S(2)}) collective-permute-start(bf16[16,2,48]{2,1,0:T(2,128)(2,1)S(1)} %get-tuple-element.28), channel_id=1, source_target_pairs={{1,0},{2,1},{3,2},{4,3},{5,4},{6,5},{7,6},{9,8},{10,9},{11,10},{12... | collective-permute-start | bytes 9224 | tf_op jit(solution)/shard_map/ppermute | solution.py:27
  85.5 22.4 %collective-permute-start.20 = (bf16[23,16,128]{2,1,0:T(8,128)(2,1)}, bf16[23,16,128]{2,1,0:T(8,128)(2,1)S(1)}, u32[]{:S(2)}, u32[]{:S(2)}) collective-permute-start(bf16[23,16,128]{2,1,0:T(8,128)(2,1)} %get-tuple-element.14.refs_7_), channel_id=1, source_target_pairs={{0,1},{1,2},{2,3},{3,4},{4,5},{5,6},{6,7},{7,0},{8,9},{9,10},{10,1... | collective-permute-start | bytes 282632 | tf_op jit(solution)/shard_map/ppermute | solution.py:21
  86.4 21.5 %collective-permute-start.21 = (bf16[23,16,128]{2,1,0:T(8,128)(2,1)}, bf16[23,16,128]{2,1,0:T(8,128)(2,1)S(1)}, u32[]{:S(2)}, u32[]{:S(2)}) collective-permute-start(bf16[23,16,128]{2,1,0:T(8,128)(2,1)} %get-tuple-element.15.refs_8_), channel_id=1, source_target_pairs={{0,7},{1,0},{2,1},{3,2},{4,3},{5,4},{6,5},{7,6},{8,15},{9,8},{10,9... | collective-permute-start | bytes 282632 | tf_op jit(solution)/shard_map/ppermute | solution.py:21
  88.0 17.2 %collective-permute-start.22 = (bf16[17,16,128]{2,1,0:T(8,128)(2,1)}, bf16[17,16,128]{2,1,0:T(8,128)(2,1)S(1)}, u32[]{:S(2)}, u32[]{:S(2)}) collective-permute-start(bf16[17,16,128]{2,1,0:T(8,128)(2,1)} %get-tuple-element.16), channel_id=1, source_target_pairs={{0,2},{1,3},{2,4},{3,5},{4,6},{5,7},{6,0},{7,1},{8,10},{9,11},{10,... | collective-permute-start | bytes 208904 | tf_op jit(solution)/shard_map/ppermute | solution.py:21
  92.9 15.0 %copy-start.19 = (bf16[5,16,128]{2,1,0:T(8,128)(2,1)}, bf16[5,16,128]{2,1,0:T(8,128)(2,1)S(1)}, u32[]{:S(2)}) copy-start(bf16[5,16,128]{2,1,0:T(8,128)(2,1)S(1)} %collective-permute-done.26.refs_6_) | copy-start | bytes 61444
  92.9 15.0 %collective-permute-start.23 = (bf16[17,16,128]{2,1,0:T(8,128)(2,1)}, bf16[17,16,128]{2,1,0:T(8,128)(2,1)S(1)}, u32[]{:S(2)}, u32[]{:S(2)}) collective-permute-start(bf16[17,16,128]{2,1,0:T(8,128)(2,1)} %get-tuple-element.17), channel_id=1, source_target_pairs={{0,6},{1,7},{2,0},{3,1},{4,2},{5,3},{6,4},{7,5},{8,14},{9,15},{10,... | collective-permute-start | bytes 208904 | tf_op jit(solution)/shard_map/ppermute | solution.py:21
  93.0 15.0 %copy-start.16 = (bf16[15,16,128]{2,1,0:T(8,128)(2,1)}, bf16[15,16,128]{2,1,0:T(8,128)(2,1)S(1)}, u32[]{:S(2)}) copy-start(bf16[15,16,128]{2,1,0:T(8,128)(2,1)S(1)} %collective-permute-done.24.refs_4_) | copy-start | bytes 184324
  93.0 8.9 %collective-permute-start.25 = (bf16[15,16,128]{2,1,0:T(8,128)(2,1)}, bf16[15,16,128]{2,1,0:T(8,128)(2,1)S(1)}, u32[]{:S(2)}, u32[]{:S(2)}) collective-permute-start(bf16[15,16,128]{2,1,0:T(8,128)(2,1)} %get-tuple-element.19), channel_id=1, source_target_pairs={{0,5},{1,6},{2,7},{3,0},{4,1},{5,2},{6,3},{7,4},{8,13},{9,14},{10,... | collective-permute-start | bytes 184328 | tf_op jit(solution)/shard_map/ppermute | solution.py:21
  101.9 6.1 %copy-start.17 = (bf16[15,16,128]{2,1,0:T(8,128)(2,1)}, bf16[15,16,128]{2,1,0:T(8,128)(2,1)S(1)}, u32[]{:S(2)}) copy-start(bf16[15,16,128]{2,1,0:T(8,128)(2,1)S(1)} %collective-permute-done.25.refs_5_) | copy-start | bytes 184324
  101.9 16.6 %collective-permute-start.29 = (bf16[2,28,48]{2,1,0:T(8,128)(2,1)S(1)}, bf16[2,28,48]{2,1,0:T(8,128)(2,1)S(1)}, u32[]{:S(2)}, u32[]{:S(2)}) collective-permute-start(bf16[2,28,48]{2,1,0:T(8,128)(2,1)S(1)} %get-tuple-element.25), channel_id=1, source_target_pairs={{0,8},{8,16},{16,24},{24,32},{32,40},{40,48},{48,56},{56,64},{64,7... | collective-permute-start | bytes 16136 | tf_op jit(solution)/shard_map/ppermute | solution.py:27
  105.3 2.7 %copy-start.14 = (bf16[17,16,128]{2,1,0:T(8,128)(2,1)}, bf16[17,16,128]{2,1,0:T(8,128)(2,1)S(1)}, u32[]{:S(2)}) copy-start(bf16[17,16,128]{2,1,0:T(8,128)(2,1)S(1)} %collective-permute-done.22.refs_2_) | copy-start | bytes 208900
  105.3 13.2 %collective-permute-start.30 = (bf16[2,28,48]{2,1,0:T(8,128)(2,1)S(1)}, bf16[2,28,48]{2,1,0:T(8,128)(2,1)S(1)}, u32[]{:S(2)}, u32[]{:S(2)}) collective-permute-start(bf16[2,28,48]{2,1,0:T(8,128)(2,1)S(1)} %get-tuple-element.26), channel_id=1, source_target_pairs={{8,0},{16,8},{24,16},{32,24},{40,32},{48,40},{56,48},{64,56},{72,6... | collective-permute-start | bytes 16136 | tf_op jit(solution)/shard_map/ppermute | solution.py:27
  107.9 0.6 copy-start.15
  107.9 0.7 copy-start.12
  108.0 0.7 copy-start.13
  111.1 17.0 %all-to-all-start = ((bf16[16,104,128]{2,1,0:T(8,128)(2,1)}), bf16[16,104,128]{2,1,0:T(8,128)(2,1)S(1)}, u32[]{:S(2)}, u32[]{:S(2)}) async-start(bf16[16,104,128]{2,1,0:T(8,128)(2,1)} %branches.1), calls=%async_computation | async-start | bytes 851968 | tf_op jit(solution)/shard_map/all_to_all | solution.py:444
  128.1 0.8 copy-start.1

commit v3 on v2

--- a/solution.py
+++ b/solution.py
@@ -70,6 +70,7 @@
     for piece in pieces
 ]
 SIZES = (23, 17, 15)
+SLOT = 136
 
 
 def products_kernel(*refs):
@@ -191,7 +192,8 @@
 
 def branches_kernel(centre, *refs):
     sides = refs[0:6]
-    opposite, own_left, own_right, own_terms, bias, out, rows, slots = refs[6:14]
+    opposite, own_left, own_right, own_terms, bias, top, bottom = refs[6:13]
+    out, rows, slots = refs[13:16]
     strip = lax.axis_index("col")
 
     diagonal = lax.broadcasted_iota(jnp.int32, (16, 16), 0) == lax.broadcasted_iota(
@@ -244,28 +246,31 @@
     wide = jnp.concatenate(
         [jnp.broadcast_to(branch, (16, 128)), jnp.zeros((112, 128), F32)], axis=0
     ).T
+    row_index = lax.axis_index("row_0") * 4 + lax.axis_index("row_1")
+    above, below = top[...].astype(F32), bottom[...].astype(F32)
     for slot in range(16):
         for c8 in range(8):
             slots[slot, c8 * 12 : c8 * 12 + 12] = rows[c8, 8 * slot + 6 : 8 * slot + 18]
         slots[slot, 96:104] = wide[0:8]
+        slots[slot, 104:136] = jnp.where(slot == row_index + 1, below, above)
         out[slot] = slots[slot].astype(BF)
 
 
-def branches(centre, moved, opposite, own_left, own_right, own_terms, bias):
+def branches(centre, moved, opposite, own_left, own_right, own_terms, bias, top, bottom):
     vmem = pl.BlockSpec(memory_space=pltpu.VMEM)
     return pl.pallas_call(
         branches_kernel,
-        out_shape=jax.ShapeDtypeStruct((16, 104, 128), BF),
-        in_specs=[vmem] * 12,
-        scratch_shapes=[pltpu.VMEM((8, 144, 128), F32), pltpu.VMEM((16, 104, 128), F32)],
+        out_shape=jax.ShapeDtypeStruct((16, SLOT, 128), BF),
+        in_specs=[vmem] * 14,
+        scratch_shapes=[pltpu.VMEM((8, 144, 128), F32), pltpu.VMEM((16, SLOT, 128), F32)],
         compiler_params=pltpu.CompilerParams(vmem_limit_bytes=VMEM_BYTES),
         name="branches",
-    )(centre, *moved, opposite, own_left, own_right, own_terms, bias)
+    )(centre, *moved, opposite, own_left, own_right, own_terms, bias, top, bottom)
 
 
 def coarse_tile(received, weight, pool_weight, bias):
     lane = lax.broadcasted_iota(jnp.int32, (104, 128), 1)
-    blocks = [received[source].astype(F32) for source in range(16)]
+    blocks = [received[source, 0:104].astype(F32) for source in range(16)]
     turned = [pltpu.roll(block, 64, 1) for block in blocks]
     halves = []
     for half in range(2):
@@ -288,8 +293,8 @@
 
 
 def decode_kernel(*refs):
-    received, proj, bias, spread, low, w1_hbm, b1, w2_hbm, b2 = refs[0:9]
-    out, fine, fine_cols, mid, mid_cols, w1, w2, weight, last, sems = refs[9:]
+    received, proj, bias, spread, low_own, w1_hbm, b1, w2_hbm, b2 = refs[0:9]
+    out, fine, fine_cols, mid, mid_cols, w1, w2, weight, last, low, shift, sems = refs[9:]
     loads = [
         pltpu.make_async_copy(w1_hbm, w1, sems.at[0]),
         pltpu.make_async_copy(w2_hbm, w2, sems.at[1]),
@@ -301,6 +306,23 @@
     small_loads.append(pltpu.make_async_copy(proj.at[4], last, sems.at[6]))
     for load in small_loads + loads:
         load.start()
+    row_index = lax.axis_index("row_0") * 4 + lax.axis_index("row_1")
+    low[...] = low_own[...]
+    shift[32:40] = jnp.zeros((8, 128), F32)
+    lane = lax.broadcasted_iota(jnp.int32, (32, 128), 1)
+    for side in range(2):
+        source = row_index - 1 + 2 * side
+        inside = (source >= 0) & (source < 16)
+        block = received[jnp.clip(source, 0, 15), 104:136].astype(F32)
+        for row in range(2):
+            values = block if row == 0 else pltpu.roll(block, 64, 1)
+            shift[0:32] = jnp.where(inside & (lane < 48), values, 0.0)
+            moved = pltpu.roll(shift[2:34], 96, 1)
+            front = shift[0:32] + pltpu.roll(shift[1:33], 48, 1)
+            front = front + jnp.where(lane >= 96, moved, 0.0)
+            filled = jnp.concatenate([front, moved[:, 0:16]], axis=1)
+            at = (18 * side + row) * 32
+            low[at : at + 32] = filled.astype(BF)
     for load in small_loads:
         load.wait()
     coarse = coarse_tile(
@@ -321,7 +343,7 @@
         small = jnp.concatenate([w1[row_tap, tap, 256:304] for tap in range(3)], axis=0)
         acc = acc + jnp.dot(low[rows], small, preferred_element_type=F32)
     at = lax.broadcasted_iota(jnp.int32, (576, 256), 0)
-    y = 16 * (lax.axis_index("row_0") * 4 + lax.axis_index("row_1")) - 1 + (at >> 5)
+    y = 16 * row_index - 1 + (at >> 5)
     x = 24 * lax.axis_index("col") - 1 + (at & 31)
     inside = (y >= 0) & (y < 2 * MAP_ROWS) & (x >= 0) & (x < 2 * MAP_COLS)
     mid[0:576] = jnp.where(inside, jnp.maximum(acc + b1[...], 0.0), 0.0)
@@ -357,6 +379,8 @@
             pltpu.VMEM(w2.shape, BF),
             pltpu.VMEM((16, 4, 16, 256), BF),
             pltpu.VMEM((16, 16, 256), BF),
+            pltpu.VMEM((640, 144), BF),
+            pltpu.VMEM((40, 128), F32),
             pltpu.SemaphoreType.DMA((7,)),
         ],
         compiler_params=pltpu.CompilerParams(vmem_limit_bytes=VMEM_BYTES),
@@ -399,10 +423,14 @@
     return reduced
 
 
-def low_columns(above, wide, below):
-    full = jnp.concatenate([above, wide, below], axis=0)
-    full = jnp.pad(full, ((0, 1), (0, 4), (0, 0))).reshape(672, -1)
+def low_columns(wide):
+    full = jnp.pad(wide, ((2, 3), (0, 4), (0, 0))).reshape(672, -1)
     return jnp.concatenate([full[tap : tap + 640] for tap in range(3)], axis=1)
+
+
+def border(rows):
+    padded = jnp.pad(rows, ((0, 0), (0, 4), (0, 16)))
+    return jnp.concatenate([padded[0], padded[1]], axis=1)
 
 
 def on_device(
@@ -427,9 +455,7 @@
     before = next_to(reduced[:, 22:24], "col", 1)
     after = next_to(reduced[:, 0:2], "col", -1)
     wide = jnp.concatenate([before, reduced, after], axis=1)
-    above = next_to(wide[14:16], ROW, 1)
-    below = next_to(wide[0:2], ROW, -1)
-    low = low_columns(above, wide, below)
+    low, top, bottom = low_columns(wide), border(wide[0:2]), border(wide[14:16])
     pieces = gather_strip(tile[:6], "row_1", "row_0")
     pieces += gather_strip(tile[6:], "row_0", "row_1")
     spread = spread_matrix()
@@ -440,7 +466,9 @@
         moved.append(around(sides[2 * rate], "col", rate + 1))
         moved.append(around(sides[2 * rate + 1], "col", -rate - 1))
     across = around(opposite, "col", 4)
-    mine = branches(centre, moved, across, sides[0], sides[1], opposite, aspp_bias)
+    mine = branches(
+        centre, moved, across, sides[0], sides[1], opposite, aspp_bias, top, bottom
+    )
     received = lax.all_to_all(mine, ROW, split_axis=0, concat_axis=0, tiled=True)
     return decode(
         received,

time: 137 us -> 117 us (0.85)
  starting transfers between devices: 56.5 us -> 45.2 us
  waiting for transfers between devices: 53.8 us -> 43.2 us
    ppermute x20, waiting for transfers between devices: 39.4 us -> 25.7 us  [swap(): lax.ppermute(value, axis, [way for a, b in pairs for way in ((a, b), (b,...]
    ppermute x4 -> x2, starting transfers between devices: 10.7 us -> 5.84 us  [next_to(): return lax.ppermute(value, axis, pairs)]
    ppermute x7, starting transfers between devices: 16.8 us -> 12.7 us  [around(): lax.ppermute(value, axis, [(i, (i + by) % devices) for i in range(devices)])]
    ppermute x7, waiting for transfers between devices: 5.63 us -> 9.65 us  [around(): lax.ppermute(value, axis, [(i, (i + by) % devices) for i in range(devices)])]
    all_to_all x1, starting transfers between devices: 7.44 us -> 3.77 us  [on_device(): lax.all_to_all(mine, ROW, split_axis=0, concat_axis=0, tiled=True)]
  transfers between devices with their start and end apart: 32 -> 30, of which waited for: 15 -> 16; matrix products, arithmetic and copies ran while one was open for 1% -> 3% of each run, Pallas kernels for 3% -> 1%
where the time goes in v3:
time: 117 us; the launch traced here: 116 us
  starting transfers between devices  45.2 us (39%)
  waiting for transfers between devices  43.2 us (37%)
  Pallas kernels  20.4 us (17%)
  local copies, waits for them, and re-layouts  3.68 us (3%)
  other arithmetic  2.48 us (2%)
    ppermute x20, waiting for transfers between devices, swap(): lax.ppermute(value, axis, [way for a, b in pairs for way in ((a, b), (b,...  25.7 us
    ppermute x20, starting transfers between devices, swap(): lax.ppermute(value, axis, [way for a, b in pairs for way in ((a, b), (b,...  22.9 us
    ppermute x7, starting transfers between devices, around(): lax.ppermute(value, axis, [(i, (i + by) % devices) for i in range(devices)])  12.7 us
    ppermute x7, waiting for transfers between devices, around(): lax.ppermute(value, axis, [(i, (i + by) % devices) for i in range(devices)])  9.65 us
    pallas_call x1, Pallas kernels, products(): pl.pallas_call(products_kernel, out_shape=[jax.ShapeDtypeStruct((12, 64,...  9.33 us
    all_to_all x1, waiting for transfers between devices, on_device(): lax.all_to_all(mine, ROW, split_axis=0, concat_axis=0, tiled=True)  7.83 us
    pallas_call x1, Pallas kernels, decode(): pl.pallas_call(decode_kernel, out_shape=jax.ShapeDtypeStruct((16, 24, 256...  7.24 us
    ppermute x2, starting transfers between devices, next_to(): return lax.ppermute(value, axis, pairs)  5.84 us
  transfers between devices with their start and end apart: 30, of which 16 were waited for; matrix products, arithmetic and copies ran while one was open for 3% of the time, Pallas kernels for 1%

profile of v3, /device:TPU:32, one launch (start us, length us, event | category | flops | bytes accessed | tf_op | source)
XLA Modules:
  0.0 116.4 jit_solution(5438026371956969731)
XLA Ops:
  0.0 1.1 fusion.6
  1.1 3.1 %collective-permute-start.11 = (bf16[6,8,2048]{2,1,0:T(8,128)(2,1)S(1)}, bf16[6,8,2048]{2,1,0:T(8,128)(2,1)S(1)}, u32[]{:S(2)}, u32[]{:S(2)}) collective-permute-start(bf16[6,8,2048]{2,1,0:T(8,128)(2,1)S(1)} %get-tuple-element.21), channel_id=1, source_target_pairs={{0,96},{96,0},{32,64},{64,32},{1,97},{97,1},{33,65},{65,33},{2,98}... | collective-permute-start | bytes 589832 | tf_op jit(solution)/shard_map/ppermute | solution.py:32
  4.2 0.1 collective-permute-start.10
  4.3 2.8 %collective-permute-start.1 = (bf16[6,8,2048]{2,1,0:T(8,128)(2,1)S(1)}, bf16[6,8,2048]{2,1,0:T(8,128)(2,1)S(1)}, u32[]{:S(2)}, u32[]{:S(2)}) collective-permute-start(bf16[6,8,2048]{2,1,0:T(8,128)(2,1)S(1)} %get-tuple-element.22), channel_id=1, source_target_pairs={{0,24},{24,0},{8,16},{16,8},{1,25},{25,1},{9,17},{17,9},{2,26},{26... | collective-permute-start | bytes 589832 | tf_op jit(solution)/shard_map/ppermute | solution.py:32
  7.1 0.2 collective-permute-start
  7.3 0.9 fusion.1
  8.3 0.1 copy.15
  8.4 3.8 %collective-permute-start.27 = (bf16[16,2,48]{2,1,0:T(2,128)(2,1)S(1)}, bf16[16,2,48]{2,1,0:T(2,128)(2,1)S(1)}, u32[]{:S(2)}, u32[]{:S(2)}) collective-permute-start(bf16[16,2,48]{2,1,0:T(2,128)(2,1)S(1)} %get-tuple-element.27), channel_id=1, source_target_pairs={{0,1},{1,2},{2,3},{3,4},{4,5},{5,6},{6,7},{8,9},{9,10},{10,11},{11... | collective-permute-start | bytes 9224 | tf_op jit(solution)/shard_map/ppermute | solution.py:27
  12.2 0.0 collective-permute-done.10
  12.2 2.0 %collective-permute-start.28 = (bf16[16,2,48]{2,1,0:T(2,128)(2,1)S(1)}, bf16[16,2,48]{2,1,0:T(2,128)(2,1)S(1)}, u32[]{:S(2)}, u32[]{:S(2)}) collective-permute-start(bf16[16,2,48]{2,1,0:T(2,128)(2,1)S(1)} %get-tuple-element.28), channel_id=1, source_target_pairs={{1,0},{2,1},{3,2},{4,3},{5,4},{6,5},{7,6},{9,8},{10,9},{11,10},{12... | collective-permute-start | bytes 9224 | tf_op jit(solution)/shard_map/ppermute | solution.py:27
  14.3 1.1 collective-permute-start.12
  15.5 0.9 collective-permute-start.13
  16.5 1.2 %collective-permute-start.2 = (bf16[3,8,2048]{2,1,0:T(8,128)(2,1)S(1)}, bf16[3,8,2048]{2,1,0:T(8,128)(2,1)S(1)}, u32[]{:S(2)}, u32[]{:S(2)}) collective-permute-start(bf16[3,8,2048]{2,1,0:T(8,128)(2,1)S(1)} %slice.73), channel_id=1, source_target_pairs={{0,24},{24,0},{8,16},{16,8},{1,25},{25,1},{9,17},{17,9},{2,26},{26... | collective-permute-start | bytes 294920 | tf_op jit(solution)/shard_map/ppermute | solution.py:32
  17.8 2.4 %collective-permute-done.12 = bf16[3,8,2048]{2,1,0:T(8,128)(2,1)S(1)} collective-permute-done((bf16[3,8,2048]{2,1,0:T(8,128)(2,1)S(1)}, bf16[3,8,2048]{2,1,0:T(8,128)(2,1)S(1)}, u32[]{:S(2)}, u32[]{:S(2)}) %collective-permute-start.12) | collective-permute-done | bytes 98336 | tf_op jit(solution)/shard_map/ppermute | solution.py:32
  20.2 1.8 %collective-permute-start.3 = (bf16[3,8,2048]{2,1,0:T(8,128)(2,1)S(1)}, bf16[3,8,2048]{2,1,0:T(8,128)(2,1)S(1)}, u32[]{:S(2)}, u32[]{:S(2)}) collective-permute-start(bf16[3,8,2048]{2,1,0:T(8,128)(2,1)S(1)} %slice.74), channel_id=1, source_target_pairs={{0,8},{8,0},{16,24},{24,16},{1,9},{9,1},{17,25},{25,17},{2,10},{10... | collective-permute-start | bytes 294920 | tf_op jit(solution)/shard_map/ppermute | solution.py:32
  22.0 0.3 collective-permute-start.14
  22.4 0.1 collective-permute-done.2
  22.5 1.2 %collective-permute-start.4 = (bf16[12,8,2048]{2,1,0:T(8,128)(2,1)S(1)}, bf16[12,8,2048]{2,1,0:T(8,128)(2,1)S(1)}, u32[]{:S(2)}, u32[]{:S(2)}) collective-permute-start(bf16[12,8,2048]{2,1,0:T(8,128)(2,1)S(1)} %pad_maximum_fusion.refs_0_), channel_id=1, source_target_pairs={{0,32},{32,0},{64,96},{96,64},{1,33},{33,1},{65,97},{97,65},{2,34}... | collective-permute-start | bytes 1179656 | tf_op jit(solution)/shard_map/ppermute | solution.py:32
  23.6 2.2 %collective-permute-done.3 = bf16[3,8,2048]{2,1,0:T(8,128)(2,1)S(1)} collective-permute-done((bf16[3,8,2048]{2,1,0:T(8,128)(2,1)S(1)}, bf16[3,8,2048]{2,1,0:T(8,128)(2,1)S(1)}, u32[]{:S(2)}, u32[]{:S(2)}) %collective-permute-start.3) | collective-permute-done | bytes 98336 | tf_op jit(solution)/shard_map/ppermute | solution.py:32
  25.9 1.1 collective-permute-start.16
  27.0 1.3 %collective-permute-start.6 = (bf16[12,8,2048]{2,1,0:T(8,128)(2,1)S(1)}, bf16[12,8,2048]{2,1,0:T(8,128)(2,1)S(1)}, u32[]{:S(2)}, u32[]{:S(2)}) collective-permute-start(bf16[12,8,2048]{2,1,0:T(8,128)(2,1)S(1)} %pad_maximum_fusion.refs_0_), channel_id=1, source_target_pairs={{0,96},{96,0},{32,64},{64,32},{1,97},{97,1},{33,65},{65,33},{2,98}... | collective-permute-start | bytes 1179656 | tf_op jit(solution)/shard_map/ppermute | solution.py:32
  28.4 1.9 %collective-permute-start.17 = (bf16[12,8,2048]{2,1,0:T(8,128)(2,1)S(1)}, bf16[12,8,2048]{2,1,0:T(8,128)(2,1)S(1)}, u32[]{:S(2)}, u32[]{:S(2)}) collective-permute-start(bf16[12,8,2048]{2,1,0:T(8,128)(2,1)S(1)} %constant_dynamic-update-slice_fusion.3.refs_9_), channel_id=1, source_target_pairs={{0,24},{24,0},{8,16},{16,8},{1,25},{25,1},{9,17},{17,9},{2,26},{26... | collective-permute-start | bytes 1179656 | tf_op jit(solution)/shard_map/ppermute | solution.py:32
  30.3 1.0 collective-permute-done.14.refs_10_
  31.2 1.2 %collective-permute-start.7 = (bf16[12,8,2048]{2,1,0:T(8,128)(2,1)S(1)}, bf16[12,8,2048]{2,1,0:T(8,128)(2,1)S(1)}, u32[]{:S(2)}, u32[]{:S(2)}) collective-permute-start(bf16[12,8,2048]{2,1,0:T(8,128)(2,1)S(1)} %constant_dynamic-update-slice_fusion.refs_1_), channel_id=1, source_target_pairs={{0,96},{96,0},{32,64},{64,32},{1,97},{97,1},{33,65},{65,33},{2,98}... | collective-permute-start | bytes 1179656 | tf_op jit(solution)/shard_map/ppermute | solution.py:32
  32.5 0.9 collective-permute-start.15
  33.4 5.7 %collective-permute-done.16.refs_12_ = bf16[12,8,2048]{2,1,0:T(8,128)(2,1)S(1)} collective-permute-done((bf16[12,8,2048]{2,1,0:T(8,128)(2,1)S(1)}, bf16[12,8,2048]{2,1,0:T(8,128)(2,1)S(1)}, u32[]{:S(2)}, u32[]{:S(2)}) %collective-permute-start.16) | collective-permute-done | bytes 393248 | tf_op jit(solution)/shard_map/ppermute | solution.py:32
  39.1 0.7 collective-permute-start.5
  39.8 0.4 collective-permute-done.6.refs_4_
  40.1 0.8 collective-permute-start.18
  40.9 5.0 %collective-permute-done.17.refs_13_ = bf16[12,8,2048]{2,1,0:T(8,128)(2,1)S(1)} collective-permute-done((bf16[12,8,2048]{2,1,0:T(8,128)(2,1)S(1)}, bf16[12,8,2048]{2,1,0:T(8,128)(2,1)S(1)}, u32[]{:S(2)}, u32[]{:S(2)}) %collective-permute-start.17) | collective-permute-done | bytes 393248 | tf_op jit(solution)/shard_map/ppermute | solution.py:32
  45.9 1.4 %collective-permute-start.8 = (bf16[12,8,2048]{2,1,0:T(8,128)(2,1)S(1)}, bf16[12,8,2048]{2,1,0:T(8,128)(2,1)S(1)}, u32[]{:S(2)}, u32[]{:S(2)}) collective-permute-start(bf16[12,8,2048]{2,1,0:T(8,128)(2,1)S(1)} %collective-permute-done.4.refs_2_), channel_id=1, source_target_pairs={{0,96},{96,0},{32,64},{64,32},{1,97},{97,1},{33,65},{65,33},{2,98}... | collective-permute-start | bytes 1179656 | tf_op jit(solution)/shard_map/ppermute | solution.py:32
  47.3 1.2 %collective-permute-done.7.refs_5_ = bf16[12,8,2048]{2,1,0:T(8,128)(2,1)S(1)} collective-permute-done((bf16[12,8,2048]{2,1,0:T(8,128)(2,1)S(1)}, bf16[12,8,2048]{2,1,0:T(8,128)(2,1)S(1)}, u32[]{:S(2)}, u32[]{:S(2)}) %collective-permute-start.7) | collective-permute-done | bytes 393248 | tf_op jit(solution)/shard_map/ppermute | solution.py:32
  48.6 0.7 collective-permute-start.19
  49.3 0.0 collective-permute-start.9
  49.3 0.1 pad_maximum_fusion.3
  49.4 0.7 collective-permute-done.5.refs_3_
  50.1 0.1 collective-permute-done.18.refs_14_
  50.2 4.8 %collective-permute-done.8.refs_6_ = bf16[12,8,2048]{2,1,0:T(8,128)(2,1)S(1)} collective-permute-done((bf16[12,8,2048]{2,1,0:T(8,128)(2,1)S(1)}, bf16[12,8,2048]{2,1,0:T(8,128)(2,1)S(1)}, u32[]{:S(2)}, u32[]{:S(2)}) %collective-permute-start.8) | collective-permute-done | bytes 393248 | tf_op jit(solution)/shard_map/ppermute | solution.py:32
  54.9 1.4 %collective-permute-done.19.refs_15_ = bf16[12,8,2048]{2,1,0:T(8,128)(2,1)S(1)} collective-permute-done((bf16[12,8,2048]{2,1,0:T(8,128)(2,1)S(1)}, bf16[12,8,2048]{2,1,0:T(8,128)(2,1)S(1)}, u32[]{:S(2)}, u32[]{:S(2)}) %collective-permute-start.19) | collective-permute-done | bytes 393248 | tf_op jit(solution)/shard_map/ppermute | solution.py:32
  56.3 0.7 collective-permute-done.9.refs_7_
  57.2 0.6 copy-done.17
  57.8 9.3 %products.1 = (f32[12,64,128]{2,1,0:T(8,128)}, bf16[23,16,128]{2,1,0:T(8,128)(2,1)}, bf16[23,16,128]{2,1,0:T(8,128)(2,1)}, bf16[17,16,128]{2,1,0:T(8,128)(2,1)},...) custom-call(bf16[12,8,2048]{2,1,0:T(8,128)(2,1)} %copy-done.3, ...), custom_call_target="tpu_custom_call" | custom-call | tf_op jit(solution)/shard_map/products/pallas_call | solution.py:175
  67.1 7.1 %collective-permute-start.24 = (bf16[15,16,128]{2,1,0:T(8,128)(2,1)}, bf16[15,16,128]{2,1,0:T(8,128)(2,1)S(1)}, u32[]{:S(2)}, u32[]{:S(2)}) collective-permute-start(bf16[15,16,128]{2,1,0:T(8,128)(2,1)} %get-tuple-element.18), channel_id=1, source_target_pairs={{0,3},{1,4},{2,5},{3,6},{4,7},{5,0},{6,1},{7,2},{8,11},{9,12},{10,... | collective-permute-start | bytes 184328 | tf_op jit(solution)/shard_map/ppermute | solution.py:21
  74.2 0.7 pad_maximum_fusion.4.refs_11_
  74.9 0.4 collective-permute-start.20
  75.3 1.8 %collective-permute-start.21 = (bf16[23,16,128]{2,1,0:T(8,128)(2,1)}, bf16[23,16,128]{2,1,0:T(8,128)(2,1)S(1)}, u32[]{:S(2)}, u32[]{:S(2)}) collective-permute-start(bf16[23,16,128]{2,1,0:T(8,128)(2,1)} %get-tuple-element.15.refs_8_), channel_id=1, source_target_pairs={{0,7},{1,0},{2,1},{3,2},{4,3},{5,4},{6,5},{7,6},{8,15},{9,8},{10,9... | collective-permute-start | bytes 282632 | tf_op jit(solution)/shard_map/ppermute | solution.py:21
  77.1 1.5 %collective-permute-start.22 = (bf16[17,16,128]{2,1,0:T(8,128)(2,1)}, bf16[17,16,128]{2,1,0:T(8,128)(2,1)S(1)}, u32[]{:S(2)}, u32[]{:S(2)}) collective-permute-start(bf16[17,16,128]{2,1,0:T(8,128)(2,1)} %get-tuple-element.16), channel_id=1, source_target_pairs={{0,2},{1,3},{2,4},{3,5},{4,6},{5,7},{6,0},{7,1},{8,10},{9,11},{10,... | collective-permute-start | bytes 208904 | tf_op jit(solution)/shard_map/ppermute | solution.py:21
  78.6 3.9 %collective-permute-done.26.refs_6_ = bf16[5,16,128]{2,1,0:T(8,128)(2,1)S(1)} collective-permute-done((bf16[5,16,128]{2,1,0:T(8,128)(2,1)}, bf16[5,16,128]{2,1,0:T(8,128)(2,1)S(1)}, u32[]{:S(2)}, u32[]{:S(2)}) %collective-permute-start.26) | collective-permute-done | bytes 20512 | tf_op jit(solution)/shard_map/ppermute | solution.py:21
  82.5 1.9 %collective-permute-start.25 = (bf16[15,16,128]{2,1,0:T(8,128)(2,1)}, bf16[15,16,128]{2,1,0:T(8,128)(2,1)S(1)}, u32[]{:S(2)}, u32[]{:S(2)}) collective-permute-start(bf16[15,16,128]{2,1,0:T(8,128)(2,1)} %get-tuple-element.19), channel_id=1, source_target_pairs={{0,5},{1,6},{2,7},{3,0},{4,1},{5,2},{6,3},{7,4},{8,13},{9,14},{10,... | collective-permute-start | bytes 184328 | tf_op jit(solution)/shard_map/ppermute | solution.py:21
  84.4 0.7 pad_maximum_fusion.5.refs_12_
  85.1 5.7 %collective-permute-done.25.refs_5_ = bf16[15,16,128]{2,1,0:T(8,128)(2,1)S(1)} collective-permute-done((bf16[15,16,128]{2,1,0:T(8,128)(2,1)}, bf16[15,16,128]{2,1,0:T(8,128)(2,1)S(1)}, u32[]{:S(2)}, u32[]{:S(2)}) %collective-permute-start.25) | collective-permute-done | bytes 61472 | tf_op jit(solution)/shard_map/ppermute | solution.py:21
  90.9 0.5 copy-done.23
  91.5 0.0 copy-done.20
  91.5 0.0 copy-done.21
  91.5 0.0 copy-done.18
  91.5 0.0 copy-done.19
  91.6 2.5 %branches.1 = bf16[16,136,128]{2,1,0:T(8,128)(2,1)} custom-call(f32[12,64,128]{2,1,0:T(8,128)} %get-tuple-element.13.centre, bf16[23,16,128]{2,1,0:T(8,128)(2,1)} %copy-done.18, bf16[23,16,128]{2,1,0:T(8,128)(2,1)} %copy-done.19, bf16[17,16,128]{2,1,0:T(8,128)(2,1)} %copy-done.20, bf16[17,16,128]{2,1,0:T(8,128)(2,1)} %copy-done.21, ...), custom_call_target="tpu_custom_call" | custom-call | tf_op jit(solution)/shard_map/branches/pallas_call | solution.py:261
  94.1 3.8 %all-to-all-start = ((bf16[16,136,128]{2,1,0:T(8,128)(2,1)}), bf16[16,136,128]{2,1,0:T(8,128)(2,1)S(1)}, u32[]{:S(2)}, u32[]{:S(2)}) async-start(bf16[16,136,128]{2,1,0:T(8,128)(2,1)} %branches.1), calls=%async_computation | async-start | bytes 1114112 | tf_op jit(solution)/shard_map/all_to_all | solution.py:472
  97.9 1.3 %spread.1.refs_3_ = bf16[640,192]{1,0:T(8,128)(2,1)} custom-call(), custom_call_target="tpu_custom_call" | custom-call | tf_op jit(solution)/shard_map/spread/pallas_call | solution.py:411
  99.3 0.1 fusion.7
  99.4 1.0 pad_maximum_fusion.2.refs_4_
  100.4 7.8 %all-to-all-done.refs_0_ = bf16[16,136,128]{2,1,0:T(8,128)(2,1)S(1)} async-done(((bf16[16,136,128]{2,1,0:T(8,128)(2,1)}), bf16[16,136,128]{2,1,0:T(8,128)(2,1)S(1)}, u32[]{:S(2)}, u32[]{:S(2)}) %all-to-all-start) | async-done | bytes 557088 | tf_op jit(solution)/shard_map/all_to_all | solution.py:472
  108.2 0.8 copy-done.1
  109.0 7.2 %decode.1 = bf16[16,24,256]{2,1,0:T(8,128)(2,1)} custom-call(bf16[16,136,128]{2,1,0:T(8,128)(2,1)} %copy-done.1, bf16[5,16,16,256]{3,2,1,0:T(8,128)(2,1)} %bitcast.27, f32[1,256]{1,0:T(1,128)} %bitcast.34, bf16[640,192]{1,0:T(8,128)(2,1)} %spread.1.refs_3_, bf16[640,144]{1,0:T(8,128)(2,1)} %pad_maximum_fusion.2.refs_4_, bf16[3,3,304,256]{3,2,1,0:T(8,128)(2,1)} %refs_5_.1, ...), custom_call_target="tpu_custom_call" | custom-call | tf_op jit(solution)/shard_map/decode/pallas_call | solution.py:369
  (75 shorter events, 0.4 us)
Async XLA Ops:
  0.0 7.3 %copy-start = (bf16[16,24,256]{2,1,0:T(8,128)(2,1)S(1)}, bf16[16,24,256]{2,1,0:T(8,128)(2,1)}, u32[]{:S(2)}) copy-start(bf16[16,24,256]{2,1,0:T(8,128)(2,1)} %param.15) | copy-start | bytes 589828
  1.1 13.2 %collective-permute-start.11 = (bf16[6,8,2048]{2,1,0:T(8,128)(2,1)S(1)}, bf16[6,8,2048]{2,1,0:T(8,128)(2,1)S(1)}, u32[]{:S(2)}, u32[]{:S(2)}) collective-permute-start(bf16[6,8,2048]{2,1,0:T(8,128)(2,1)S(1)} %get-tuple-element.21), channel_id=1, source_target_pairs={{0,96},{96,0},{32,64},{64,32},{1,97},{97,1},{33,65},{65,33},{2,98}... | collective-permute-start | bytes 589832 | tf_op jit(solution)/shard_map/ppermute | solution.py:32
  4.2 8.0 %collective-permute-start.10 = (bf16[6,8,2048]{2,1,0:T(8,128)(2,1)S(1)}, bf16[6,8,2048]{2,1,0:T(8,128)(2,1)S(1)}, u32[]{:S(2)}, u32[]{:S(2)}) collective-permute-start(bf16[6,8,2048]{2,1,0:T(8,128)(2,1)S(1)} %get-tuple-element.21), channel_id=1, source_target_pairs={{0,32},{32,0},{64,96},{96,64},{1,33},{33,1},{65,97},{97,65},{2,34}... | collective-permute-start | bytes 589832 | tf_op jit(solution)/shard_map/ppermute | solution.py:32
  4.3 12.2 %collective-permute-start.1 = (bf16[6,8,2048]{2,1,0:T(8,128)(2,1)S(1)}, bf16[6,8,2048]{2,1,0:T(8,128)(2,1)S(1)}, u32[]{:S(2)}, u32[]{:S(2)}) collective-permute-start(bf16[6,8,2048]{2,1,0:T(8,128)(2,1)S(1)} %get-tuple-element.22), channel_id=1, source_target_pairs={{0,24},{24,0},{8,16},{16,8},{1,25},{25,1},{9,17},{17,9},{2,26},{26... | collective-permute-start | bytes 589832 | tf_op jit(solution)/shard_map/ppermute | solution.py:32
  7.1 8.4 %collective-permute-start = (bf16[6,8,2048]{2,1,0:T(8,128)(2,1)S(1)}, bf16[6,8,2048]{2,1,0:T(8,128)(2,1)S(1)}, u32[]{:S(2)}, u32[]{:S(2)}) collective-permute-start(bf16[6,8,2048]{2,1,0:T(8,128)(2,1)S(1)} %get-tuple-element.22), channel_id=1, source_target_pairs={{0,8},{8,0},{16,24},{24,16},{1,9},{9,1},{17,25},{25,17},{2,10},{10... | collective-permute-start | bytes 589832 | tf_op jit(solution)/shard_map/ppermute | solution.py:32
  8.4 18.6 %collective-permute-start.27 = (bf16[16,2,48]{2,1,0:T(2,128)(2,1)S(1)}, bf16[16,2,48]{2,1,0:T(2,128)(2,1)S(1)}, u32[]{:S(2)}, u32[]{:S(2)}) collective-permute-start(bf16[16,2,48]{2,1,0:T(2,128)(2,1)S(1)} %get-tuple-element.27), channel_id=1, source_target_pairs={{0,1},{1,2},{2,3},{3,4},{4,5},{5,6},{6,7},{8,9},{9,10},{10,11},{11... | collective-permute-start | bytes 9224 | tf_op jit(solution)/shard_map/ppermute | solution.py:27
  12.2 16.1 %collective-permute-start.28 = (bf16[16,2,48]{2,1,0:T(2,128)(2,1)S(1)}, bf16[16,2,48]{2,1,0:T(2,128)(2,1)S(1)}, u32[]{:S(2)}, u32[]{:S(2)}) collective-permute-start(bf16[16,2,48]{2,1,0:T(2,128)(2,1)S(1)} %get-tuple-element.28), channel_id=1, source_target_pairs={{1,0},{2,1},{3,2},{4,3},{5,4},{6,5},{7,6},{9,8},{10,9},{11,10},{12... | collective-permute-start | bytes 9224 | tf_op jit(solution)/shard_map/ppermute | solution.py:27
  14.3 5.9 %collective-permute-start.12 = (bf16[3,8,2048]{2,1,0:T(8,128)(2,1)S(1)}, bf16[3,8,2048]{2,1,0:T(8,128)(2,1)S(1)}, u32[]{:S(2)}, u32[]{:S(2)}) collective-permute-start(bf16[3,8,2048]{2,1,0:T(8,128)(2,1)S(1)} %slice.76), channel_id=1, source_target_pairs={{0,96},{96,0},{32,64},{64,32},{1,97},{97,1},{33,65},{65,33},{2,98}... | collective-permute-start | bytes 294920 | tf_op jit(solution)/shard_map/ppermute | solution.py:32
  15.5 33.8 %copy-start.2 = (bf16[12,8,2048]{2,1,0:T(8,128)(2,1)}, bf16[12,8,2048]{2,1,0:T(8,128)(2,1)S(1)}, u32[]{:S(2)}) copy-start(bf16[12,8,2048]{2,1,0:T(8,128)(2,1)S(1)} %pad_maximum_fusion.1.refs_8_) | copy-start | bytes 1179652
  15.5 6.5 %collective-permute-start.13 = (bf16[3,8,2048]{2,1,0:T(8,128)(2,1)S(1)}, bf16[3,8,2048]{2,1,0:T(8,128)(2,1)S(1)}, u32[]{:S(2)}, u32[]{:S(2)}) collective-permute-start(bf16[3,8,2048]{2,1,0:T(8,128)(2,1)S(1)} %slice.77), channel_id=1, source_target_pairs={{0,32},{32,0},{64,96},{96,64},{1,33},{33,1},{65,97},{97,65},{2,34}... | collective-permute-start | bytes 294920 | tf_op jit(solution)/shard_map/ppermute | solution.py:32
  16.5 40.5 %copy-start.3 = (bf16[12,8,2048]{2,1,0:T(8,128)(2,1)}, bf16[12,8,2048]{2,1,0:T(8,128)(2,1)S(1)}, u32[]{:S(2)}) copy-start(bf16[12,8,2048]{2,1,0:T(8,128)(2,1)S(1)} %pad_maximum_fusion.refs_0_) | copy-start | bytes 1179652
  16.5 5.9 %collective-permute-start.2 = (bf16[3,8,2048]{2,1,0:T(8,128)(2,1)S(1)}, bf16[3,8,2048]{2,1,0:T(8,128)(2,1)S(1)}, u32[]{:S(2)}, u32[]{:S(2)}) collective-permute-start(bf16[3,8,2048]{2,1,0:T(8,128)(2,1)S(1)} %slice.73), channel_id=1, source_target_pairs={{0,24},{24,0},{8,16},{16,8},{1,25},{25,1},{9,17},{17,9},{2,26},{26... | collective-permute-start | bytes 294920 | tf_op jit(solution)/shard_map/ppermute | solution.py:32
  20.2 5.7 %collective-permute-start.3 = (bf16[3,8,2048]{2,1,0:T(8,128)(2,1)S(1)}, bf16[3,8,2048]{2,1,0:T(8,128)(2,1)S(1)}, u32[]{:S(2)}, u32[]{:S(2)}) collective-permute-start(bf16[3,8,2048]{2,1,0:T(8,128)(2,1)S(1)} %slice.74), channel_id=1, source_target_pairs={{0,8},{8,0},{16,24},{24,16},{1,9},{9,1},{17,25},{25,17},{2,10},{10... | collective-permute-start | bytes 294920 | tf_op jit(solution)/shard_map/ppermute | solution.py:32
  22.0 9.2 %collective-permute-start.14 = (bf16[12,8,2048]{2,1,0:T(8,128)(2,1)S(1)}, bf16[12,8,2048]{2,1,0:T(8,128)(2,1)S(1)}, u32[]{:S(2)}, u32[]{:S(2)}) collective-permute-start(bf16[12,8,2048]{2,1,0:T(8,128)(2,1)S(1)} %pad_maximum_fusion.1.refs_8_), channel_id=1, source_target_pairs={{0,8},{8,0},{16,24},{24,16},{1,9},{9,1},{17,25},{25,17},{2,10},{10... | collective-permute-start | bytes 1179656 | tf_op jit(solution)/shard_map/ppermute | solution.py:32
  22.3 34.7 %copy-start.5 = (bf16[12,8,2048]{2,1,0:T(8,128)(2,1)}, bf16[12,8,2048]{2,1,0:T(8,128)(2,1)S(1)}, u32[]{:S(2)}) copy-start(bf16[12,8,2048]{2,1,0:T(8,128)(2,1)S(1)} %constant_dynamic-update-slice_fusion.3.refs_9_) | copy-start | bytes 1179652
  22.5 10.0 %collective-permute-start.4 = (bf16[12,8,2048]{2,1,0:T(8,128)(2,1)S(1)}, bf16[12,8,2048]{2,1,0:T(8,128)(2,1)S(1)}, u32[]{:S(2)}, u32[]{:S(2)}) collective-permute-start(bf16[12,8,2048]{2,1,0:T(8,128)(2,1)S(1)} %pad_maximum_fusion.refs_0_), channel_id=1, source_target_pairs={{0,32},{32,0},{64,96},{96,64},{1,33},{33,1},{65,97},{97,65},{2,34}... | collective-permute-start | bytes 1179656 | tf_op jit(solution)/shard_map/ppermute | solution.py:32
  25.9 13.2 %collective-permute-start.16 = (bf16[12,8,2048]{2,1,0:T(8,128)(2,1)S(1)}, bf16[12,8,2048]{2,1,0:T(8,128)(2,1)S(1)}, u32[]{:S(2)}, u32[]{:S(2)}) collective-permute-start(bf16[12,8,2048]{2,1,0:T(8,128)(2,1)S(1)} %pad_maximum_fusion.1.refs_8_), channel_id=1, source_target_pairs={{0,24},{24,0},{8,16},{16,8},{1,25},{25,1},{9,17},{17,9},{2,26},{26... | collective-permute-start | bytes 1179656 | tf_op jit(solution)/shard_map/ppermute | solution.py:32
  27.0 30.0 %copy-start.4 = (bf16[12,8,2048]{2,1,0:T(8,128)(2,1)}, bf16[12,8,2048]{2,1,0:T(8,128)(2,1)S(1)}, u32[]{:S(2)}) copy-start(bf16[12,8,2048]{2,1,0:T(8,128)(2,1)S(1)} %constant_dynamic-update-slice_fusion.refs_1_) | copy-start | bytes 1179652
  27.0 13.1 %collective-permute-start.6 = (bf16[12,8,2048]{2,1,0:T(8,128)(2,1)S(1)}, bf16[12,8,2048]{2,1,0:T(8,128)(2,1)S(1)}, u32[]{:S(2)}, u32[]{:S(2)}) collective-permute-start(bf16[12,8,2048]{2,1,0:T(8,128)(2,1)S(1)} %pad_maximum_fusion.refs_0_), channel_id=1, source_target_pairs={{0,96},{96,0},{32,64},{64,32},{1,97},{97,1},{33,65},{65,33},{2,98}... | collective-permute-start | bytes 1179656 | tf_op jit(solution)/shard_map/ppermute | solution.py:32
  28.4 17.6 %collective-permute-start.17 = (bf16[12,8,2048]{2,1,0:T(8,128)(2,1)S(1)}, bf16[12,8,2048]{2,1,0:T(8,128)(2,1)S(1)}, u32[]{:S(2)}, u32[]{:S(2)}) collective-permute-start(bf16[12,8,2048]{2,1,0:T(8,128)(2,1)S(1)} %constant_dynamic-update-slice_fusion.3.refs_9_), channel_id=1, source_target_pairs={{0,24},{24,0},{8,16},{16,8},{1,25},{25,1},{9,17},{17,9},{2,26},{26... | collective-permute-start | bytes 1179656 | tf_op jit(solution)/shard_map/ppermute | solution.py:32
  31.2 25.8 %copy-start.6 = (bf16[12,8,2048]{2,1,0:T(8,128)(2,1)}, bf16[12,8,2048]{2,1,0:T(8,128)(2,1)S(1)}, u32[]{:S(2)}) copy-start(bf16[12,8,2048]{2,1,0:T(8,128)(2,1)S(1)} %collective-permute-done.14.refs_10_) | copy-start | bytes 1179652
  31.2 17.3 %collective-permute-start.7 = (bf16[12,8,2048]{2,1,0:T(8,128)(2,1)S(1)}, bf16[12,8,2048]{2,1,0:T(8,128)(2,1)S(1)}, u32[]{:S(2)}, u32[]{:S(2)}) collective-permute-start(bf16[12,8,2048]{2,1,0:T(8,128)(2,1)S(1)} %constant_dynamic-update-slice_fusion.refs_1_), channel_id=1, source_target_pairs={{0,96},{96,0},{32,64},{64,32},{1,97},{97,1},{33,65},{65,33},{2,98}... | collective-permute-start | bytes 1179656 | tf_op jit(solution)/shard_map/ppermute | solution.py:32
  32.5 24.6 %copy-start.7 = (bf16[12,8,2048]{2,1,0:T(8,128)(2,1)}, bf16[12,8,2048]{2,1,0:T(8,128)(2,1)S(1)}, u32[]{:S(2)}) copy-start(bf16[12,8,2048]{2,1,0:T(8,128)(2,1)S(1)} %collective-permute-done.4.refs_2_) | copy-start | bytes 1179652
  32.5 16.8 %collective-permute-start.15 = (bf16[12,8,2048]{2,1,0:T(8,128)(2,1)S(1)}, bf16[12,8,2048]{2,1,0:T(8,128)(2,1)S(1)}, u32[]{:S(2)}, u32[]{:S(2)}) collective-permute-start(bf16[12,8,2048]{2,1,0:T(8,128)(2,1)S(1)} %constant_dynamic-update-slice_fusion.3.refs_9_), channel_id=1, source_target_pairs={{0,8},{8,0},{16,24},{24,16},{1,9},{9,1},{17,25},{25,17},{2,10},{10... | collective-permute-start | bytes 1179656 | tf_op jit(solution)/shard_map/ppermute | solution.py:32
  39.1 18.0 %copy-start.8 = (bf16[12,8,2048]{2,1,0:T(8,128)(2,1)}, bf16[12,8,2048]{2,1,0:T(8,128)(2,1)S(1)}, u32[]{:S(2)}) copy-start(bf16[12,8,2048]{2,1,0:T(8,128)(2,1)S(1)} %collective-permute-done.16.refs_12_) | copy-start | bytes 1179652
  39.1 11.0 %collective-permute-start.5 = (bf16[12,8,2048]{2,1,0:T(8,128)(2,1)S(1)}, bf16[12,8,2048]{2,1,0:T(8,128)(2,1)S(1)}, u32[]{:S(2)}, u32[]{:S(2)}) collective-permute-start(bf16[12,8,2048]{2,1,0:T(8,128)(2,1)S(1)} %constant_dynamic-update-slice_fusion.refs_1_), channel_id=1, source_target_pairs={{0,32},{32,0},{64,96},{96,64},{1,33},{33,1},{65,97},{97,65},{2,34}... | collective-permute-start | bytes 1179656 | tf_op jit(solution)/shard_map/ppermute | solution.py:32
  40.1 17.0 %copy-start.9 = (bf16[12,8,2048]{2,1,0:T(8,128)(2,1)}, bf16[12,8,2048]{2,1,0:T(8,128)(2,1)S(1)}, u32[]{:S(2)}) copy-start(bf16[12,8,2048]{2,1,0:T(8,128)(2,1)S(1)} %collective-permute-done.6.refs_4_) | copy-start | bytes 1179652
  40.1 10.0 %collective-permute-start.18 = (bf16[12,8,2048]{2,1,0:T(8,128)(2,1)S(1)}, bf16[12,8,2048]{2,1,0:T(8,128)(2,1)S(1)}, u32[]{:S(2)}, u32[]{:S(2)}) collective-permute-start(bf16[12,8,2048]{2,1,0:T(8,128)(2,1)S(1)} %collective-permute-done.14.refs_10_), channel_id=1, source_target_pairs={{0,24},{24,0},{8,16},{16,8},{1,25},{25,1},{9,17},{17,9},{2,26},{26... | collective-permute-start | bytes 1179656 | tf_op jit(solution)/shard_map/ppermute | solution.py:32
  45.9 11.1 %copy-start.10 = (bf16[12,8,2048]{2,1,0:T(8,128)(2,1)}, bf16[12,8,2048]{2,1,0:T(8,128)(2,1)S(1)}, u32[]{:S(2)}) copy-start(bf16[12,8,2048]{2,1,0:T(8,128)(2,1)S(1)} %collective-permute-done.17.refs_13_) | copy-start | bytes 1179652
  45.9 9.0 %collective-permute-start.8 = (bf16[12,8,2048]{2,1,0:T(8,128)(2,1)S(1)}, bf16[12,8,2048]{2,1,0:T(8,128)(2,1)S(1)}, u32[]{:S(2)}, u32[]{:S(2)}) collective-permute-start(bf16[12,8,2048]{2,1,0:T(8,128)(2,1)S(1)} %collective-permute-done.4.refs_2_), channel_id=1, source_target_pairs={{0,96},{96,0},{32,64},{64,32},{1,97},{97,1},{33,65},{65,33},{2,98}... | collective-permute-start | bytes 1179656 | tf_op jit(solution)/shard_map/ppermute | solution.py:32
  48.6 8.5 %copy-start.11 = (bf16[12,8,2048]{2,1,0:T(8,128)(2,1)}, bf16[12,8,2048]{2,1,0:T(8,128)(2,1)S(1)}, u32[]{:S(2)}) copy-start(bf16[12,8,2048]{2,1,0:T(8,128)(2,1)S(1)} %collective-permute-done.7.refs_5_) | copy-start | bytes 1179652
  48.6 7.8 %collective-permute-start.19 = (bf16[12,8,2048]{2,1,0:T(8,128)(2,1)S(1)}, bf16[12,8,2048]{2,1,0:T(8,128)(2,1)S(1)}, u32[]{:S(2)}, u32[]{:S(2)}) collective-permute-start(bf16[12,8,2048]{2,1,0:T(8,128)(2,1)S(1)} %collective-permute-done.17.refs_13_), channel_id=1, source_target_pairs={{0,8},{8,0},{16,24},{24,16},{1,9},{9,1},{17,25},{25,17},{2,10},{10... | collective-permute-start | bytes 1179656 | tf_op jit(solution)/shard_map/ppermute | solution.py:32
  49.3 7.9 %copy-start.12 = (bf16[12,8,2048]{2,1,0:T(8,128)(2,1)}, bf16[12,8,2048]{2,1,0:T(8,128)(2,1)S(1)}, u32[]{:S(2)}) copy-start(bf16[12,8,2048]{2,1,0:T(8,128)(2,1)S(1)} %collective-permute-done.15.refs_11_) | copy-start | bytes 1179652
  49.3 7.8 %collective-permute-start.9 = (bf16[12,8,2048]{2,1,0:T(8,128)(2,1)S(1)}, bf16[12,8,2048]{2,1,0:T(8,128)(2,1)S(1)}, u32[]{:S(2)}, u32[]{:S(2)}) collective-permute-start(bf16[12,8,2048]{2,1,0:T(8,128)(2,1)S(1)} %collective-permute-done.7.refs_5_), channel_id=1, source_target_pairs={{0,32},{32,0},{64,96},{96,64},{1,33},{33,1},{65,97},{97,65},{2,34}... | collective-permute-start | bytes 1179656 | tf_op jit(solution)/shard_map/ppermute | solution.py:32
  50.1 7.0 %copy-start.13 = (bf16[12,8,2048]{2,1,0:T(8,128)(2,1)}, bf16[12,8,2048]{2,1,0:T(8,128)(2,1)S(1)}, u32[]{:S(2)}) copy-start(bf16[12,8,2048]{2,1,0:T(8,128)(2,1)S(1)} %collective-permute-done.5.refs_3_) | copy-start | bytes 1179652
  50.2 7.0 %copy-start.14 = (bf16[12,8,2048]{2,1,0:T(8,128)(2,1)}, bf16[12,8,2048]{2,1,0:T(8,128)(2,1)S(1)}, u32[]{:S(2)}) copy-start(bf16[12,8,2048]{2,1,0:T(8,128)(2,1)S(1)} %collective-permute-done.18.refs_14_) | copy-start | bytes 1179652
  54.9 2.2 %copy-start.15 = (bf16[12,8,2048]{2,1,0:T(8,128)(2,1)}, bf16[12,8,2048]{2,1,0:T(8,128)(2,1)S(1)}, u32[]{:S(2)}) copy-start(bf16[12,8,2048]{2,1,0:T(8,128)(2,1)S(1)} %collective-permute-done.8.refs_6_) | copy-start | bytes 1179652
  56.3 0.8 copy-start.16
  57.0 0.7 copy-start.17
  67.1 15.4 %collective-permute-start.24 = (bf16[15,16,128]{2,1,0:T(8,128)(2,1)}, bf16[15,16,128]{2,1,0:T(8,128)(2,1)S(1)}, u32[]{:S(2)}, u32[]{:S(2)}) collective-permute-start(bf16[15,16,128]{2,1,0:T(8,128)(2,1)} %get-tuple-element.18), channel_id=1, source_target_pairs={{0,3},{1,4},{2,5},{3,6},{4,7},{5,0},{6,1},{7,2},{8,11},{9,12},{10,... | collective-permute-start | bytes 184328 | tf_op jit(solution)/shard_map/ppermute | solution.py:21
  74.2 8.2 %collective-permute-start.26 = (bf16[5,16,128]{2,1,0:T(8,128)(2,1)}, bf16[5,16,128]{2,1,0:T(8,128)(2,1)S(1)}, u32[]{:S(2)}, u32[]{:S(2)}) collective-permute-start(bf16[5,16,128]{2,1,0:T(8,128)(2,1)} %get-tuple-element.20.refs_9_), channel_id=1, source_target_pairs={{0,4},{1,5},{2,6},{3,7},{4,0},{5,1},{6,2},{7,3},{8,12},{9,13},{10,... | collective-permute-start | bytes 61448 | tf_op jit(solution)/shard_map/ppermute | solution.py:21
  74.9 15.9 %collective-permute-start.20 = (bf16[23,16,128]{2,1,0:T(8,128)(2,1)}, bf16[23,16,128]{2,1,0:T(8,128)(2,1)S(1)}, u32[]{:S(2)}, u32[]{:S(2)}) collective-permute-start(bf16[23,16,128]{2,1,0:T(8,128)(2,1)} %get-tuple-element.14.refs_7_), channel_id=1, source_target_pairs={{0,1},{1,2},{2,3},{3,4},{4,5},{5,6},{6,7},{7,0},{8,9},{9,10},{10,1... | collective-permute-start | bytes 282632 | tf_op jit(solution)/shard_map/ppermute | solution.py:21
  75.3 15.6 %collective-permute-start.21 = (bf16[23,16,128]{2,1,0:T(8,128)(2,1)}, bf16[23,16,128]{2,1,0:T(8,128)(2,1)S(1)}, u32[]{:S(2)}, u32[]{:S(2)}) collective-permute-start(bf16[23,16,128]{2,1,0:T(8,128)(2,1)} %get-tuple-element.15.refs_8_), channel_id=1, source_target_pairs={{0,7},{1,0},{2,1},{3,2},{4,3},{5,4},{6,5},{7,6},{8,15},{9,8},{10,9... | collective-permute-start | bytes 282632 | tf_op jit(solution)/shard_map/ppermute | solution.py:21
  77.1 13.7 %collective-permute-start.22 = (bf16[17,16,128]{2,1,0:T(8,128)(2,1)}, bf16[17,16,128]{2,1,0:T(8,128)(2,1)S(1)}, u32[]{:S(2)}, u32[]{:S(2)}) collective-permute-start(bf16[17,16,128]{2,1,0:T(8,128)(2,1)} %get-tuple-element.16), channel_id=1, source_target_pairs={{0,2},{1,3},{2,4},{3,5},{4,6},{5,7},{6,0},{7,1},{8,10},{9,11},{10,... | collective-permute-start | bytes 208904 | tf_op jit(solution)/shard_map/ppermute | solution.py:21
  82.5 8.4 %copy-start.24 = (bf16[5,16,128]{2,1,0:T(8,128)(2,1)}, bf16[5,16,128]{2,1,0:T(8,128)(2,1)S(1)}, u32[]{:S(2)}) copy-start(bf16[5,16,128]{2,1,0:T(8,128)(2,1)S(1)} %collective-permute-done.26.refs_6_) | copy-start | bytes 61444
  82.5 8.4 %collective-permute-start.23 = (bf16[17,16,128]{2,1,0:T(8,128)(2,1)}, bf16[17,16,128]{2,1,0:T(8,128)(2,1)S(1)}, u32[]{:S(2)}, u32[]{:S(2)}) collective-permute-start(bf16[17,16,128]{2,1,0:T(8,128)(2,1)} %get-tuple-element.17), channel_id=1, source_target_pairs={{0,6},{1,7},{2,0},{3,1},{4,2},{5,3},{6,4},{7,5},{8,14},{9,15},{10,... | collective-permute-start | bytes 208904 | tf_op jit(solution)/shard_map/ppermute | solution.py:21
  82.5 8.4 %copy-start.22 = (bf16[15,16,128]{2,1,0:T(8,128)(2,1)}, bf16[15,16,128]{2,1,0:T(8,128)(2,1)S(1)}, u32[]{:S(2)}) copy-start(bf16[15,16,128]{2,1,0:T(8,128)(2,1)S(1)} %collective-permute-done.24.refs_4_) | copy-start | bytes 184324
  82.5 8.3 %collective-permute-start.25 = (bf16[15,16,128]{2,1,0:T(8,128)(2,1)}, bf16[15,16,128]{2,1,0:T(8,128)(2,1)S(1)}, u32[]{:S(2)}, u32[]{:S(2)}) collective-permute-start(bf16[15,16,128]{2,1,0:T(8,128)(2,1)} %get-tuple-element.19), channel_id=1, source_target_pairs={{0,5},{1,6},{2,7},{3,0},{4,1},{5,2},{6,3},{7,4},{8,13},{9,14},{10,... | collective-permute-start | bytes 184328 | tf_op jit(solution)/shard_map/ppermute | solution.py:21
  90.8 0.6 copy-start.23
  90.8 0.7 copy-start.20
  90.8 0.7 copy-start.21
  90.9 0.7 copy-start.18
  90.9 0.7 copy-start.19
  94.1 14.1 %all-to-all-start = ((bf16[16,136,128]{2,1,0:T(8,128)(2,1)}), bf16[16,136,128]{2,1,0:T(8,128)(2,1)S(1)}, u32[]{:S(2)}, u32[]{:S(2)}) async-start(bf16[16,136,128]{2,1,0:T(8,128)(2,1)} %branches.1), calls=%async_computation | async-start | bytes 1114112 | tf_op jit(solution)/shard_map/all_to_all | solution.py:472
  108.2 0.8 copy-start.1

commit v4 on v3

--- a/solution.py
+++ b/solution.py
@@ -30,6 +30,10 @@
 def swap(value, axis, near):
     pairs = ((0, 1), (2, 3)) if near else ((0, 3), (1, 2))
     return lax.ppermute(value, axis, [way for a, b in pairs for way in ((a, b), (b, a))])
+
+
+def on_chip(value):
+    return pltpu.with_memory_space_constraint(value, pltpu.VMEM)
 
 
 OWN, NEAR, WRAP, FAR = range(4)
@@ -170,13 +174,13 @@
 
 def products(pieces, atrous, point, pool):
     depth = atrous.shape[1]
-    sides = [jax.ShapeDtypeStruct((size, 16, MAP_ROWS), BF) for size in SIZES for _ in range(2)]
+    sides = [pltpu.VMEM((size, 16, MAP_ROWS), BF) for size in SIZES for _ in range(2)]
     anywhere = pl.BlockSpec(memory_space=pl.ANY)
     return pl.pallas_call(
         products_kernel,
-        out_shape=[jax.ShapeDtypeStruct((12, 64, MAP_ROWS), F32)]
+        out_shape=[pltpu.VMEM((12, 64, MAP_ROWS), F32)]
         + sides
-        + [jax.ShapeDtypeStruct((5, 16, MAP_ROWS), BF)],
+        + [pltpu.VMEM((5, 16, MAP_ROWS), BF)],
         in_specs=[anywhere] * 19,
         scratch_shapes=[
             pltpu.VMEM((12, 16, 8, depth), BF),
@@ -260,12 +264,12 @@
     vmem = pl.BlockSpec(memory_space=pltpu.VMEM)
     return pl.pallas_call(
         branches_kernel,
-        out_shape=jax.ShapeDtypeStruct((16, SLOT, 128), BF),
+        out_shape=pltpu.VMEM((16, SLOT, 128), BF),
         in_specs=[vmem] * 14,
         scratch_shapes=[pltpu.VMEM((8, 144, 128), F32), pltpu.VMEM((16, SLOT, 128), F32)],
         compiler_params=pltpu.CompilerParams(vmem_limit_bytes=VMEM_BYTES),
         name="branches",
-    )(centre, *moved, opposite, own_left, own_right, own_terms, bias, top, bottom)
+    )(*map(on_chip, (centre, *moved, opposite, own_left, own_right, own_terms)), bias, top, bottom)
 
 
 def coarse_tile(received, weight, pool_weight, bias):
@@ -385,7 +389,7 @@
         ],
         compiler_params=pltpu.CompilerParams(vmem_limit_bytes=VMEM_BYTES),
         name="decode",
-    )(received, proj, bias, spread, low, w1, b1, w2, b2)
+    )(on_chip(received), proj, bias, on_chip(spread), on_chip(low), w1, b1, w2, b2)
 
 
 def spread_kernel(out):
@@ -410,7 +414,7 @@
 def spread_matrix():
     return pl.pallas_call(
         spread_kernel,
-        out_shape=jax.ShapeDtypeStruct((640, 192), BF),
+        out_shape=pltpu.VMEM((640, 192), BF),
         name="spread",
     )()
 

time: 117 us -> 114 us (0.974)
  Pallas kernels: 20.4 us -> 17.7 us
  local copies, waits for them, and re-layouts: 3.68 us -> 2.15 us
    pallas_call x3, Pallas kernels: 13.2 us -> 11 us  [the longest x1 8.44 us: products(): pl.pallas_call(products_kernel, out_shape=[pltpu.VMEM((12, 64, MAP_ROWS),...]
    unnamed x54 -> x38, local copies, waits for them, and re-layouts: 2.24 us -> 0.71 us
    all_to_all x1, waiting for transfers between devices: 7.83 us -> 9.27 us  [on_device(): lax.all_to_all(mine, ROW, split_axis=0, concat_axis=0, tiled=True)]
where the time goes in v4:
time: 114 us; the launch traced here: 113 us
  starting transfers between devices  45.3 us (40%)
  waiting for transfers between devices  44.3 us (39%)
  Pallas kernels  17.7 us (16%)
  local copies, waits for them, and re-layouts  2.15 us (2%)
  other arithmetic  1.75 us (2%)
    ppermute x20, waiting for transfers between devices, swap(): lax.ppermute(value, axis, [way for a, b in pairs for way in ((a, b), (b,...  25.7 us
    ppermute x20, starting transfers between devices, swap(): lax.ppermute(value, axis, [way for a, b in pairs for way in ((a, b), (b,...  22.9 us
    ppermute x7, starting transfers between devices, around(): lax.ppermute(value, axis, [(i, (i + by) % devices) for i in range(devices)])  12.9 us
    ppermute x7, waiting for transfers between devices, around(): lax.ppermute(value, axis, [(i, (i + by) % devices) for i in range(devices)])  9.31 us
    all_to_all x1, waiting for transfers between devices, on_device(): lax.all_to_all(mine, ROW, split_axis=0, concat_axis=0, tiled=True)  9.27 us
    pallas_call x1, Pallas kernels, products(): pl.pallas_call(products_kernel, out_shape=[pltpu.VMEM((12, 64, MAP_ROWS),...  8.44 us
    pallas_call x1, Pallas kernels, decode(): pl.pallas_call(decode_kernel, out_shape=jax.ShapeDtypeStruct((16, 24, 256...  6.69 us
    ppermute x2, starting transfers between devices, next_to(): return lax.ppermute(value, axis, pairs)  5.84 us
  transfers between devices with their start and end apart: 30, of which 16 were waited for; matrix products, arithmetic and copies ran while one was open for 3% of the time, Pallas kernels for 1%

profile of v4, /device:TPU:32, one launch (start us, length us, event | category | flops | bytes accessed | tf_op | source)
XLA Modules:
  0.0 112.6 jit_solution(5361180733833860134)
XLA Ops:
  0.0 1.1 fusion.6
  1.1 3.1 %collective-permute-start.11 = (bf16[6,8,2048]{2,1,0:T(8,128)(2,1)S(1)}, bf16[6,8,2048]{2,1,0:T(8,128)(2,1)S(1)}, u32[]{:S(2)}, u32[]{:S(2)}) collective-permute-start(bf16[6,8,2048]{2,1,0:T(8,128)(2,1)S(1)} %get-tuple-element.21), channel_id=1, source_target_pairs={{0,96},{96,0},{32,64},{64,32},{1,97},{97,1},{33,65},{65,33},{2,98}... | collective-permute-start | bytes 589832 | tf_op jit(solution)/shard_map/ppermute | solution.py:32
  4.2 0.1 collective-permute-start.10
  4.3 2.8 %collective-permute-start.1 = (bf16[6,8,2048]{2,1,0:T(8,128)(2,1)S(1)}, bf16[6,8,2048]{2,1,0:T(8,128)(2,1)S(1)}, u32[]{:S(2)}, u32[]{:S(2)}) collective-permute-start(bf16[6,8,2048]{2,1,0:T(8,128)(2,1)S(1)} %get-tuple-element.22), channel_id=1, source_target_pairs={{0,24},{24,0},{8,16},{16,8},{1,25},{25,1},{9,17},{17,9},{2,26},{26... | collective-permute-start | bytes 589832 | tf_op jit(solution)/shard_map/ppermute | solution.py:32
  7.1 0.2 collective-permute-start
  7.3 0.9 fusion.1
  8.3 0.1 copy.15
  8.4 3.8 %collective-permute-start.27 = (bf16[16,2,48]{2,1,0:T(2,128)(2,1)S(1)}, bf16[16,2,48]{2,1,0:T(2,128)(2,1)S(1)}, u32[]{:S(2)}, u32[]{:S(2)}) collective-permute-start(bf16[16,2,48]{2,1,0:T(2,128)(2,1)S(1)} %get-tuple-element.27), channel_id=1, source_target_pairs={{0,1},{1,2},{2,3},{3,4},{4,5},{5,6},{6,7},{8,9},{9,10},{10,11},{11... | collective-permute-start | bytes 9224 | tf_op jit(solution)/shard_map/ppermute | solution.py:27
  12.2 0.0 collective-permute-done.10
  12.2 2.0 %collective-permute-start.28 = (bf16[16,2,48]{2,1,0:T(2,128)(2,1)S(1)}, bf16[16,2,48]{2,1,0:T(2,128)(2,1)S(1)}, u32[]{:S(2)}, u32[]{:S(2)}) collective-permute-start(bf16[16,2,48]{2,1,0:T(2,128)(2,1)S(1)} %get-tuple-element.28), channel_id=1, source_target_pairs={{1,0},{2,1},{3,2},{4,3},{5,4},{6,5},{7,6},{9,8},{10,9},{11,10},{12... | collective-permute-start | bytes 9224 | tf_op jit(solution)/shard_map/ppermute | solution.py:27
  14.3 0.0 collective-permute-done.11
  14.3 1.1 %collective-permute-start.12 = (bf16[3,8,2048]{2,1,0:T(8,128)(2,1)S(1)}, bf16[3,8,2048]{2,1,0:T(8,128)(2,1)S(1)}, u32[]{:S(2)}, u32[]{:S(2)}) collective-permute-start(bf16[3,8,2048]{2,1,0:T(8,128)(2,1)S(1)} %slice.76), channel_id=1, source_target_pairs={{0,96},{96,0},{32,64},{64,32},{1,97},{97,1},{33,65},{65,33},{2,98}... | collective-permute-start | bytes 294920 | tf_op jit(solution)/shard_map/ppermute | solution.py:32
  15.5 0.9 collective-permute-start.13
  16.5 1.2 %collective-permute-start.2 = (bf16[3,8,2048]{2,1,0:T(8,128)(2,1)S(1)}, bf16[3,8,2048]{2,1,0:T(8,128)(2,1)S(1)}, u32[]{:S(2)}, u32[]{:S(2)}) collective-permute-start(bf16[3,8,2048]{2,1,0:T(8,128)(2,1)S(1)} %slice.73), channel_id=1, source_target_pairs={{0,24},{24,0},{8,16},{16,8},{1,25},{25,1},{9,17},{17,9},{2,26},{26... | collective-permute-start | bytes 294920 | tf_op jit(solution)/shard_map/ppermute | solution.py:32
  17.8 2.4 %collective-permute-done.12 = bf16[3,8,2048]{2,1,0:T(8,128)(2,1)S(1)} collective-permute-done((bf16[3,8,2048]{2,1,0:T(8,128)(2,1)S(1)}, bf16[3,8,2048]{2,1,0:T(8,128)(2,1)S(1)}, u32[]{:S(2)}, u32[]{:S(2)}) %collective-permute-start.12) | collective-permute-done | bytes 98336 | tf_op jit(solution)/shard_map/ppermute | solution.py:32
  20.2 1.8 %collective-permute-start.3 = (bf16[3,8,2048]{2,1,0:T(8,128)(2,1)S(1)}, bf16[3,8,2048]{2,1,0:T(8,128)(2,1)S(1)}, u32[]{:S(2)}, u32[]{:S(2)}) collective-permute-start(bf16[3,8,2048]{2,1,0:T(8,128)(2,1)S(1)} %slice.74), channel_id=1, source_target_pairs={{0,8},{8,0},{16,24},{24,16},{1,9},{9,1},{17,25},{25,17},{2,10},{10... | collective-permute-start | bytes 294920 | tf_op jit(solution)/shard_map/ppermute | solution.py:32
  22.0 0.3 collective-permute-start.14
  22.4 0.1 collective-permute-done.2
  22.5 1.2 %collective-permute-start.4 = (bf16[12,8,2048]{2,1,0:T(8,128)(2,1)S(1)}, bf16[12,8,2048]{2,1,0:T(8,128)(2,1)S(1)}, u32[]{:S(2)}, u32[]{:S(2)}) collective-permute-start(bf16[12,8,2048]{2,1,0:T(8,128)(2,1)S(1)} %pad_maximum_fusion.refs_0_), channel_id=1, source_target_pairs={{0,32},{32,0},{64,96},{96,64},{1,33},{33,1},{65,97},{97,65},{2,34}... | collective-permute-start | bytes 1179656 | tf_op jit(solution)/shard_map/ppermute | solution.py:32
  23.6 2.2 %collective-permute-done.3 = bf16[3,8,2048]{2,1,0:T(8,128)(2,1)S(1)} collective-permute-done((bf16[3,8,2048]{2,1,0:T(8,128)(2,1)S(1)}, bf16[3,8,2048]{2,1,0:T(8,128)(2,1)S(1)}, u32[]{:S(2)}, u32[]{:S(2)}) %collective-permute-start.3) | collective-permute-done | bytes 98336 | tf_op jit(solution)/shard_map/ppermute | solution.py:32
  25.9 1.1 %collective-permute-start.16 = (bf16[12,8,2048]{2,1,0:T(8,128)(2,1)S(1)}, bf16[12,8,2048]{2,1,0:T(8,128)(2,1)S(1)}, u32[]{:S(2)}, u32[]{:S(2)}) collective-permute-start(bf16[12,8,2048]{2,1,0:T(8,128)(2,1)S(1)} %pad_maximum_fusion.1.refs_8_), channel_id=1, source_target_pairs={{0,24},{24,0},{8,16},{16,8},{1,25},{25,1},{9,17},{17,9},{2,26},{26... | collective-permute-start | bytes 1179656 | tf_op jit(solution)/shard_map/ppermute | solution.py:32
  27.0 0.0 collective-permute-done.27
  27.0 1.3 %collective-permute-start.6 = (bf16[12,8,2048]{2,1,0:T(8,128)(2,1)S(1)}, bf16[12,8,2048]{2,1,0:T(8,128)(2,1)S(1)}, u32[]{:S(2)}, u32[]{:S(2)}) collective-permute-start(bf16[12,8,2048]{2,1,0:T(8,128)(2,1)S(1)} %pad_maximum_fusion.refs_0_), channel_id=1, source_target_pairs={{0,96},{96,0},{32,64},{64,32},{1,97},{97,1},{33,65},{65,33},{2,98}... | collective-permute-start | bytes 1179656 | tf_op jit(solution)/shard_map/ppermute | solution.py:32
  28.4 1.9 %collective-permute-start.17 = (bf16[12,8,2048]{2,1,0:T(8,128)(2,1)S(1)}, bf16[12,8,2048]{2,1,0:T(8,128)(2,1)S(1)}, u32[]{:S(2)}, u32[]{:S(2)}) collective-permute-start(bf16[12,8,2048]{2,1,0:T(8,128)(2,1)S(1)} %constant_dynamic-update-slice_fusion.3.refs_9_), channel_id=1, source_target_pairs={{0,24},{24,0},{8,16},{16,8},{1,25},{25,1},{9,17},{17,9},{2,26},{26... | collective-permute-start | bytes 1179656 | tf_op jit(solution)/shard_map/ppermute | solution.py:32
  30.3 1.0 collective-permute-done.14.refs_10_
  31.2 1.2 %collective-permute-start.7 = (bf16[12,8,2048]{2,1,0:T(8,128)(2,1)S(1)}, bf16[12,8,2048]{2,1,0:T(8,128)(2,1)S(1)}, u32[]{:S(2)}, u32[]{:S(2)}) collective-permute-start(bf16[12,8,2048]{2,1,0:T(8,128)(2,1)S(1)} %constant_dynamic-update-slice_fusion.refs_1_), channel_id=1, source_target_pairs={{0,96},{96,0},{32,64},{64,32},{1,97},{97,1},{33,65},{65,33},{2,98}... | collective-permute-start | bytes 1179656 | tf_op jit(solution)/shard_map/ppermute | solution.py:32
  32.5 0.9 collective-permute-start.15
  33.4 5.7 %collective-permute-done.16.refs_12_ = bf16[12,8,2048]{2,1,0:T(8,128)(2,1)S(1)} collective-permute-done((bf16[12,8,2048]{2,1,0:T(8,128)(2,1)S(1)}, bf16[12,8,2048]{2,1,0:T(8,128)(2,1)S(1)}, u32[]{:S(2)}, u32[]{:S(2)}) %collective-permute-start.16) | collective-permute-done | bytes 393248 | tf_op jit(solution)/shard_map/ppermute | solution.py:32
  39.1 0.7 collective-permute-start.5
  39.8 0.4 collective-permute-done.6.refs_4_
  40.1 0.8 collective-permute-start.18
  40.9 5.0 %collective-permute-done.17.refs_13_ = bf16[12,8,2048]{2,1,0:T(8,128)(2,1)S(1)} collective-permute-done((bf16[12,8,2048]{2,1,0:T(8,128)(2,1)S(1)}, bf16[12,8,2048]{2,1,0:T(8,128)(2,1)S(1)}, u32[]{:S(2)}, u32[]{:S(2)}) %collective-permute-start.17) | collective-permute-done | bytes 393248 | tf_op jit(solution)/shard_map/ppermute | solution.py:32
  45.9 1.4 %collective-permute-start.8 = (bf16[12,8,2048]{2,1,0:T(8,128)(2,1)S(1)}, bf16[12,8,2048]{2,1,0:T(8,128)(2,1)S(1)}, u32[]{:S(2)}, u32[]{:S(2)}) collective-permute-start(bf16[12,8,2048]{2,1,0:T(8,128)(2,1)S(1)} %collective-permute-done.4.refs_2_), channel_id=1, source_target_pairs={{0,96},{96,0},{32,64},{64,32},{1,97},{97,1},{33,65},{65,33},{2,98}... | collective-permute-start | bytes 1179656 | tf_op jit(solution)/shard_map/ppermute | solution.py:32
  47.3 1.2 %collective-permute-done.7.refs_5_ = bf16[12,8,2048]{2,1,0:T(8,128)(2,1)S(1)} collective-permute-done((bf16[12,8,2048]{2,1,0:T(8,128)(2,1)S(1)}, bf16[12,8,2048]{2,1,0:T(8,128)(2,1)S(1)}, u32[]{:S(2)}, u32[]{:S(2)}) %collective-permute-start.7) | collective-permute-done | bytes 393248 | tf_op jit(solution)/shard_map/ppermute | solution.py:32
  48.6 0.7 collective-permute-start.19
  49.3 0.0 collective-permute-start.9
  49.3 0.1 pad_maximum_fusion.3
  49.4 0.7 collective-permute-done.5.refs_3_
  50.1 0.1 collective-permute-done.18.refs_14_
  50.2 4.8 %collective-permute-done.8.refs_6_ = bf16[12,8,2048]{2,1,0:T(8,128)(2,1)S(1)} collective-permute-done((bf16[12,8,2048]{2,1,0:T(8,128)(2,1)S(1)}, bf16[12,8,2048]{2,1,0:T(8,128)(2,1)S(1)}, u32[]{:S(2)}, u32[]{:S(2)}) %collective-permute-start.8) | collective-permute-done | bytes 393248 | tf_op jit(solution)/shard_map/ppermute | solution.py:32
  54.9 1.4 %collective-permute-done.19.refs_15_ = bf16[12,8,2048]{2,1,0:T(8,128)(2,1)S(1)} collective-permute-done((bf16[12,8,2048]{2,1,0:T(8,128)(2,1)S(1)}, bf16[12,8,2048]{2,1,0:T(8,128)(2,1)S(1)}, u32[]{:S(2)}, u32[]{:S(2)}) %collective-permute-start.19) | collective-permute-done | bytes 393248 | tf_op jit(solution)/shard_map/ppermute | solution.py:32
  56.3 0.7 collective-permute-done.9.refs_7_
  57.2 0.6 copy-done.16
  57.8 8.4 %products.1 = (f32[12,64,128]{2,1,0:T(8,128)S(1)}, bf16[23,16,128]{2,1,0:T(8,128)(2,1)S(1)}, bf16[23,16,128]{2,1,0:T(8,128)(2,1)S(1)}, bf16[17,16,128]{2,1,0:T(8...) custom-call(bf16[12,8,2048]{2,1,0:T(8,128)(2,1)} %copy-done.2, ...), custom_call_target="tpu_custom_call" | custom-call | tf_op jit(solution)/shard_map/products/pallas_call | solution.py:179
  66.2 7.1 %collective-permute-start.24 = (bf16[15,16,128]{2,1,0:T(8,128)(2,1)S(1)}, bf16[15,16,128]{2,1,0:T(8,128)(2,1)S(1)}, u32[]{:S(2)}, u32[]{:S(2)}) collective-permute-start(bf16[15,16,128]{2,1,0:T(8,128)(2,1)S(1)} %get-tuple-element.18), channel_id=1, source_target_pairs={{0,3},{1,4},{2,5},{3,6},{4,7},{5,0},{6,1},{7,2},{8,11},{9,12},{10,... | collective-permute-start | bytes 184328 | tf_op jit(solution)/shard_map/ppermute | solution.py:21
  73.3 0.0 collective-permute-start.26
  73.3 0.7 pad_maximum_fusion.4.refs_11_
  74.0 0.4 collective-permute-start.20
  74.4 1.8 %collective-permute-start.21 = (bf16[23,16,128]{2,1,0:T(8,128)(2,1)S(1)}, bf16[23,16,128]{2,1,0:T(8,128)(2,1)S(1)}, u32[]{:S(2)}, u32[]{:S(2)}) collective-permute-start(bf16[23,16,128]{2,1,0:T(8,128)(2,1)S(1)} %get-tuple-element.15.refs_8_), channel_id=1, source_target_pairs={{0,7},{1,0},{2,1},{3,2},{4,3},{5,4},{6,5},{7,6},{8,15},{9,8},{10,9... | collective-permute-start | bytes 282632 | tf_op jit(solution)/shard_map/ppermute | solution.py:21
  76.2 1.5 %collective-permute-start.22 = (bf16[17,16,128]{2,1,0:T(8,128)(2,1)S(1)}, bf16[17,16,128]{2,1,0:T(8,128)(2,1)S(1)}, u32[]{:S(2)}, u32[]{:S(2)}) collective-permute-start(bf16[17,16,128]{2,1,0:T(8,128)(2,1)S(1)} %get-tuple-element.16), channel_id=1, source_target_pairs={{0,2},{1,3},{2,4},{3,5},{4,6},{5,7},{6,0},{7,1},{8,10},{9,11},{10,... | collective-permute-start | bytes 208904 | tf_op jit(solution)/shard_map/ppermute | solution.py:21
  77.7 3.7 %collective-permute-done.26.refs_6_ = bf16[5,16,128]{2,1,0:T(8,128)(2,1)S(1)} collective-permute-done((bf16[5,16,128]{2,1,0:T(8,128)(2,1)S(1)}, bf16[5,16,128]{2,1,0:T(8,128)(2,1)S(1)}, u32[]{:S(2)}, u32[]{:S(2)}) %collective-permute-start.26) | collective-permute-done | bytes 20512 | tf_op jit(solution)/shard_map/ppermute | solution.py:21
  81.4 0.0 collective-permute-start.23
  81.4 0.0 collective-permute-done.24.refs_4_
  81.4 2.1 %collective-permute-start.25 = (bf16[15,16,128]{2,1,0:T(8,128)(2,1)S(1)}, bf16[15,16,128]{2,1,0:T(8,128)(2,1)S(1)}, u32[]{:S(2)}, u32[]{:S(2)}) collective-permute-start(bf16[15,16,128]{2,1,0:T(8,128)(2,1)S(1)} %get-tuple-element.19), channel_id=1, source_target_pairs={{0,5},{1,6},{2,7},{3,0},{4,1},{5,2},{6,3},{7,4},{8,13},{9,14},{10,... | collective-permute-start | bytes 184328 | tf_op jit(solution)/shard_map/ppermute | solution.py:21
  83.5 0.7 pad_maximum_fusion.5.refs_12_
  84.1 5.6 %collective-permute-done.25.refs_5_ = bf16[15,16,128]{2,1,0:T(8,128)(2,1)S(1)} collective-permute-done((bf16[15,16,128]{2,1,0:T(8,128)(2,1)S(1)}, bf16[15,16,128]{2,1,0:T(8,128)(2,1)S(1)}, u32[]{:S(2)}, u32[]{:S(2)}) %collective-permute-start.25) | collective-permute-done | bytes 61472 | tf_op jit(solution)/shard_map/ppermute | solution.py:21
  89.7 0.0 collective-permute-done.22.refs_2_
  89.7 2.0 %branches.1 = bf16[16,136,128]{2,1,0:T(8,128)(2,1)} custom-call(f32[12,64,128]{2,1,0:T(8,128)S(1)} %get-tuple-element.13.centre, bf16[23,16,128]{2,1,0:T(8,128)(2,1)S(1)} %collective-permute-done.20.refs_0_, bf16[23,16,128]{2,1,0:T(8,128)(2,1)S(1)} %collective-permute-done.21.refs_1_, bf16[17,16,128]{2,1,0:T(8,128)(2,1)S(1)} %collective-permute-done.22.refs_2_, ...), custom_call_target="tpu_custom_call" | custom-call | tf_op jit(solution)/shard_map/branches/pallas_call | solution.py:265
  91.7 3.7 %all-to-all-start = ((bf16[16,136,128]{2,1,0:T(8,128)(2,1)}), bf16[16,136,128]{2,1,0:T(8,128)(2,1)S(1)}, u32[]{:S(2)}, u32[]{:S(2)}) async-start(bf16[16,136,128]{2,1,0:T(8,128)(2,1)} %branches.1), calls=%async_computation | async-start | bytes 1114112 | tf_op jit(solution)/shard_map/all_to_all | solution.py:476
  95.4 0.6 spread.1.refs_3_
  96.1 0.1 fusion.7
  96.2 0.3 pad_maximum_fusion.2.refs_4_
  96.5 9.3 %all-to-all-done.refs_0_ = bf16[16,136,128]{2,1,0:T(8,128)(2,1)S(1)} async-done(((bf16[16,136,128]{2,1,0:T(8,128)(2,1)}), bf16[16,136,128]{2,1,0:T(8,128)(2,1)S(1)}, u32[]{:S(2)}, u32[]{:S(2)}) %all-to-all-start) | async-done | bytes 557088 | tf_op jit(solution)/shard_map/all_to_all | solution.py:476
  105.7 6.7 %decode.1 = bf16[16,24,256]{2,1,0:T(8,128)(2,1)} custom-call(bf16[16,136,128]{2,1,0:T(8,128)(2,1)S(1)} %all-to-all-done.refs_0_, bf16[5,16,16,256]{3,2,1,0:T(8,128)(2,1)} %bitcast.27, f32[1,256]{1,0:T(1,128)} %bitcast.34, bf16[640,192]{1,0:T(8,128)(2,1)S(1)} %spread.1.refs_3_, bf16[640,144]{1,0:T(8,128)(2,1)S(1)} %pad_maximum_fusion.2.refs_4_, ...), custom_call_target="tpu_custom_call" | custom-call | tf_op jit(solution)/shard_map/decode/pallas_call | solution.py:373
  (59 shorter events, 0.3 us)
Async XLA Ops:
  0.0 7.3 %copy-start = (bf16[16,24,256]{2,1,0:T(8,128)(2,1)S(1)}, bf16[16,24,256]{2,1,0:T(8,128)(2,1)}, u32[]{:S(2)}) copy-start(bf16[16,24,256]{2,1,0:T(8,128)(2,1)} %param.15) | copy-start | bytes 589828
  1.1 13.2 %collective-permute-start.11 = (bf16[6,8,2048]{2,1,0:T(8,128)(2,1)S(1)}, bf16[6,8,2048]{2,1,0:T(8,128)(2,1)S(1)}, u32[]{:S(2)}, u32[]{:S(2)}) collective-permute-start(bf16[6,8,2048]{2,1,0:T(8,128)(2,1)S(1)} %get-tuple-element.21), channel_id=1, source_target_pairs={{0,96},{96,0},{32,64},{64,32},{1,97},{97,1},{33,65},{65,33},{2,98}... | collective-permute-start | bytes 589832 | tf_op jit(solution)/shard_map/ppermute | solution.py:32
  4.2 8.0 %collective-permute-start.10 = (bf16[6,8,2048]{2,1,0:T(8,128)(2,1)S(1)}, bf16[6,8,2048]{2,1,0:T(8,128)(2,1)S(1)}, u32[]{:S(2)}, u32[]{:S(2)}) collective-permute-start(bf16[6,8,2048]{2,1,0:T(8,128)(2,1)S(1)} %get-tuple-element.21), channel_id=1, source_target_pairs={{0,32},{32,0},{64,96},{96,64},{1,33},{33,1},{65,97},{97,65},{2,34}... | collective-permute-start | bytes 589832 | tf_op jit(solution)/shard_map/ppermute | solution.py:32
  4.3 12.2 %collective-permute-start.1 = (bf16[6,8,2048]{2,1,0:T(8,128)(2,1)S(1)}, bf16[6,8,2048]{2,1,0:T(8,128)(2,1)S(1)}, u32[]{:S(2)}, u32[]{:S(2)}) collective-permute-start(bf16[6,8,2048]{2,1,0:T(8,128)(2,1)S(1)} %get-tuple-element.22), channel_id=1, source_target_pairs={{0,24},{24,0},{8,16},{16,8},{1,25},{25,1},{9,17},{17,9},{2,26},{26... | collective-permute-start | bytes 589832 | tf_op jit(solution)/shard_map/ppermute | solution.py:32
  7.1 8.4 %collective-permute-start = (bf16[6,8,2048]{2,1,0:T(8,128)(2,1)S(1)}, bf16[6,8,2048]{2,1,0:T(8,128)(2,1)S(1)}, u32[]{:S(2)}, u32[]{:S(2)}) collective-permute-start(bf16[6,8,2048]{2,1,0:T(8,128)(2,1)S(1)} %get-tuple-element.22), channel_id=1, source_target_pairs={{0,8},{8,0},{16,24},{24,16},{1,9},{9,1},{17,25},{25,17},{2,10},{10... | collective-permute-start | bytes 589832 | tf_op jit(solution)/shard_map/ppermute | solution.py:32
  8.4 18.6 %collective-permute-start.27 = (bf16[16,2,48]{2,1,0:T(2,128)(2,1)S(1)}, bf16[16,2,48]{2,1,0:T(2,128)(2,1)S(1)}, u32[]{:S(2)}, u32[]{:S(2)}) collective-permute-start(bf16[16,2,48]{2,1,0:T(2,128)(2,1)S(1)} %get-tuple-element.27), channel_id=1, source_target_pairs={{0,1},{1,2},{2,3},{3,4},{4,5},{5,6},{6,7},{8,9},{9,10},{10,11},{11... | collective-permute-start | bytes 9224 | tf_op jit(solution)/shard_map/ppermute | solution.py:27
  12.2 16.1 %collective-permute-start.28 = (bf16[16,2,48]{2,1,0:T(2,128)(2,1)S(1)}, bf16[16,2,48]{2,1,0:T(2,128)(2,1)S(1)}, u32[]{:S(2)}, u32[]{:S(2)}) collective-permute-start(bf16[16,2,48]{2,1,0:T(2,128)(2,1)S(1)} %get-tuple-element.28), channel_id=1, source_target_pairs={{1,0},{2,1},{3,2},{4,3},{5,4},{6,5},{7,6},{9,8},{10,9},{11,10},{12... | collective-permute-start | bytes 9224 | tf_op jit(solution)/shard_map/ppermute | solution.py:27
  14.3 5.9 %collective-permute-start.12 = (bf16[3,8,2048]{2,1,0:T(8,128)(2,1)S(1)}, bf16[3,8,2048]{2,1,0:T(8,128)(2,1)S(1)}, u32[]{:S(2)}, u32[]{:S(2)}) collective-permute-start(bf16[3,8,2048]{2,1,0:T(8,128)(2,1)S(1)} %slice.76), channel_id=1, source_target_pairs={{0,96},{96,0},{32,64},{64,32},{1,97},{97,1},{33,65},{65,33},{2,98}... | collective-permute-start | bytes 294920 | tf_op jit(solution)/shard_map/ppermute | solution.py:32
  15.5 33.8 %copy-start.1 = (bf16[12,8,2048]{2,1,0:T(8,128)(2,1)}, bf16[12,8,2048]{2,1,0:T(8,128)(2,1)S(1)}, u32[]{:S(2)}) copy-start(bf16[12,8,2048]{2,1,0:T(8,128)(2,1)S(1)} %pad_maximum_fusion.1.refs_8_) | copy-start | bytes 1179652
  15.5 6.5 %collective-permute-start.13 = (bf16[3,8,2048]{2,1,0:T(8,128)(2,1)S(1)}, bf16[3,8,2048]{2,1,0:T(8,128)(2,1)S(1)}, u32[]{:S(2)}, u32[]{:S(2)}) collective-permute-start(bf16[3,8,2048]{2,1,0:T(8,128)(2,1)S(1)} %slice.77), channel_id=1, source_target_pairs={{0,32},{32,0},{64,96},{96,64},{1,33},{33,1},{65,97},{97,65},{2,34}... | collective-permute-start | bytes 294920 | tf_op jit(solution)/shard_map/ppermute | solution.py:32
  16.5 40.5 %copy-start.2 = (bf16[12,8,2048]{2,1,0:T(8,128)(2,1)}, bf16[12,8,2048]{2,1,0:T(8,128)(2,1)S(1)}, u32[]{:S(2)}) copy-start(bf16[12,8,2048]{2,1,0:T(8,128)(2,1)S(1)} %pad_maximum_fusion.refs_0_) | copy-start | bytes 1179652
  16.5 5.9 %collective-permute-start.2 = (bf16[3,8,2048]{2,1,0:T(8,128)(2,1)S(1)}, bf16[3,8,2048]{2,1,0:T(8,128)(2,1)S(1)}, u32[]{:S(2)}, u32[]{:S(2)}) collective-permute-start(bf16[3,8,2048]{2,1,0:T(8,128)(2,1)S(1)} %slice.73), channel_id=1, source_target_pairs={{0,24},{24,0},{8,16},{16,8},{1,25},{25,1},{9,17},{17,9},{2,26},{26... | collective-permute-start | bytes 294920 | tf_op jit(solution)/shard_map/ppermute | solution.py:32
  20.2 5.7 %collective-permute-start.3 = (bf16[3,8,2048]{2,1,0:T(8,128)(2,1)S(1)}, bf16[3,8,2048]{2,1,0:T(8,128)(2,1)S(1)}, u32[]{:S(2)}, u32[]{:S(2)}) collective-permute-start(bf16[3,8,2048]{2,1,0:T(8,128)(2,1)S(1)} %slice.74), channel_id=1, source_target_pairs={{0,8},{8,0},{16,24},{24,16},{1,9},{9,1},{17,25},{25,17},{2,10},{10... | collective-permute-start | bytes 294920 | tf_op jit(solution)/shard_map/ppermute | solution.py:32
  22.0 9.2 %collective-permute-start.14 = (bf16[12,8,2048]{2,1,0:T(8,128)(2,1)S(1)}, bf16[12,8,2048]{2,1,0:T(8,128)(2,1)S(1)}, u32[]{:S(2)}, u32[]{:S(2)}) collective-permute-start(bf16[12,8,2048]{2,1,0:T(8,128)(2,1)S(1)} %pad_maximum_fusion.1.refs_8_), channel_id=1, source_target_pairs={{0,8},{8,0},{16,24},{24,16},{1,9},{9,1},{17,25},{25,17},{2,10},{10... | collective-permute-start | bytes 1179656 | tf_op jit(solution)/shard_map/ppermute | solution.py:32
  22.3 34.7 %copy-start.4 = (bf16[12,8,2048]{2,1,0:T(8,128)(2,1)}, bf16[12,8,2048]{2,1,0:T(8,128)(2,1)S(1)}, u32[]{:S(2)}) copy-start(bf16[12,8,2048]{2,1,0:T(8,128)(2,1)S(1)} %constant_dynamic-update-slice_fusion.3.refs_9_) | copy-start | bytes 1179652
  22.5 10.0 %collective-permute-start.4 = (bf16[12,8,2048]{2,1,0:T(8,128)(2,1)S(1)}, bf16[12,8,2048]{2,1,0:T(8,128)(2,1)S(1)}, u32[]{:S(2)}, u32[]{:S(2)}) collective-permute-start(bf16[12,8,2048]{2,1,0:T(8,128)(2,1)S(1)} %pad_maximum_fusion.refs_0_), channel_id=1, source_target_pairs={{0,32},{32,0},{64,96},{96,64},{1,33},{33,1},{65,97},{97,65},{2,34}... | collective-permute-start | bytes 1179656 | tf_op jit(solution)/shard_map/ppermute | solution.py:32
  25.9 13.2 %collective-permute-start.16 = (bf16[12,8,2048]{2,1,0:T(8,128)(2,1)S(1)}, bf16[12,8,2048]{2,1,0:T(8,128)(2,1)S(1)}, u32[]{:S(2)}, u32[]{:S(2)}) collective-permute-start(bf16[12,8,2048]{2,1,0:T(8,128)(2,1)S(1)} %pad_maximum_fusion.1.refs_8_), channel_id=1, source_target_pairs={{0,24},{24,0},{8,16},{16,8},{1,25},{25,1},{9,17},{17,9},{2,26},{26... | collective-permute-start | bytes 1179656 | tf_op jit(solution)/shard_map/ppermute | solution.py:32
  27.0 30.0 %copy-start.3 = (bf16[12,8,2048]{2,1,0:T(8,128)(2,1)}, bf16[12,8,2048]{2,1,0:T(8,128)(2,1)S(1)}, u32[]{:S(2)}) copy-start(bf16[12,8,2048]{2,1,0:T(8,128)(2,1)S(1)} %constant_dynamic-update-slice_fusion.refs_1_) | copy-start | bytes 1179652
  27.0 13.1 %collective-permute-start.6 = (bf16[12,8,2048]{2,1,0:T(8,128)(2,1)S(1)}, bf16[12,8,2048]{2,1,0:T(8,128)(2,1)S(1)}, u32[]{:S(2)}, u32[]{:S(2)}) collective-permute-start(bf16[12,8,2048]{2,1,0:T(8,128)(2,1)S(1)} %pad_maximum_fusion.refs_0_), channel_id=1, source_target_pairs={{0,96},{96,0},{32,64},{64,32},{1,97},{97,1},{33,65},{65,33},{2,98}... | collective-permute-start | bytes 1179656 | tf_op jit(solution)/shard_map/ppermute | solution.py:32
  28.4 17.6 %collective-permute-start.17 = (bf16[12,8,2048]{2,1,0:T(8,128)(2,1)S(1)}, bf16[12,8,2048]{2,1,0:T(8,128)(2,1)S(1)}, u32[]{:S(2)}, u32[]{:S(2)}) collective-permute-start(bf16[12,8,2048]{2,1,0:T(8,128)(2,1)S(1)} %constant_dynamic-update-slice_fusion.3.refs_9_), channel_id=1, source_target_pairs={{0,24},{24,0},{8,16},{16,8},{1,25},{25,1},{9,17},{17,9},{2,26},{26... | collective-permute-start | bytes 1179656 | tf_op jit(solution)/shard_map/ppermute | solution.py:32
  31.2 25.8 %copy-start.5 = (bf16[12,8,2048]{2,1,0:T(8,128)(2,1)}, bf16[12,8,2048]{2,1,0:T(8,128)(2,1)S(1)}, u32[]{:S(2)}) copy-start(bf16[12,8,2048]{2,1,0:T(8,128)(2,1)S(1)} %collective-permute-done.14.refs_10_) | copy-start | bytes 1179652
  31.2 17.3 %collective-permute-start.7 = (bf16[12,8,2048]{2,1,0:T(8,128)(2,1)S(1)}, bf16[12,8,2048]{2,1,0:T(8,128)(2,1)S(1)}, u32[]{:S(2)}, u32[]{:S(2)}) collective-permute-start(bf16[12,8,2048]{2,1,0:T(8,128)(2,1)S(1)} %constant_dynamic-update-slice_fusion.refs_1_), channel_id=1, source_target_pairs={{0,96},{96,0},{32,64},{64,32},{1,97},{97,1},{33,65},{65,33},{2,98}... | collective-permute-start | bytes 1179656 | tf_op jit(solution)/shard_map/ppermute | solution.py:32
  32.5 24.6 %copy-start.6 = (bf16[12,8,2048]{2,1,0:T(8,128)(2,1)}, bf16[12,8,2048]{2,1,0:T(8,128)(2,1)S(1)}, u32[]{:S(2)}) copy-start(bf16[12,8,2048]{2,1,0:T(8,128)(2,1)S(1)} %collective-permute-done.4.refs_2_) | copy-start | bytes 1179652
  32.5 16.8 %collective-permute-start.15 = (bf16[12,8,2048]{2,1,0:T(8,128)(2,1)S(1)}, bf16[12,8,2048]{2,1,0:T(8,128)(2,1)S(1)}, u32[]{:S(2)}, u32[]{:S(2)}) collective-permute-start(bf16[12,8,2048]{2,1,0:T(8,128)(2,1)S(1)} %constant_dynamic-update-slice_fusion.3.refs_9_), channel_id=1, source_target_pairs={{0,8},{8,0},{16,24},{24,16},{1,9},{9,1},{17,25},{25,17},{2,10},{10... | collective-permute-start | bytes 1179656 | tf_op jit(solution)/shard_map/ppermute | solution.py:32
  39.1 18.0 %copy-start.7 = (bf16[12,8,2048]{2,1,0:T(8,128)(2,1)}, bf16[12,8,2048]{2,1,0:T(8,128)(2,1)S(1)}, u32[]{:S(2)}) copy-start(bf16[12,8,2048]{2,1,0:T(8,128)(2,1)S(1)} %collective-permute-done.16.refs_12_) | copy-start | bytes 1179652
  39.1 11.0 %collective-permute-start.5 = (bf16[12,8,2048]{2,1,0:T(8,128)(2,1)S(1)}, bf16[12,8,2048]{2,1,0:T(8,128)(2,1)S(1)}, u32[]{:S(2)}, u32[]{:S(2)}) collective-permute-start(bf16[12,8,2048]{2,1,0:T(8,128)(2,1)S(1)} %constant_dynamic-update-slice_fusion.refs_1_), channel_id=1, source_target_pairs={{0,32},{32,0},{64,96},{96,64},{1,33},{33,1},{65,97},{97,65},{2,34}... | collective-permute-start | bytes 1179656 | tf_op jit(solution)/shard_map/ppermute | solution.py:32
  40.1 17.0 %copy-start.8 = (bf16[12,8,2048]{2,1,0:T(8,128)(2,1)}, bf16[12,8,2048]{2,1,0:T(8,128)(2,1)S(1)}, u32[]{:S(2)}) copy-start(bf16[12,8,2048]{2,1,0:T(8,128)(2,1)S(1)} %collective-permute-done.6.refs_4_) | copy-start | bytes 1179652
  40.1 10.0 %collective-permute-start.18 = (bf16[12,8,2048]{2,1,0:T(8,128)(2,1)S(1)}, bf16[12,8,2048]{2,1,0:T(8,128)(2,1)S(1)}, u32[]{:S(2)}, u32[]{:S(2)}) collective-permute-start(bf16[12,8,2048]{2,1,0:T(8,128)(2,1)S(1)} %collective-permute-done.14.refs_10_), channel_id=1, source_target_pairs={{0,24},{24,0},{8,16},{16,8},{1,25},{25,1},{9,17},{17,9},{2,26},{26... | collective-permute-start | bytes 1179656 | tf_op jit(solution)/shard_map/ppermute | solution.py:32
  45.9 11.1 %copy-start.9 = (bf16[12,8,2048]{2,1,0:T(8,128)(2,1)}, bf16[12,8,2048]{2,1,0:T(8,128)(2,1)S(1)}, u32[]{:S(2)}) copy-start(bf16[12,8,2048]{2,1,0:T(8,128)(2,1)S(1)} %collective-permute-done.17.refs_13_) | copy-start | bytes 1179652
  45.9 9.0 %collective-permute-start.8 = (bf16[12,8,2048]{2,1,0:T(8,128)(2,1)S(1)}, bf16[12,8,2048]{2,1,0:T(8,128)(2,1)S(1)}, u32[]{:S(2)}, u32[]{:S(2)}) collective-permute-start(bf16[12,8,2048]{2,1,0:T(8,128)(2,1)S(1)} %collective-permute-done.4.refs_2_), channel_id=1, source_target_pairs={{0,96},{96,0},{32,64},{64,32},{1,97},{97,1},{33,65},{65,33},{2,98}... | collective-permute-start | bytes 1179656 | tf_op jit(solution)/shard_map/ppermute | solution.py:32
  48.6 8.5 %copy-start.10 = (bf16[12,8,2048]{2,1,0:T(8,128)(2,1)}, bf16[12,8,2048]{2,1,0:T(8,128)(2,1)S(1)}, u32[]{:S(2)}) copy-start(bf16[12,8,2048]{2,1,0:T(8,128)(2,1)S(1)} %collective-permute-done.7.refs_5_) | copy-start | bytes 1179652
  48.6 7.8 %collective-permute-start.19 = (bf16[12,8,2048]{2,1,0:T(8,128)(2,1)S(1)}, bf16[12,8,2048]{2,1,0:T(8,128)(2,1)S(1)}, u32[]{:S(2)}, u32[]{:S(2)}) collective-permute-start(bf16[12,8,2048]{2,1,0:T(8,128)(2,1)S(1)} %collective-permute-done.17.refs_13_), channel_id=1, source_target_pairs={{0,8},{8,0},{16,24},{24,16},{1,9},{9,1},{17,25},{25,17},{2,10},{10... | collective-permute-start | bytes 1179656 | tf_op jit(solution)/shard_map/ppermute | solution.py:32
  49.3 7.9 %copy-start.11 = (bf16[12,8,2048]{2,1,0:T(8,128)(2,1)}, bf16[12,8,2048]{2,1,0:T(8,128)(2,1)S(1)}, u32[]{:S(2)}) copy-start(bf16[12,8,2048]{2,1,0:T(8,128)(2,1)S(1)} %collective-permute-done.15.refs_11_) | copy-start | bytes 1179652
  49.3 7.8 %collective-permute-start.9 = (bf16[12,8,2048]{2,1,0:T(8,128)(2,1)S(1)}, bf16[12,8,2048]{2,1,0:T(8,128)(2,1)S(1)}, u32[]{:S(2)}, u32[]{:S(2)}) collective-permute-start(bf16[12,8,2048]{2,1,0:T(8,128)(2,1)S(1)} %collective-permute-done.7.refs_5_), channel_id=1, source_target_pairs={{0,32},{32,0},{64,96},{96,64},{1,33},{33,1},{65,97},{97,65},{2,34}... | collective-permute-start | bytes 1179656 | tf_op jit(solution)/shard_map/ppermute | solution.py:32
  50.1 7.0 %copy-start.12 = (bf16[12,8,2048]{2,1,0:T(8,128)(2,1)}, bf16[12,8,2048]{2,1,0:T(8,128)(2,1)S(1)}, u32[]{:S(2)}) copy-start(bf16[12,8,2048]{2,1,0:T(8,128)(2,1)S(1)} %collective-permute-done.5.refs_3_) | copy-start | bytes 1179652
  50.2 7.0 %copy-start.13 = (bf16[12,8,2048]{2,1,0:T(8,128)(2,1)}, bf16[12,8,2048]{2,1,0:T(8,128)(2,1)S(1)}, u32[]{:S(2)}) copy-start(bf16[12,8,2048]{2,1,0:T(8,128)(2,1)S(1)} %collective-permute-done.18.refs_14_) | copy-start | bytes 1179652
  54.9 2.2 %copy-start.14 = (bf16[12,8,2048]{2,1,0:T(8,128)(2,1)}, bf16[12,8,2048]{2,1,0:T(8,128)(2,1)S(1)}, u32[]{:S(2)}) copy-start(bf16[12,8,2048]{2,1,0:T(8,128)(2,1)S(1)} %collective-permute-done.8.refs_6_) | copy-start | bytes 1179652
  56.3 0.8 copy-start.15
  57.0 0.7 copy-start.16
  66.2 15.2 %collective-permute-start.24 = (bf16[15,16,128]{2,1,0:T(8,128)(2,1)S(1)}, bf16[15,16,128]{2,1,0:T(8,128)(2,1)S(1)}, u32[]{:S(2)}, u32[]{:S(2)}) collective-permute-start(bf16[15,16,128]{2,1,0:T(8,128)(2,1)S(1)} %get-tuple-element.18), channel_id=1, source_target_pairs={{0,3},{1,4},{2,5},{3,6},{4,7},{5,0},{6,1},{7,2},{8,11},{9,12},{10,... | collective-permute-start | bytes 184328 | tf_op jit(solution)/shard_map/ppermute | solution.py:21
  73.3 8.0 %collective-permute-start.26 = (bf16[5,16,128]{2,1,0:T(8,128)(2,1)S(1)}, bf16[5,16,128]{2,1,0:T(8,128)(2,1)S(1)}, u32[]{:S(2)}, u32[]{:S(2)}) collective-permute-start(bf16[5,16,128]{2,1,0:T(8,128)(2,1)S(1)} %get-tuple-element.20.refs_9_), channel_id=1, source_target_pairs={{0,4},{1,5},{2,6},{3,7},{4,0},{5,1},{6,2},{7,3},{8,12},{9,13},{10,... | collective-permute-start | bytes 61448 | tf_op jit(solution)/shard_map/ppermute | solution.py:21
  74.0 15.7 %collective-permute-start.20 = (bf16[23,16,128]{2,1,0:T(8,128)(2,1)S(1)}, bf16[23,16,128]{2,1,0:T(8,128)(2,1)S(1)}, u32[]{:S(2)}, u32[]{:S(2)}) collective-permute-start(bf16[23,16,128]{2,1,0:T(8,128)(2,1)S(1)} %get-tuple-element.14.refs_7_), channel_id=1, source_target_pairs={{0,1},{1,2},{2,3},{3,4},{4,5},{5,6},{6,7},{7,0},{8,9},{9,10},{10,1... | collective-permute-start | bytes 282632 | tf_op jit(solution)/shard_map/ppermute | solution.py:21
  74.4 15.4 %collective-permute-start.21 = (bf16[23,16,128]{2,1,0:T(8,128)(2,1)S(1)}, bf16[23,16,128]{2,1,0:T(8,128)(2,1)S(1)}, u32[]{:S(2)}, u32[]{:S(2)}) collective-permute-start(bf16[23,16,128]{2,1,0:T(8,128)(2,1)S(1)} %get-tuple-element.15.refs_8_), channel_id=1, source_target_pairs={{0,7},{1,0},{2,1},{3,2},{4,3},{5,4},{6,5},{7,6},{8,15},{9,8},{10,9... | collective-permute-start | bytes 282632 | tf_op jit(solution)/shard_map/ppermute | solution.py:21
  76.2 13.5 %collective-permute-start.22 = (bf16[17,16,128]{2,1,0:T(8,128)(2,1)S(1)}, bf16[17,16,128]{2,1,0:T(8,128)(2,1)S(1)}, u32[]{:S(2)}, u32[]{:S(2)}) collective-permute-start(bf16[17,16,128]{2,1,0:T(8,128)(2,1)S(1)} %get-tuple-element.16), channel_id=1, source_target_pairs={{0,2},{1,3},{2,4},{3,5},{4,6},{5,7},{6,0},{7,1},{8,10},{9,11},{10,... | collective-permute-start | bytes 208904 | tf_op jit(solution)/shard_map/ppermute | solution.py:21
  81.4 8.4 %collective-permute-start.23 = (bf16[17,16,128]{2,1,0:T(8,128)(2,1)S(1)}, bf16[17,16,128]{2,1,0:T(8,128)(2,1)S(1)}, u32[]{:S(2)}, u32[]{:S(2)}) collective-permute-start(bf16[17,16,128]{2,1,0:T(8,128)(2,1)S(1)} %get-tuple-element.17), channel_id=1, source_target_pairs={{0,6},{1,7},{2,0},{3,1},{4,2},{5,3},{6,4},{7,5},{8,14},{9,15},{10,... | collective-permute-start | bytes 208904 | tf_op jit(solution)/shard_map/ppermute | solution.py:21
  81.4 8.3 %collective-permute-start.25 = (bf16[15,16,128]{2,1,0:T(8,128)(2,1)S(1)}, bf16[15,16,128]{2,1,0:T(8,128)(2,1)S(1)}, u32[]{:S(2)}, u32[]{:S(2)}) collective-permute-start(bf16[15,16,128]{2,1,0:T(8,128)(2,1)S(1)} %get-tuple-element.19), channel_id=1, source_target_pairs={{0,5},{1,6},{2,7},{3,0},{4,1},{5,2},{6,3},{7,4},{8,13},{9,14},{10,... | collective-permute-start | bytes 184328 | tf_op jit(solution)/shard_map/ppermute | solution.py:21
  91.7 14.0 %all-to-all-start = ((bf16[16,136,128]{2,1,0:T(8,128)(2,1)}), bf16[16,136,128]{2,1,0:T(8,128)(2,1)S(1)}, u32[]{:S(2)}, u32[]{:S(2)}) async-start(bf16[16,136,128]{2,1,0:T(8,128)(2,1)} %branches.1), calls=%async_computation | async-start | bytes 1114112 | tf_op jit(solution)/shard_map/all_to_all | solution.py:476

commit v5 on v4

--- a/solution.py
+++ b/solution.py
@@ -1,3 +1,5 @@
+import functools
+
 import jax
 import jax.numpy as jnp
 from jax import lax
@@ -13,7 +15,7 @@
 MAP_COLS = 96
 BF = jnp.bfloat16
 F32 = jnp.float32
-VMEM_BYTES = 56 * 1024 * 1024
+VMEM_BYTES = 32 * 1024 * 1024
 
 
 def around(value, axis, by):
@@ -67,9 +69,9 @@
 
 LOW = ((0, 6, 0, OWN), (6, 6, 0, NEAR))
 HIGH = ((0, 6, 0, WRAP), (6, 3, 0, FAR), (9, 3, 3, FAR))
-PIECES = [
+EARLY = [
     (2 * which + part, *piece, kind)
-    for which, kind in enumerate((OWN, NEAR, WRAP, FAR))
+    for which, kind in enumerate((OWN, NEAR, WRAP))
     for part, pieces in enumerate((LOW, HIGH))
     for piece in pieces
 ]
@@ -77,35 +79,98 @@
 SLOT = 136
 
 
-def products_kernel(*refs):
-    refs = (None, *refs)
-    parts = (refs[1:9], refs[9:17])
-    atrous, point, pool = refs[17:20]
-    centre = refs[20]
-    sides = refs[21:27]
-    opposite = refs[27]
-    feats, weights, total, feat_sems, weight_sems = refs[28:33]
+def weight_copies(atrous, point, pool, weights, sems):
+    return [
+        pltpu.make_async_copy(atrous, weights.at[pl.ds(0, 432)], sems.at[0]),
+        pltpu.make_async_copy(point, weights.at[pl.ds(432, 16)], sems.at[1]),
+        pltpu.make_async_copy(pool, weights.at[pl.ds(448, 16)], sems.at[2]),
+    ]
+
+
+def transposed_dot(weights, block):
+    return lax.dot_general(
+        weights, block, (((1,), (1,)), ((), ())), preferred_element_type=F32
+    )
+
+
+def early_kernel(*refs):
+    parts = (refs[0:6], refs[6:12])
+    atrous, point, pool, out, feats, weights, feat_sems, weight_sems = refs[12:20]
     own_y, own_x = lax.axis_index("row_0"), lax.axis_index("row_1")
     copies = []
     for colour in range(2):
         group = []
-        for number, (which, start, count, col, first, second) in enumerate(PIECES):
+        for number, (which, start, count, col, first, second) in enumerate(EARLY):
             kind_y, kind_x = (second, first) if colour == 0 else (first, second)
             tile = position(own_y, kind_y) * 4 + position(own_x, kind_x)
             group.append(
                 pltpu.make_async_copy(
                     parts[colour][which].at[pl.ds(start, count)],
                     feats.at[pl.ds(6 * colour + col, count), tile],
-                    feat_sems.at[colour * len(PIECES) + number],
+                    feat_sems.at[colour * len(EARLY) + number],
                 )
             )
         copies.append(group)
-    loads = [
-        pltpu.make_async_copy(atrous, weights.at[pl.ds(0, 432)], weight_sems.at[0]),
-        pltpu.make_async_copy(point, weights.at[pl.ds(432, 16)], weight_sems.at[1]),
-        pltpu.make_async_copy(pool, weights.at[pl.ds(448, 16)], weight_sems.at[2]),
-    ]
+    loads = weight_copies(atrous, point, pool, weights, weight_sems)
     for copy in loads + copies[0] + copies[1]:
+        copy.start()
+    zeros = jnp.zeros((6, 8, feats.shape[-1]), BF)
+    for other in range(4):
+        feats[0:6, position(own_y, FAR) * 4 + other] = zeros
+        feats[6:12, other * 4 + position(own_x, FAR)] = zeros
+
+    def pair(index, carry):
+        block = feats[pl.ds(2 * index, 2)].reshape(2 * MAP_ROWS, feats.shape[-1])
+        out[index] = transposed_dot(weights[...], block)
+        return carry
+
+    for copy in loads + copies[0]:
+        copy.wait()
+    lax.fori_loop(0, 3, pair, 0)
+    for copy in copies[1]:
+        copy.wait()
+    lax.fori_loop(3, 6, pair, 0)
+
+
+def early_products(pieces, atrous, point, pool):
+    depth = atrous.shape[1]
+    anywhere = pl.BlockSpec(memory_space=pl.ANY)
+    return pl.pallas_call(
+        early_kernel,
+        out_shape=pltpu.VMEM((6, 464, 256), F32),
+        in_specs=[anywhere] * 15,
+        scratch_shapes=[
+            pltpu.VMEM((12, 16, 8, depth), BF),
+            pltpu.VMEM((464, depth), BF),
+            pltpu.SemaphoreType.DMA((2 * len(EARLY),)),
+            pltpu.SemaphoreType.DMA((3,)),
+        ],
+        compiler_params=pltpu.CompilerParams(vmem_limit_bytes=VMEM_BYTES),
+        name="early",
+    )(*pieces, atrous, point, pool)
+
+
+def products_kernel(*refs):
+    early, low_a, high_a, low_b, high_b, atrous, point, pool = refs[0:8]
+    centre = refs[8]
+    sides = refs[9:15]
+    opposite = refs[15]
+    feats, weights, total, far, feat_sems, weight_sems = refs[16:22]
+    own_y, own_x = lax.axis_index("row_0"), lax.axis_index("row_1")
+    far_y, far_x = position(own_y, FAR), position(own_x, FAR)
+    copies = []
+    for colour, (own, received) in enumerate(((own_x, (low_a, high_a)), (own_y, (low_b, high_b)))):
+        for part, pieces in enumerate((LOW, HIGH)):
+            for start, count, col, kind in pieces:
+                copies.append(
+                    pltpu.make_async_copy(
+                        received[part].at[pl.ds(start, count)],
+                        feats.at[colour, pl.ds(col, count), position(own, kind)],
+                        feat_sems.at[len(copies)],
+                    )
+                )
+    copies += weight_copies(atrous, point, pool, weights, weight_sems)
+    for copy in copies:
         copy.start()
     total[...] = jnp.zeros_like(total)
     lane = lax.broadcasted_iota(jnp.int32, (16, MAP_ROWS), 1)
@@ -117,14 +182,23 @@
         inside = (lane + offset >= 0) & (lane + offset < MAP_ROWS)
         return jnp.where(inside, moved, 0.0)
 
-    def pair(index, carry):
-        block = feats[pl.ds(2 * index, 2)].reshape(2 * MAP_ROWS, feats.shape[-1])
-        result = lax.dot_general(
-            weights[...], block, (((1,), (1,)), ((), ())), preferred_element_type=F32
-        )
+    at = lax.broadcasted_iota(jnp.int32, (464, MAP_ROWS), 1)
+
+    def merged(colour, inner, columns):
+        chunk = far[colour, :, pl.ds(pl.multiple_of(128 * (inner // 4), 128), 128)]
+        if colour == 0:
+            moved = pltpu.roll(chunk, (32 * far_y - 32 * inner + 256) % 128, 1)
+            return jnp.where((at >> 5) == far_y, moved, columns)
+        for band in range(4):
+            moved = pltpu.roll(chunk, (24 * band + 8 * far_x - 32 * inner + 256) % 128, 1)
+            columns = jnp.where((at >> 3) == 4 * band + far_x, moved, columns)
+        return columns
+
+    def pair(index, carry, colour):
         for side in range(2):
             col = 2 * index + side
-            columns = result[:, side * MAP_ROWS : (side + 1) * MAP_ROWS]
+            columns = early[index, :, side * MAP_ROWS : (side + 1) * MAP_ROWS]
+            columns = merged(colour, col - 6 * colour, columns)
 
             def group(number, columns=columns):
                 return columns[number * 16 : (number + 1) * 16]
@@ -142,12 +216,13 @@
             total[...] += group(28)
         return carry
 
-    for copy in loads + copies[0]:
+    for copy in copies:
         copy.wait()
-    lax.fori_loop(0, 3, pair, 0)
-    for copy in copies[1]:
-        copy.wait()
-    lax.fori_loop(3, 6, pair, 0)
+    for colour in range(2):
+        block = feats[colour].reshape(192, feats.shape[-1])
+        far[colour, :, 0:192] = transposed_dot(weights[...], block)
+    for colour in range(2):
+        lax.fori_loop(3 * colour, 3 * colour + 3, functools.partial(pair, colour=colour), 0)
     strip = jnp.sum(total[...], axis=1, keepdims=True)
     high = strip.astype(BF).astype(F32)
     middle = (strip - high).astype(BF).astype(F32)
@@ -172,7 +247,7 @@
             opposite[2 - 2 * way + edge] = far[there]
 
 
-def products(pieces, atrous, point, pool):
+def products(early, pieces, atrous, point, pool):
     depth = atrous.shape[1]
     sides = [pltpu.VMEM((size, 16, MAP_ROWS), BF) for size in SIZES for _ in range(2)]
     anywhere = pl.BlockSpec(memory_space=pl.ANY)
@@ -181,17 +256,18 @@
         out_shape=[pltpu.VMEM((12, 64, MAP_ROWS), F32)]
         + sides
         + [pltpu.VMEM((5, 16, MAP_ROWS), BF)],
-        in_specs=[anywhere] * 19,
+        in_specs=[pl.BlockSpec(memory_space=pltpu.VMEM)] + [anywhere] * 7,
         scratch_shapes=[
-            pltpu.VMEM((12, 16, 8, depth), BF),
+            pltpu.VMEM((2, 6, 4, 8, depth), BF),
             pltpu.VMEM((464, depth), BF),
             pltpu.VMEM((16, MAP_ROWS), F32),
-            pltpu.SemaphoreType.DMA((2 * len(PIECES),)),
+            pltpu.VMEM((2, 464, 256), F32),
+            pltpu.SemaphoreType.DMA((2 * (len(LOW) + len(HIGH)),)),
             pltpu.SemaphoreType.DMA((3,)),
         ],
         compiler_params=pltpu.CompilerParams(vmem_limit_bytes=VMEM_BYTES),
         name="products",
-    )(*pieces, atrous, point, pool)
+    )(on_chip(early), *pieces, atrous, point, pool)
 
 
 def branches_kernel(centre, *refs):
@@ -387,7 +463,7 @@
             pltpu.VMEM((40, 128), F32),
             pltpu.SemaphoreType.DMA((7,)),
         ],
-        compiler_params=pltpu.CompilerParams(vmem_limit_bytes=VMEM_BYTES),
+        compiler_params=pltpu.CompilerParams(vmem_limit_bytes=56 * 1024 * 1024),
         name="decode",
     )(on_chip(received), proj, bias, on_chip(spread), on_chip(low), w1, b1, w2, b2)
 
@@ -460,11 +536,14 @@
     after = next_to(reduced[:, 0:2], "col", -1)
     wide = jnp.concatenate([before, reduced, after], axis=1)
     low, top, bottom = low_columns(wide), border(wide[0:2]), border(wide[14:16])
-    pieces = gather_strip(tile[:6], "row_1", "row_0")
-    pieces += gather_strip(tile[6:], "row_0", "row_1")
+    pieces_a = gather_strip(tile[:6], "row_1", "row_0")
+    pieces_b = gather_strip(tile[6:], "row_0", "row_1")
     spread = spread_matrix()
     atrous = jnp.transpose(atrous_weight, (0, 1, 2, 4, 3)).reshape(432, in_width)
-    centre, *sides, opposite = products(pieces, atrous, point_weight.T, pool_weight.T)
+    point, pool = point_weight.T, pool_weight.T
+    early = early_products(pieces_a[:6] + pieces_b[:6], atrous, point, pool)
+    late = pieces_a[6:] + pieces_b[6:]
+    centre, *sides, opposite = products(early, late, atrous, point, pool)
     moved = []
     for rate in range(3):
         moved.append(around(sides[2 * rate], "col", rate + 1))

time: 114 us -> 110 us (0.965)
  waiting for transfers between devices: 44.3 us -> 38.2 us
  Pallas kernels: 17.7 us -> 20.6 us
  starting transfers between devices: 45.3 us -> 47.1 us
  other arithmetic: 1.75 us -> 0.56 us
    ppermute x20, waiting for transfers between devices: 25.7 us -> 19 us  [swap(): lax.ppermute(value, axis, [way for a, b in pairs for way in ((a, b), (b,...]
    pallas_call x0 -> x1, Pallas kernels: none -> 6.62 us  [early_products(): pl.pallas_call(early_kernel, out_shape=pltpu.VMEM((6, 464, 256), F32), in...]
    pallas_call x1, Pallas kernels: 8.44 us -> 5.44 us  [products(): pl.pallas_call(products_kernel, out_shape=[pltpu.VMEM((12, 64, MAP_ROWS),...]
    all_to_all x1, starting transfers between devices: 3.7 us -> 5.04 us  [on_device(): lax.all_to_all(mine, ROW, split_axis=0, concat_axis=0, tiled=True)]
    concatenate x2, other arithmetic: 1.35 us -> 0.16 us  [border(): return jnp.concatenate([padded[0], padded[1]], axis=1)]
  transfers between devices with their start and end apart: 30 -> 30, of which waited for: 16 -> 13; matrix products, arithmetic and copies ran while one was open for 3% -> 2% of each run, Pallas kernels for 1% -> 7%
where the time goes in v5:
time: 110 us; the launch traced here: 109 us
  starting transfers between devices  47.1 us (43%)
  waiting for transfers between devices  38.2 us (35%)
  Pallas kernels  20.6 us (19%)
  local copies, waits for them, and re-layouts  1.51 us (1%)
    ppermute x20, starting transfers between devices, swap(): lax.ppermute(value, axis, [way for a, b in pairs for way in ((a, b), (b,...  22.9 us
    ppermute x20, waiting for transfers between devices, swap(): lax.ppermute(value, axis, [way for a, b in pairs for way in ((a, b), (b,...  19 us
    ppermute x7, starting transfers between devices, around(): lax.ppermute(value, axis, [(i, (i + by) % devices) for i in range(devices)])  13.3 us
    ppermute x7, waiting for transfers between devices, around(): lax.ppermute(value, axis, [(i, (i + by) % devices) for i in range(devices)])  9.91 us
    all_to_all x1, waiting for transfers between devices, on_device(): lax.all_to_all(mine, ROW, split_axis=0, concat_axis=0, tiled=True)  9.26 us
    pallas_call x1, Pallas kernels, decode(): pl.pallas_call(decode_kernel, out_shape=jax.ShapeDtypeStruct((16, 24, 256...  6.69 us
    pallas_call x1, Pallas kernels, early_products(): pl.pallas_call(early_kernel, out_shape=pltpu.VMEM((6, 464, 256), F32), in...  6.62 us
    ppermute x2, starting transfers between devices, next_to(): return lax.ppermute(value, axis, pairs)  5.84 us
  transfers between devices with their start and end apart: 30, of which 13 were waited for; matrix products, arithmetic and copies ran while one was open for 2% of the time, Pallas kernels for 7%

profile of v5, /device:TPU:32, one launch (start us, length us, event | category | flops | bytes accessed | tf_op | source)
XLA Modules:
  0.0 109.3 jit_solution(4297523833871437555)
XLA Ops:
  0.0 1.1 fusion.6
  1.1 3.1 %collective-permute-start.9 = (bf16[6,8,2048]{2,1,0:T(8,128)(2,1)S(1)}, bf16[6,8,2048]{2,1,0:T(8,128)(2,1)S(1)}, u32[]{:S(2)}, u32[]{:S(2)}) collective-permute-start(bf16[6,8,2048]{2,1,0:T(8,128)(2,1)S(1)} %get-tuple-element.21), channel_id=1, source_target_pairs={{0,96},{96,0},{32,64},{64,32},{1,97},{97,1},{33,65},{65,33},{2,98}... | collective-permute-start | bytes 589832 | tf_op jit(solution)/shard_map/ppermute | solution.py:34
  4.2 0.1 collective-permute-start.8
  4.3 2.8 %collective-permute-start.1 = (bf16[6,8,2048]{2,1,0:T(8,128)(2,1)S(1)}, bf16[6,8,2048]{2,1,0:T(8,128)(2,1)S(1)}, u32[]{:S(2)}, u32[]{:S(2)}) collective-permute-start(bf16[6,8,2048]{2,1,0:T(8,128)(2,1)S(1)} %get-tuple-element.22), channel_id=1, source_target_pairs={{0,24},{24,0},{8,16},{16,8},{1,25},{25,1},{9,17},{17,9},{2,26},{26... | collective-permute-start | bytes 589832 | tf_op jit(solution)/shard_map/ppermute | solution.py:34
  7.1 0.2 collective-permute-start
  7.3 0.9 fusion.1
  8.3 0.1 copy.15
  8.4 3.8 %collective-permute-start.27 = (bf16[16,2,48]{2,1,0:T(2,128)(2,1)S(1)}, bf16[16,2,48]{2,1,0:T(2,128)(2,1)S(1)}, u32[]{:S(2)}, u32[]{:S(2)}) collective-permute-start(bf16[16,2,48]{2,1,0:T(2,128)(2,1)S(1)} %get-tuple-element.27), channel_id=1, source_target_pairs={{0,1},{1,2},{2,3},{3,4},{4,5},{5,6},{6,7},{8,9},{9,10},{10,11},{11... | collective-permute-start | bytes 9224 | tf_op jit(solution)/shard_map/ppermute | solution.py:29
  12.2 0.0 collective-permute-done.8
  12.2 2.0 %collective-permute-start.28 = (bf16[16,2,48]{2,1,0:T(2,128)(2,1)S(1)}, bf16[16,2,48]{2,1,0:T(2,128)(2,1)S(1)}, u32[]{:S(2)}, u32[]{:S(2)}) collective-permute-start(bf16[16,2,48]{2,1,0:T(2,128)(2,1)S(1)} %get-tuple-element.28), channel_id=1, source_target_pairs={{1,0},{2,1},{3,2},{4,3},{5,4},{6,5},{7,6},{9,8},{10,9},{11,10},{12... | collective-permute-start | bytes 9224 | tf_op jit(solution)/shard_map/ppermute | solution.py:29
  14.3 0.0 collective-permute-done.9
  14.3 1.1 %collective-permute-start.10 = (bf16[3,8,2048]{2,1,0:T(8,128)(2,1)S(1)}, bf16[3,8,2048]{2,1,0:T(8,128)(2,1)S(1)}, u32[]{:S(2)}, u32[]{:S(2)}) collective-permute-start(bf16[3,8,2048]{2,1,0:T(8,128)(2,1)S(1)} %slice.76), channel_id=1, source_target_pairs={{0,96},{96,0},{32,64},{64,32},{1,97},{97,1},{33,65},{65,33},{2,98}... | collective-permute-start | bytes 294920 | tf_op jit(solution)/shard_map/ppermute | solution.py:34
  15.5 0.0 copy-start.2
  15.5 0.0 copy-start.3
  15.5 0.0 collective-permute-done
  15.5 0.9 collective-permute-start.11
  16.6 1.2 %collective-permute-start.2 = (bf16[3,8,2048]{2,1,0:T(8,128)(2,1)S(1)}, bf16[3,8,2048]{2,1,0:T(8,128)(2,1)S(1)}, u32[]{:S(2)}, u32[]{:S(2)}) collective-permute-start(bf16[3,8,2048]{2,1,0:T(8,128)(2,1)S(1)} %slice.73), channel_id=1, source_target_pairs={{0,24},{24,0},{8,16},{16,8},{1,25},{25,1},{9,17},{17,9},{2,26},{26... | collective-permute-start | bytes 294920 | tf_op jit(solution)/shard_map/ppermute | solution.py:34
  17.8 2.4 %collective-permute-done.10 = bf16[3,8,2048]{2,1,0:T(8,128)(2,1)S(1)} collective-permute-done((bf16[3,8,2048]{2,1,0:T(8,128)(2,1)S(1)}, bf16[3,8,2048]{2,1,0:T(8,128)(2,1)S(1)}, u32[]{:S(2)}, u32[]{:S(2)}) %collective-permute-start.10) | collective-permute-done | bytes 98336 | tf_op jit(solution)/shard_map/ppermute | solution.py:34
  20.2 1.8 %collective-permute-start.3 = (bf16[3,8,2048]{2,1,0:T(8,128)(2,1)S(1)}, bf16[3,8,2048]{2,1,0:T(8,128)(2,1)S(1)}, u32[]{:S(2)}, u32[]{:S(2)}) collective-permute-start(bf16[3,8,2048]{2,1,0:T(8,128)(2,1)S(1)} %slice.74), channel_id=1, source_target_pairs={{0,8},{8,0},{16,24},{24,16},{1,9},{9,1},{17,25},{25,17},{2,10},{10... | collective-permute-start | bytes 294920 | tf_op jit(solution)/shard_map/ppermute | solution.py:34
  22.0 0.3 collective-permute-start.12
  22.3 0.1 collective-permute-done.2
  22.5 1.2 %collective-permute-start.4 = (bf16[12,8,2048]{2,1,0:T(8,128)(2,1)S(1)}, bf16[12,8,2048]{2,1,0:T(8,128)(2,1)S(1)}, u32[]{:S(2)}, u32[]{:S(2)}) collective-permute-start(bf16[12,8,2048]{2,1,0:T(8,128)(2,1)S(1)} %pad_maximum_fusion.refs_0_), channel_id=1, source_target_pairs={{0,32},{32,0},{64,96},{96,64},{1,33},{33,1},{65,97},{97,65},{2,34}... | collective-permute-start | bytes 1179656 | tf_op jit(solution)/shard_map/ppermute | solution.py:34
  23.7 2.2 %collective-permute-done.3 = bf16[3,8,2048]{2,1,0:T(8,128)(2,1)S(1)} collective-permute-done((bf16[3,8,2048]{2,1,0:T(8,128)(2,1)S(1)}, bf16[3,8,2048]{2,1,0:T(8,128)(2,1)S(1)}, u32[]{:S(2)}, u32[]{:S(2)}) %collective-permute-start.3) | collective-permute-done | bytes 98336 | tf_op jit(solution)/shard_map/ppermute | solution.py:34
  25.9 1.1 %collective-permute-start.14 = (bf16[12,8,2048]{2,1,0:T(8,128)(2,1)S(1)}, bf16[12,8,2048]{2,1,0:T(8,128)(2,1)S(1)}, u32[]{:S(2)}, u32[]{:S(2)}) collective-permute-start(bf16[12,8,2048]{2,1,0:T(8,128)(2,1)S(1)} %pad_maximum_fusion.1.refs_6_), channel_id=1, source_target_pairs={{0,24},{24,0},{8,16},{16,8},{1,25},{25,1},{9,17},{17,9},{2,26},{26... | collective-permute-start | bytes 1179656 | tf_op jit(solution)/shard_map/ppermute | solution.py:34
  27.0 0.0 collective-permute-done.27
  27.0 1.4 %collective-permute-start.6 = (bf16[12,8,2048]{2,1,0:T(8,128)(2,1)S(1)}, bf16[12,8,2048]{2,1,0:T(8,128)(2,1)S(1)}, u32[]{:S(2)}, u32[]{:S(2)}) collective-permute-start(bf16[12,8,2048]{2,1,0:T(8,128)(2,1)S(1)} %pad_maximum_fusion.refs_0_), channel_id=1, source_target_pairs={{0,96},{96,0},{32,64},{64,32},{1,97},{97,1},{33,65},{65,33},{2,98}... | collective-permute-start | bytes 1179656 | tf_op jit(solution)/shard_map/ppermute | solution.py:34
  28.4 1.9 %collective-permute-start.15 = (bf16[12,8,2048]{2,1,0:T(8,128)(2,1)S(1)}, bf16[12,8,2048]{2,1,0:T(8,128)(2,1)S(1)}, u32[]{:S(2)}, u32[]{:S(2)}) collective-permute-start(bf16[12,8,2048]{2,1,0:T(8,128)(2,1)S(1)} %constant_dynamic-update-slice_fusion.3.refs_7_), channel_id=1, source_target_pairs={{0,24},{24,0},{8,16},{16,8},{1,25},{25,1},{9,17},{17,9},{2,26},{26... | collective-permute-start | bytes 1179656 | tf_op jit(solution)/shard_map/ppermute | solution.py:34
  30.3 1.0 collective-permute-done.12.refs_8_
  31.2 1.2 %collective-permute-start.7 = (bf16[12,8,2048]{2,1,0:T(8,128)(2,1)S(1)}, bf16[12,8,2048]{2,1,0:T(8,128)(2,1)S(1)}, u32[]{:S(2)}, u32[]{:S(2)}) collective-permute-start(bf16[12,8,2048]{2,1,0:T(8,128)(2,1)S(1)} %constant_dynamic-update-slice_fusion.refs_1_), channel_id=1, source_target_pairs={{0,96},{96,0},{32,64},{64,32},{1,97},{97,1},{33,65},{65,33},{2,98}... | collective-permute-start | bytes 1179656 | tf_op jit(solution)/shard_map/ppermute | solution.py:34
  32.5 0.0 collective-permute-done.4.refs_2_
  32.5 0.9 collective-permute-start.13
  33.4 5.7 %collective-permute-done.14.refs_10_ = bf16[12,8,2048]{2,1,0:T(8,128)(2,1)S(1)} collective-permute-done((bf16[12,8,2048]{2,1,0:T(8,128)(2,1)S(1)}, bf16[12,8,2048]{2,1,0:T(8,128)(2,1)S(1)}, u32[]{:S(2)}, u32[]{:S(2)}) %collective-permute-start.14) | collective-permute-done | bytes 393248 | tf_op jit(solution)/shard_map/ppermute | solution.py:34
  39.1 0.7 collective-permute-start.5
  39.8 0.4 collective-permute-done.6.refs_4_
  40.1 0.8 collective-permute-start.18
  40.9 5.0 %collective-permute-done.15.refs_11_ = bf16[12,8,2048]{2,1,0:T(8,128)(2,1)S(1)} collective-permute-done((bf16[12,8,2048]{2,1,0:T(8,128)(2,1)S(1)}, bf16[12,8,2048]{2,1,0:T(8,128)(2,1)S(1)}, u32[]{:S(2)}, u32[]{:S(2)}) %collective-permute-start.15) | collective-permute-done | bytes 393248 | tf_op jit(solution)/shard_map/ppermute | solution.py:34
  45.9 1.4 %collective-permute-start.16 = (bf16[12,8,2048]{2,1,0:T(8,128)(2,1)S(1)}, bf16[12,8,2048]{2,1,0:T(8,128)(2,1)S(1)}, u32[]{:S(2)}, u32[]{:S(2)}) collective-permute-start(bf16[12,8,2048]{2,1,0:T(8,128)(2,1)S(1)} %collective-permute-done.4.refs_2_), channel_id=1, source_target_pairs={{0,96},{96,0},{32,64},{64,32},{1,97},{97,1},{33,65},{65,33},{2,98}... | collective-permute-start | bytes 1179656 | tf_op jit(solution)/shard_map/ppermute | solution.py:34
  47.4 1.2 %collective-permute-done.7.refs_5_ = bf16[12,8,2048]{2,1,0:T(8,128)(2,1)S(1)} collective-permute-done((bf16[12,8,2048]{2,1,0:T(8,128)(2,1)S(1)}, bf16[12,8,2048]{2,1,0:T(8,128)(2,1)S(1)}, u32[]{:S(2)}, u32[]{:S(2)}) %collective-permute-start.7) | collective-permute-done | bytes 393248 | tf_op jit(solution)/shard_map/ppermute | solution.py:34
  48.5 0.7 collective-permute-start.19
  49.2 0.0 collective-permute-done.13.refs_9_
  49.2 0.0 collective-permute-start.17
  49.2 0.1 pad_maximum_fusion.3
  49.3 0.8 collective-permute-done.5.refs_3_
  50.1 6.6 %early.1.refs_0_ = f32[6,464,256]{2,1,0:T(8,128)S(1)} custom-call(bf16[12,8,2048]{2,1,0:T(8,128)(2,1)S(1)} %pad_maximum_fusion.refs_0_, bf16[12,8,2048]{2,1,0:T(8,128)(2,1)S(1)} %constant_dynamic-update-slice_fusion.refs_1_, bf16[12,8,2048]{2,1,0:T(8,128)(2,1)S(1)} %collective-permute-done.4.refs_2_, ...), custom_call_target="tpu_custom_call" | custom-call | tf_op jit(solution)/shard_map/early/pallas_call | solution.py:138
  56.7 0.0 copy-start.4
  56.7 0.0 collective-permute-done.18.refs_3_
  56.8 0.2 collective-permute-done.17.refs_2_
  57.0 5.4 %products.1 = (f32[12,64,128]{2,1,0:T(8,128)S(1)}, bf16[23,16,128]{2,1,0:T(8,128)(2,1)S(1)}, bf16[23,16,128]{2,1,0:T(8,128)(2,1)S(1)}, bf16[17,16,128]{2,1,0:T(8...) custom-call(f32[6,464,256]{2,1,0:T(8,128)S(1)} %early.1.refs_0_, ...), custom_call_target="tpu_custom_call" | custom-call | tf_op jit(solution)/shard_map/products/pallas_call | solution.py:254
  62.5 7.5 %collective-permute-start.24 = (bf16[15,16,128]{2,1,0:T(8,128)(2,1)S(1)}, bf16[15,16,128]{2,1,0:T(8,128)(2,1)S(1)}, u32[]{:S(2)}, u32[]{:S(2)}) collective-permute-start(bf16[15,16,128]{2,1,0:T(8,128)(2,1)S(1)} %get-tuple-element.18), channel_id=1, source_target_pairs={{0,3},{1,4},{2,5},{3,6},{4,7},{5,0},{6,1},{7,2},{8,11},{9,12},{10,... | collective-permute-start | bytes 184328 | tf_op jit(solution)/shard_map/ppermute | solution.py:23
  70.0 0.1 pad_maximum_fusion.4.refs_11_
  70.0 0.7 collective-permute-start.20
  70.8 1.9 %collective-permute-start.21 = (bf16[23,16,128]{2,1,0:T(8,128)(2,1)S(1)}, bf16[23,16,128]{2,1,0:T(8,128)(2,1)S(1)}, u32[]{:S(2)}, u32[]{:S(2)}) collective-permute-start(bf16[23,16,128]{2,1,0:T(8,128)(2,1)S(1)} %get-tuple-element.15.refs_8_), channel_id=1, source_target_pairs={{0,7},{1,0},{2,1},{3,2},{4,3},{5,4},{6,5},{7,6},{8,15},{9,8},{10,9... | collective-permute-start | bytes 282632 | tf_op jit(solution)/shard_map/ppermute | solution.py:23
  72.7 0.7 collective-permute-start.22
  73.3 4.3 %collective-permute-done.26.refs_6_ = bf16[5,16,128]{2,1,0:T(8,128)(2,1)S(1)} collective-permute-done((bf16[5,16,128]{2,1,0:T(8,128)(2,1)S(1)}, bf16[5,16,128]{2,1,0:T(8,128)(2,1)S(1)}, u32[]{:S(2)}, u32[]{:S(2)}) %collective-permute-start.26) | collective-permute-done | bytes 20512 | tf_op jit(solution)/shard_map/ppermute | solution.py:23
  77.7 2.5 %collective-permute-start.25 = (bf16[15,16,128]{2,1,0:T(8,128)(2,1)S(1)}, bf16[15,16,128]{2,1,0:T(8,128)(2,1)S(1)}, u32[]{:S(2)}, u32[]{:S(2)}) collective-permute-start(bf16[15,16,128]{2,1,0:T(8,128)(2,1)S(1)} %get-tuple-element.19), channel_id=1, source_target_pairs={{0,5},{1,6},{2,7},{3,0},{4,1},{5,2},{6,3},{7,4},{8,13},{9,14},{10,... | collective-permute-start | bytes 184328 | tf_op jit(solution)/shard_map/ppermute | solution.py:23
  80.2 0.1 pad_maximum_fusion.5.refs_12_
  80.3 5.6 %collective-permute-done.25.refs_5_ = bf16[15,16,128]{2,1,0:T(8,128)(2,1)S(1)} collective-permute-done((bf16[15,16,128]{2,1,0:T(8,128)(2,1)S(1)}, bf16[15,16,128]{2,1,0:T(8,128)(2,1)S(1)}, u32[]{:S(2)}, u32[]{:S(2)}) %collective-permute-start.25) | collective-permute-done | bytes 61472 | tf_op jit(solution)/shard_map/ppermute | solution.py:23
  85.9 1.2 %branches.1 = bf16[16,136,128]{2,1,0:T(8,128)(2,1)} custom-call(f32[12,64,128]{2,1,0:T(8,128)S(1)} %get-tuple-element.13.centre, bf16[23,16,128]{2,1,0:T(8,128)(2,1)S(1)} %collective-permute-done.20.refs_0_, bf16[23,16,128]{2,1,0:T(8,128)(2,1)S(1)} %collective-permute-done.21.refs_1_, bf16[17,16,128]{2,1,0:T(8,128)(2,1)S(1)} %collective-permute-done.22.refs_2_, ...), custom_call_target="tpu_custom_call" | custom-call | tf_op jit(solution)/shard_map/branches/pallas_call | solution.py:341
  87.1 5.0 %all-to-all-start = ((bf16[16,136,128]{2,1,0:T(8,128)(2,1)}), bf16[16,136,128]{2,1,0:T(8,128)(2,1)S(1)}, u32[]{:S(2)}, u32[]{:S(2)}) async-start(bf16[16,136,128]{2,1,0:T(8,128)(2,1)} %branches.1), calls=%async_computation | async-start | bytes 1114112 | tf_op jit(solution)/shard_map/all_to_all | solution.py:555
  92.1 0.6 spread.1.refs_3_
  92.8 0.1 fusion.7
  92.9 0.3 pad_maximum_fusion.2.refs_4_
  93.2 9.3 %all-to-all-done.refs_0_ = bf16[16,136,128]{2,1,0:T(8,128)(2,1)S(1)} async-done(((bf16[16,136,128]{2,1,0:T(8,128)(2,1)}), bf16[16,136,128]{2,1,0:T(8,128)(2,1)S(1)}, u32[]{:S(2)}, u32[]{:S(2)}) %all-to-all-start) | async-done | bytes 557088 | tf_op jit(solution)/shard_map/all_to_all | solution.py:555
  102.4 6.7 %decode.1 = bf16[16,24,256]{2,1,0:T(8,128)(2,1)} custom-call(bf16[16,136,128]{2,1,0:T(8,128)(2,1)S(1)} %all-to-all-done.refs_0_, bf16[5,16,16,256]{3,2,1,0:T(8,128)(2,1)} %bitcast.32, f32[1,256]{1,0:T(1,128)} %bitcast.37, bf16[640,192]{1,0:T(8,128)(2,1)S(1)} %spread.1.refs_3_, bf16[640,144]{1,0:T(8,128)(2,1)S(1)} %pad_maximum_fusion.2.refs_4_, ...), custom_call_target="tpu_custom_call" | custom-call | tf_op jit(solution)/shard_map/decode/pallas_call | solution.py:449
  (36 shorter events, 0.3 us)
Async XLA Ops:
  0.0 7.3 %copy-start = (bf16[16,24,256]{2,1,0:T(8,128)(2,1)S(1)}, bf16[16,24,256]{2,1,0:T(8,128)(2,1)}, u32[]{:S(2)}) copy-start(bf16[16,24,256]{2,1,0:T(8,128)(2,1)} %param.15) | copy-start | bytes 589828
  1.1 13.2 %collective-permute-start.9 = (bf16[6,8,2048]{2,1,0:T(8,128)(2,1)S(1)}, bf16[6,8,2048]{2,1,0:T(8,128)(2,1)S(1)}, u32[]{:S(2)}, u32[]{:S(2)}) collective-permute-start(bf16[6,8,2048]{2,1,0:T(8,128)(2,1)S(1)} %get-tuple-element.21), channel_id=1, source_target_pairs={{0,96},{96,0},{32,64},{64,32},{1,97},{97,1},{33,65},{65,33},{2,98}... | collective-permute-start | bytes 589832 | tf_op jit(solution)/shard_map/ppermute | solution.py:34
  4.2 8.0 %collective-permute-start.8 = (bf16[6,8,2048]{2,1,0:T(8,128)(2,1)S(1)}, bf16[6,8,2048]{2,1,0:T(8,128)(2,1)S(1)}, u32[]{:S(2)}, u32[]{:S(2)}) collective-permute-start(bf16[6,8,2048]{2,1,0:T(8,128)(2,1)S(1)} %get-tuple-element.21), channel_id=1, source_target_pairs={{0,32},{32,0},{64,96},{96,64},{1,33},{33,1},{65,97},{97,65},{2,34}... | collective-permute-start | bytes 589832 | tf_op jit(solution)/shard_map/ppermute | solution.py:34
  4.3 12.2 %collective-permute-start.1 = (bf16[6,8,2048]{2,1,0:T(8,128)(2,1)S(1)}, bf16[6,8,2048]{2,1,0:T(8,128)(2,1)S(1)}, u32[]{:S(2)}, u32[]{:S(2)}) collective-permute-start(bf16[6,8,2048]{2,1,0:T(8,128)(2,1)S(1)} %get-tuple-element.22), channel_id=1, source_target_pairs={{0,24},{24,0},{8,16},{16,8},{1,25},{25,1},{9,17},{17,9},{2,26},{26... | collective-permute-start | bytes 589832 | tf_op jit(solution)/shard_map/ppermute | solution.py:34
  7.1 8.4 %collective-permute-start = (bf16[6,8,2048]{2,1,0:T(8,128)(2,1)S(1)}, bf16[6,8,2048]{2,1,0:T(8,128)(2,1)S(1)}, u32[]{:S(2)}, u32[]{:S(2)}) collective-permute-start(bf16[6,8,2048]{2,1,0:T(8,128)(2,1)S(1)} %get-tuple-element.22), channel_id=1, source_target_pairs={{0,8},{8,0},{16,24},{24,16},{1,9},{9,1},{17,25},{25,17},{2,10},{10... | collective-permute-start | bytes 589832 | tf_op jit(solution)/shard_map/ppermute | solution.py:34
  8.4 18.6 %collective-permute-start.27 = (bf16[16,2,48]{2,1,0:T(2,128)(2,1)S(1)}, bf16[16,2,48]{2,1,0:T(2,128)(2,1)S(1)}, u32[]{:S(2)}, u32[]{:S(2)}) collective-permute-start(bf16[16,2,48]{2,1,0:T(2,128)(2,1)S(1)} %get-tuple-element.27), channel_id=1, source_target_pairs={{0,1},{1,2},{2,3},{3,4},{4,5},{5,6},{6,7},{8,9},{9,10},{10,11},{11... | collective-permute-start | bytes 9224 | tf_op jit(solution)/shard_map/ppermute | solution.py:29
  12.2 16.1 %collective-permute-start.28 = (bf16[16,2,48]{2,1,0:T(2,128)(2,1)S(1)}, bf16[16,2,48]{2,1,0:T(2,128)(2,1)S(1)}, u32[]{:S(2)}, u32[]{:S(2)}) collective-permute-start(bf16[16,2,48]{2,1,0:T(2,128)(2,1)S(1)} %get-tuple-element.28), channel_id=1, source_target_pairs={{1,0},{2,1},{3,2},{4,3},{5,4},{6,5},{7,6},{9,8},{10,9},{11,10},{12... | collective-permute-start | bytes 9224 | tf_op jit(solution)/shard_map/ppermute | solution.py:29
  14.3 5.9 %collective-permute-start.10 = (bf16[3,8,2048]{2,1,0:T(8,128)(2,1)S(1)}, bf16[3,8,2048]{2,1,0:T(8,128)(2,1)S(1)}, u32[]{:S(2)}, u32[]{:S(2)}) collective-permute-start(bf16[3,8,2048]{2,1,0:T(8,128)(2,1)S(1)} %slice.76), channel_id=1, source_target_pairs={{0,96},{96,0},{32,64},{64,32},{1,97},{97,1},{33,65},{65,33},{2,98}... | collective-permute-start | bytes 294920 | tf_op jit(solution)/shard_map/ppermute | solution.py:34
  15.4 34.6 %copy-start.1 = (bf16[3,3,3,2048,16]{3,4,2,1,0:T(8,128)(2,1)S(1)}, bf16[3,3,3,2048,16]{3,4,2,1,0:T(8,128)(2,1)}, u32[]{:S(2)}) copy-start(bf16[3,3,3,2048,16]{3,4,2,1,0:T(8,128)(2,1)} %param.17) | copy-start | bytes 5308420
  15.5 34.6 %copy-start.2 = (bf16[2048,16]{0,1:T(8,128)(2,1)S(1)}, bf16[2048,16]{0,1:T(8,128)(2,1)}, u32[]{:S(2)}) copy-start(bf16[2048,16]{0,1:T(8,128)(2,1)} %param.16) | copy-start | bytes 196612
  15.5 34.6 %copy-start.3 = (bf16[2048,16]{0,1:T(8,128)(2,1)S(1)}, bf16[2048,16]{0,1:T(8,128)(2,1)}, u32[]{:S(2)}) copy-start(bf16[2048,16]{0,1:T(8,128)(2,1)} %param.18) | copy-start | bytes 196612
  15.5 6.5 %collective-permute-start.11 = (bf16[3,8,2048]{2,1,0:T(8,128)(2,1)S(1)}, bf16[3,8,2048]{2,1,0:T(8,128)(2,1)S(1)}, u32[]{:S(2)}, u32[]{:S(2)}) collective-permute-start(bf16[3,8,2048]{2,1,0:T(8,128)(2,1)S(1)} %slice.77), channel_id=1, source_target_pairs={{0,32},{32,0},{64,96},{96,64},{1,33},{33,1},{65,97},{97,65},{2,34}... | collective-permute-start | bytes 294920 | tf_op jit(solution)/shard_map/ppermute | solution.py:34
  16.6 5.9 %collective-permute-start.2 = (bf16[3,8,2048]{2,1,0:T(8,128)(2,1)S(1)}, bf16[3,8,2048]{2,1,0:T(8,128)(2,1)S(1)}, u32[]{:S(2)}, u32[]{:S(2)}) collective-permute-start(bf16[3,8,2048]{2,1,0:T(8,128)(2,1)S(1)} %slice.73), channel_id=1, source_target_pairs={{0,24},{24,0},{8,16},{16,8},{1,25},{25,1},{9,17},{17,9},{2,26},{26... | collective-permute-start | bytes 294920 | tf_op jit(solution)/shard_map/ppermute | solution.py:34
  20.2 5.7 %collective-permute-start.3 = (bf16[3,8,2048]{2,1,0:T(8,128)(2,1)S(1)}, bf16[3,8,2048]{2,1,0:T(8,128)(2,1)S(1)}, u32[]{:S(2)}, u32[]{:S(2)}) collective-permute-start(bf16[3,8,2048]{2,1,0:T(8,128)(2,1)S(1)} %slice.74), channel_id=1, source_target_pairs={{0,8},{8,0},{16,24},{24,16},{1,9},{9,1},{17,25},{25,17},{2,10},{10... | collective-permute-start | bytes 294920 | tf_op jit(solution)/shard_map/ppermute | solution.py:34
  22.0 9.2 %collective-permute-start.12 = (bf16[12,8,2048]{2,1,0:T(8,128)(2,1)S(1)}, bf16[12,8,2048]{2,1,0:T(8,128)(2,1)S(1)}, u32[]{:S(2)}, u32[]{:S(2)}) collective-permute-start(bf16[12,8,2048]{2,1,0:T(8,128)(2,1)S(1)} %pad_maximum_fusion.1.refs_6_), channel_id=1, source_target_pairs={{0,8},{8,0},{16,24},{24,16},{1,9},{9,1},{17,25},{25,17},{2,10},{10... | collective-permute-start | bytes 1179656 | tf_op jit(solution)/shard_map/ppermute | solution.py:34
  22.5 10.0 %collective-permute-start.4 = (bf16[12,8,2048]{2,1,0:T(8,128)(2,1)S(1)}, bf16[12,8,2048]{2,1,0:T(8,128)(2,1)S(1)}, u32[]{:S(2)}, u32[]{:S(2)}) collective-permute-start(bf16[12,8,2048]{2,1,0:T(8,128)(2,1)S(1)} %pad_maximum_fusion.refs_0_), channel_id=1, source_target_pairs={{0,32},{32,0},{64,96},{96,64},{1,33},{33,1},{65,97},{97,65},{2,34}... | collective-permute-start | bytes 1179656 | tf_op jit(solution)/shard_map/ppermute | solution.py:34
  25.9 13.2 %collective-permute-start.14 = (bf16[12,8,2048]{2,1,0:T(8,128)(2,1)S(1)}, bf16[12,8,2048]{2,1,0:T(8,128)(2,1)S(1)}, u32[]{:S(2)}, u32[]{:S(2)}) collective-permute-start(bf16[12,8,2048]{2,1,0:T(8,128)(2,1)S(1)} %pad_maximum_fusion.1.refs_6_), channel_id=1, source_target_pairs={{0,24},{24,0},{8,16},{16,8},{1,25},{25,1},{9,17},{17,9},{2,26},{26... | collective-permute-start | bytes 1179656 | tf_op jit(solution)/shard_map/ppermute | solution.py:34
  27.0 13.1 %collective-permute-start.6 = (bf16[12,8,2048]{2,1,0:T(8,128)(2,1)S(1)}, bf16[12,8,2048]{2,1,0:T(8,128)(2,1)S(1)}, u32[]{:S(2)}, u32[]{:S(2)}) collective-permute-start(bf16[12,8,2048]{2,1,0:T(8,128)(2,1)S(1)} %pad_maximum_fusion.refs_0_), channel_id=1, source_target_pairs={{0,96},{96,0},{32,64},{64,32},{1,97},{97,1},{33,65},{65,33},{2,98}... | collective-permute-start | bytes 1179656 | tf_op jit(solution)/shard_map/ppermute | solution.py:34
  28.4 17.6 %collective-permute-start.15 = (bf16[12,8,2048]{2,1,0:T(8,128)(2,1)S(1)}, bf16[12,8,2048]{2,1,0:T(8,128)(2,1)S(1)}, u32[]{:S(2)}, u32[]{:S(2)}) collective-permute-start(bf16[12,8,2048]{2,1,0:T(8,128)(2,1)S(1)} %constant_dynamic-update-slice_fusion.3.refs_7_), channel_id=1, source_target_pairs={{0,24},{24,0},{8,16},{16,8},{1,25},{25,1},{9,17},{17,9},{2,26},{26... | collective-permute-start | bytes 1179656 | tf_op jit(solution)/shard_map/ppermute | solution.py:34
  31.2 17.3 %collective-permute-start.7 = (bf16[12,8,2048]{2,1,0:T(8,128)(2,1)S(1)}, bf16[12,8,2048]{2,1,0:T(8,128)(2,1)S(1)}, u32[]{:S(2)}, u32[]{:S(2)}) collective-permute-start(bf16[12,8,2048]{2,1,0:T(8,128)(2,1)S(1)} %constant_dynamic-update-slice_fusion.refs_1_), channel_id=1, source_target_pairs={{0,96},{96,0},{32,64},{64,32},{1,97},{97,1},{33,65},{65,33},{2,98}... | collective-permute-start | bytes 1179656 | tf_op jit(solution)/shard_map/ppermute | solution.py:34
  32.5 16.8 %collective-permute-start.13 = (bf16[12,8,2048]{2,1,0:T(8,128)(2,1)S(1)}, bf16[12,8,2048]{2,1,0:T(8,128)(2,1)S(1)}, u32[]{:S(2)}, u32[]{:S(2)}) collective-permute-start(bf16[12,8,2048]{2,1,0:T(8,128)(2,1)S(1)} %constant_dynamic-update-slice_fusion.3.refs_7_), channel_id=1, source_target_pairs={{0,8},{8,0},{16,24},{24,16},{1,9},{9,1},{17,25},{25,17},{2,10},{10... | collective-permute-start | bytes 1179656 | tf_op jit(solution)/shard_map/ppermute | solution.py:34
  39.1 11.0 %collective-permute-start.5 = (bf16[12,8,2048]{2,1,0:T(8,128)(2,1)S(1)}, bf16[12,8,2048]{2,1,0:T(8,128)(2,1)S(1)}, u32[]{:S(2)}, u32[]{:S(2)}) collective-permute-start(bf16[12,8,2048]{2,1,0:T(8,128)(2,1)S(1)} %constant_dynamic-update-slice_fusion.refs_1_), channel_id=1, source_target_pairs={{0,32},{32,0},{64,96},{96,64},{1,33},{33,1},{65,97},{97,65},{2,34}... | collective-permute-start | bytes 1179656 | tf_op jit(solution)/shard_map/ppermute | solution.py:34
  40.1 16.6 %collective-permute-start.18 = (bf16[12,8,2048]{2,1,0:T(8,128)(2,1)S(1)}, bf16[12,8,2048]{2,1,0:T(8,128)(2,1)S(1)}, u32[]{:S(2)}, u32[]{:S(2)}) collective-permute-start(bf16[12,8,2048]{2,1,0:T(8,128)(2,1)S(1)} %collective-permute-done.12.refs_8_), channel_id=1, source_target_pairs={{0,24},{24,0},{8,16},{16,8},{1,25},{25,1},{9,17},{17,9},{2,26},{26... | collective-permute-start | bytes 1179656 | tf_op jit(solution)/shard_map/ppermute | solution.py:34
  45.9 10.8 %collective-permute-start.16 = (bf16[12,8,2048]{2,1,0:T(8,128)(2,1)S(1)}, bf16[12,8,2048]{2,1,0:T(8,128)(2,1)S(1)}, u32[]{:S(2)}, u32[]{:S(2)}) collective-permute-start(bf16[12,8,2048]{2,1,0:T(8,128)(2,1)S(1)} %collective-permute-done.4.refs_2_), channel_id=1, source_target_pairs={{0,96},{96,0},{32,64},{64,32},{1,97},{97,1},{33,65},{65,33},{2,98}... | collective-permute-start | bytes 1179656 | tf_op jit(solution)/shard_map/ppermute | solution.py:34
  48.5 8.2 %collective-permute-start.19 = (bf16[12,8,2048]{2,1,0:T(8,128)(2,1)S(1)}, bf16[12,8,2048]{2,1,0:T(8,128)(2,1)S(1)}, u32[]{:S(2)}, u32[]{:S(2)}) collective-permute-start(bf16[12,8,2048]{2,1,0:T(8,128)(2,1)S(1)} %collective-permute-done.15.refs_11_), channel_id=1, source_target_pairs={{0,8},{8,0},{16,24},{24,16},{1,9},{9,1},{17,25},{25,17},{2,10},{10... | collective-permute-start | bytes 1179656 | tf_op jit(solution)/shard_map/ppermute | solution.py:34
  49.2 7.8 %collective-permute-start.17 = (bf16[12,8,2048]{2,1,0:T(8,128)(2,1)S(1)}, bf16[12,8,2048]{2,1,0:T(8,128)(2,1)S(1)}, u32[]{:S(2)}, u32[]{:S(2)}) collective-permute-start(bf16[12,8,2048]{2,1,0:T(8,128)(2,1)S(1)} %collective-permute-done.7.refs_5_), channel_id=1, source_target_pairs={{0,32},{32,0},{64,96},{96,64},{1,33},{33,1},{65,97},{97,65},{2,34}... | collective-permute-start | bytes 1179656 | tf_op jit(solution)/shard_map/ppermute | solution.py:34
  56.7 29.1 %copy-start.4 = (f32[5,16]{1,0:T(8,128)S(1)}, f32[5,16]{1,0:T(8,128)}, u32[]{:S(2)}) copy-start(f32[5,16]{1,0:T(8,128)} %refs_10_.1) | copy-start | bytes 964
  62.5 15.2 %collective-permute-start.24 = (bf16[15,16,128]{2,1,0:T(8,128)(2,1)S(1)}, bf16[15,16,128]{2,1,0:T(8,128)(2,1)S(1)}, u32[]{:S(2)}, u32[]{:S(2)}) collective-permute-start(bf16[15,16,128]{2,1,0:T(8,128)(2,1)S(1)} %get-tuple-element.18), channel_id=1, source_target_pairs={{0,3},{1,4},{2,5},{3,6},{4,7},{5,0},{6,1},{7,2},{8,11},{9,12},{10,... | collective-permute-start | bytes 184328 | tf_op jit(solution)/shard_map/ppermute | solution.py:23
  69.9 7.7 %collective-permute-start.26 = (bf16[5,16,128]{2,1,0:T(8,128)(2,1)S(1)}, bf16[5,16,128]{2,1,0:T(8,128)(2,1)S(1)}, u32[]{:S(2)}, u32[]{:S(2)}) collective-permute-start(bf16[5,16,128]{2,1,0:T(8,128)(2,1)S(1)} %get-tuple-element.20.refs_9_), channel_id=1, source_target_pairs={{0,4},{1,5},{2,6},{3,7},{4,0},{5,1},{6,2},{7,3},{8,12},{9,13},{10,... | collective-permute-start | bytes 61448 | tf_op jit(solution)/shard_map/ppermute | solution.py:23
  70.0 15.8 %collective-permute-start.20 = (bf16[23,16,128]{2,1,0:T(8,128)(2,1)S(1)}, bf16[23,16,128]{2,1,0:T(8,128)(2,1)S(1)}, u32[]{:S(2)}, u32[]{:S(2)}) collective-permute-start(bf16[23,16,128]{2,1,0:T(8,128)(2,1)S(1)} %get-tuple-element.14.refs_7_), channel_id=1, source_target_pairs={{0,1},{1,2},{2,3},{3,4},{4,5},{5,6},{6,7},{7,0},{8,9},{9,10},{10,1... | collective-permute-start | bytes 282632 | tf_op jit(solution)/shard_map/ppermute | solution.py:23
  70.8 15.1 %collective-permute-start.21 = (bf16[23,16,128]{2,1,0:T(8,128)(2,1)S(1)}, bf16[23,16,128]{2,1,0:T(8,128)(2,1)S(1)}, u32[]{:S(2)}, u32[]{:S(2)}) collective-permute-start(bf16[23,16,128]{2,1,0:T(8,128)(2,1)S(1)} %get-tuple-element.15.refs_8_), channel_id=1, source_target_pairs={{0,7},{1,0},{2,1},{3,2},{4,3},{5,4},{6,5},{7,6},{8,15},{9,8},{10,9... | collective-permute-start | bytes 282632 | tf_op jit(solution)/shard_map/ppermute | solution.py:23
  72.7 13.2 %collective-permute-start.22 = (bf16[17,16,128]{2,1,0:T(8,128)(2,1)S(1)}, bf16[17,16,128]{2,1,0:T(8,128)(2,1)S(1)}, u32[]{:S(2)}, u32[]{:S(2)}) collective-permute-start(bf16[17,16,128]{2,1,0:T(8,128)(2,1)S(1)} %get-tuple-element.16), channel_id=1, source_target_pairs={{0,2},{1,3},{2,4},{3,5},{4,6},{5,7},{6,0},{7,1},{8,10},{9,11},{10,... | collective-permute-start | bytes 208904 | tf_op jit(solution)/shard_map/ppermute | solution.py:23
  77.7 8.2 %collective-permute-start.23 = (bf16[17,16,128]{2,1,0:T(8,128)(2,1)S(1)}, bf16[17,16,128]{2,1,0:T(8,128)(2,1)S(1)}, u32[]{:S(2)}, u32[]{:S(2)}) collective-permute-start(bf16[17,16,128]{2,1,0:T(8,128)(2,1)S(1)} %get-tuple-element.17), channel_id=1, source_target_pairs={{0,6},{1,7},{2,0},{3,1},{4,2},{5,3},{6,4},{7,5},{8,14},{9,15},{10,... | collective-permute-start | bytes 208904 | tf_op jit(solution)/shard_map/ppermute | solution.py:23
  77.7 8.2 %collective-permute-start.25 = (bf16[15,16,128]{2,1,0:T(8,128)(2,1)S(1)}, bf16[15,16,128]{2,1,0:T(8,128)(2,1)S(1)}, u32[]{:S(2)}, u32[]{:S(2)}) collective-permute-start(bf16[15,16,128]{2,1,0:T(8,128)(2,1)S(1)} %get-tuple-element.19), channel_id=1, source_target_pairs={{0,5},{1,6},{2,7},{3,0},{4,1},{5,2},{6,3},{7,4},{8,13},{9,14},{10,... | collective-permute-start | bytes 184328 | tf_op jit(solution)/shard_map/ppermute | solution.py:23
  87.1 15.4 %all-to-all-start = ((bf16[16,136,128]{2,1,0:T(8,128)(2,1)}), bf16[16,136,128]{2,1,0:T(8,128)(2,1)S(1)}, u32[]{:S(2)}, u32[]{:S(2)}) async-start(bf16[16,136,128]{2,1,0:T(8,128)(2,1)} %branches.1), calls=%async_computation | async-start | bytes 1114112 | tf_op jit(solution)/shard_map/all_to_all | solution.py:555
